TPU v7x, 32 devices: a whole 2x2x4 slice. The times are simulated.
32 devices in a mesh: grp: 8 (over y, x, core), shard: 4 (over z).
Axes of the slice: x: 2, y: 2, z: 4, core: 2. Of those that a mesh axis runs over, the one named last changes fastest.
Arguments:
- tokens: bfloat16 [16, 1024, 768], P('grp', 'shard'), may hold values from -6 to 6
- cotangent: bfloat16 [16, 1024, 768], P('grp', 'shard'), may hold values from -6 to 6
- lengths: int32 [16], P('grp'), may hold values from 256 to 1024, as said below
- w_qkv: bfloat16 [768, 2304], P('shard'), may hold values from -0.21875 to 0.21875
- bias_q: bfloat16 [768], P('shard'), may hold values from -3 to 3
- bias_v: bfloat16 [768], P('shard'), may hold values from -3 to 3
- w_out: bfloat16 [768, 768], P('shard'), may hold values from -1.75 to 1.75
- bias_out: bfloat16 [768], P('shard'), may hold values from -3 to 3
- gain_attn: bfloat16 [768], P('shard'), may hold values from 0.25 to 1.75
- shift_attn: bfloat16 [768], P('shard'), may hold values from -3 to 3
- w_up: bfloat16 [768, 3072], P('shard'), may hold values from -0.21875 to 0.21875
- bias_up: bfloat16 [3072], P('shard'), may hold values from -3 to 3
- w_down: bfloat16 [3072, 768], P('shard'), may hold values from -0.109375 to 0.109375
- bias_down: bfloat16 [768], P('shard'), may hold values from -3 to 3
- gain_ffn: bfloat16 [768], P('shard'), may hold values from 0.25 to 1.75
- shift_ffn: bfloat16 [768], P('shard'), may hold values from -3 to 3
Outputs:
- layer_out: bfloat16 [16, 1024, 768], P('grp', 'shard')
- grad_tokens: bfloat16 [16, 1024, 768], P('grp', 'shard')
- grad_w_qkv: float32 [768, 2304], P('shard')
- grad_bias_q: float32 [768], P('shard')
- grad_bias_v: float32 [768], P('shard')
- grad_w_out: float32 [768, 768], P('shard')
- grad_bias_out: float32 [768], P('shard')
- grad_gain_attn: float32 [768], P('shard')
- grad_shift_attn: float32 [768], P('shard')
- grad_w_up: float32 [768, 3072], P('shard')
- grad_bias_up: float32 [3072], P('shard')
- grad_w_down: float32 [3072, 768], P('shard')
- grad_bias_down: float32 [768], P('shard')
- grad_gain_ffn: float32 [768], P('shard')
- grad_shift_ffn: float32 [768], P('shard')
Inputs may be any that keep to these rules, and one draw needn't show every extreme that they name: `lengths`: valid slots of a sequence come first; some sequence fills all 1024 slots.
All inputs are finite; a program needn't handle non-finite values.
Results may differ from a plain program's by a relative error of at most 0.03.
Values may be sent and summed in bfloat16 or wider, within the bound.
No kernel may reach another device: no remote copies, remote signals or barrier semaphores. Data moves between devices by JAX's collectives and lax.ppermute only.
A program may use at most 256 MiB of HBM per device.

v0:
```python
import functools
import math

import jax
import jax.numpy as jnp
from jax import lax
from jax.experimental import pallas as pl
from jax.experimental.pallas import tpu as pltpu
from jax.sharding import PartitionSpec as P


H = 12
HD = 64


eps = 1e-12
masked_score = -1000000000.0


def layer_norm(values_in, gain_vec, shift_vec):
    row_mean = jnp.mean(values_in, axis=-1, keepdims=True)
    centered = values_in - row_mean
    variance = jnp.mean(centered * centered, axis=-1, keepdims=True)
    return centered * lax.rsqrt(variance + eps) * gain_vec + shift_vec


def gelu_exact(values_in):
    return jax.nn.gelu(values_in, approximate=False)


def contract_cols(left_mat, right_mat):
    return lax.dot_general(
        left_mat, right_mat, (((1,), (1,)), ((), ())), preferred_element_type=jnp.float32
    )


def contract_rows(left_mat, right_mat):
    return lax.dot_general(
        left_mat, right_mat, (((0,), (0,)), ((), ())), preferred_element_type=jnp.float32
    )


def column_sums(matrix):
    return jnp.sum(matrix.astype(jnp.float32), axis=0)


def unpack(weights_full):
    (
        qkv_weight,
        query_bias,
        value_bias,
        out_weight,
        out_bias,
        gain_one,
        shift_one,
        up_weight,
        up_bias,
        down_weight,
        down_bias,
        gain_two,
        shift_two,
    ) = weights_full
    as_float = lambda vector: vector.astype(jnp.float32)
    return (
        qkv_weight,
        as_float(query_bias),
        as_float(value_bias),
        out_weight,
        as_float(out_bias),
        as_float(gain_one),
        as_float(shift_one),
        up_weight,
        as_float(up_bias),
        down_weight,
        as_float(down_bias),
        as_float(gain_two),
        as_float(shift_two),
    )


def head_scores(queries, keys, key_mask, head_idx):
    col_start = head_idx * HD
    q_head = lax.dynamic_slice_in_dim(queries, col_start, HD, 1)
    k_head = lax.dynamic_slice_in_dim(keys, col_start, HD, 1)
    scores = contract_cols(q_head, k_head) * HD ** (-0.5)
    return (q_head, k_head, jnp.where(key_mask[None, :], scores, masked_score))


def attend_forward(queries, keys, values, key_mask):
    row_count, width = queries.shape

    def one_head(head_idx, carry):
        context, lse_rows = carry
        q_head, k_head, scores = head_scores(queries, keys, key_mask, head_idx)
        v_head = lax.dynamic_slice_in_dim(values, head_idx * HD, HD, 1)
        row_max = jnp.max(scores, axis=1, keepdims=True)
        exp_scores = jnp.exp(scores - row_max)
        row_total = jnp.sum(exp_scores, axis=1, keepdims=True)
        prob_low = (exp_scores / row_total).astype(jnp.bfloat16)
        head_out = jnp.dot(prob_low, v_head, preferred_element_type=jnp.float32)
        context = lax.dynamic_update_slice_in_dim(context, head_out, head_idx * HD, 1)
        lse_rows = lax.dynamic_update_slice_in_dim(
            lse_rows, row_max + jnp.log(row_total), head_idx, 1
        )
        return (context, lse_rows)

    start_state = (
        jnp.zeros((row_count, width), jnp.float32),
        jnp.zeros((row_count, H), jnp.float32),
    )
    return lax.fori_loop(0, H, one_head, start_state)


def attend_backward(queries, keys, values, key_mask, lse_rows, grad_context):
    row_count, width = queries.shape
    slot_count = keys.shape[0]

    def one_head(head_idx, carry):
        grad_q, grad_k, grad_v = carry
        col_start = head_idx * HD
        q_head, k_head, scores = head_scores(queries, keys, key_mask, head_idx)
        v_head = lax.dynamic_slice_in_dim(values, col_start, HD, 1)
        grad_head = lax.dynamic_slice_in_dim(grad_context, col_start, HD, 1)
        probs = jnp.exp(scores - lax.dynamic_slice_in_dim(lse_rows, head_idx, 1, 1))
        grad_probs = contract_cols(grad_head, v_head)
        delta = jnp.sum(probs * grad_probs, axis=1, keepdims=True)
        grad_scores = (probs * (grad_probs - delta)).astype(jnp.bfloat16)
        head_gq = jnp.dot(grad_scores, k_head, preferred_element_type=jnp.float32) * HD ** (-0.5)
        head_gk = contract_rows(grad_scores, q_head) * HD ** (-0.5)
        head_gv = contract_rows(probs.astype(jnp.bfloat16), grad_head)
        grad_q = lax.dynamic_update_slice_in_dim(grad_q, head_gq, col_start, 1)
        grad_k = lax.dynamic_update_slice_in_dim(grad_k, head_gk, col_start, 1)
        grad_v = lax.dynamic_update_slice_in_dim(grad_v, head_gv, col_start, 1)
        return (grad_q, grad_k, grad_v)

    start_state = (
        jnp.zeros((row_count, width), jnp.float32),
        jnp.zeros((slot_count, width), jnp.float32),
        jnp.zeros((slot_count, width), jnp.float32),
    )
    return lax.fori_loop(0, H, one_head, start_state)


def per_device(
    tokens,
    cotangent,
    lengths,
    w_qkv,
    bias_q,
    bias_v,
    w_out,
    bias_out,
    gain_attn,
    shift_attn,
    w_up,
    bias_up,
    w_down,
    bias_down,
    gain_ffn,
    shift_ffn,
):
    batch_count, row_count, width = tokens.shape
    dev_count = lax.axis_size("shard")
    slot_count = row_count * dev_count
    first_row = lax.axis_index("shard") * row_count
    key_place = jnp.arange(slot_count, dtype=jnp.int32)
    row_place = first_row + jnp.arange(row_count, dtype=jnp.int32)
    sharded = (
        w_qkv,
        bias_q,
        bias_v,
        w_out,
        bias_out,
        gain_attn,
        shift_attn,
        w_up,
        bias_up,
        w_down,
        bias_down,
        gain_ffn,
        shift_ffn,
    )
    totals = [
        jnp.zeros((piece.shape[0] * dev_count,) + piece.shape[1:], jnp.float32) for piece in sharded
    ]
    layer_rows = []
    grad_rows = []
    for batch_idx in range(batch_count):
        weights_full = unpack(
            (
                lax.all_gather(w_qkv, "shard", axis=0, tiled=True),
                lax.all_gather(bias_q, "shard", axis=0, tiled=True),
                lax.all_gather(bias_v, "shard", axis=0, tiled=True),
                lax.all_gather(w_out, "shard", axis=0, tiled=True),
                lax.all_gather(bias_out, "shard", axis=0, tiled=True),
                lax.all_gather(gain_attn, "shard", axis=0, tiled=True),
                lax.all_gather(shift_attn, "shard", axis=0, tiled=True),
                lax.all_gather(w_up, "shard", axis=0, tiled=True),
                lax.all_gather(bias_up, "shard", axis=0, tiled=True),
                lax.all_gather(w_down, "shard", axis=0, tiled=True),
                lax.all_gather(bias_down, "shard", axis=0, tiled=True),
                lax.all_gather(gain_ffn, "shard", axis=0, tiled=True),
                lax.all_gather(shift_ffn, "shard", axis=0, tiled=True),
            )
        )
        (
            qkv_weight,
            query_bias,
            value_bias,
            out_weight,
            out_bias,
            gain_one,
            shift_one,
            up_weight,
            up_bias,
            down_weight,
            down_bias,
            gain_two,
            shift_two,
        ) = weights_full
        seq_in = tokens[batch_idx]
        seq_len = lengths[batch_idx]
        key_mask = key_place < seq_len
        own_valid = row_place < seq_len
        row_mask = own_valid.astype(jnp.float32)[:, None]
        qkv_bias = jnp.concatenate([query_bias, jnp.zeros_like(query_bias), value_bias])
        qkv_low = (
            jnp.dot(seq_in, qkv_weight, preferred_element_type=jnp.float32) + qkv_bias
        ).astype(jnp.bfloat16)
        queries = qkv_low[:, :width]
        key_part = qkv_low[:, width : 2 * width]
        value_part = qkv_low[:, 2 * width :]
        keys_all, values_all = (
            lax.all_gather(key_part, "shard", axis=0, tiled=True),
            lax.all_gather(value_part, "shard", axis=0, tiled=True),
        )
        context, lse_rows = attend_forward(queries, keys_all, values_all, key_mask)
        context_low = context.astype(jnp.bfloat16)
        attn_out = jnp.dot(context_low, out_weight, preferred_element_type=jnp.float32) + out_bias
        hidden, norm_one_back = jax.vjp(
            layer_norm, seq_in.astype(jnp.float32) + attn_out, gain_one, shift_one
        )
        hidden_low = hidden.astype(jnp.bfloat16)
        up_proj = jnp.dot(hidden_low, up_weight, preferred_element_type=jnp.float32) + up_bias
        activation, gelu_back = jax.vjp(gelu_exact, up_proj)
        act_low = activation.astype(jnp.bfloat16)
        ffn_out = jnp.dot(act_low, down_weight, preferred_element_type=jnp.float32) + down_bias
        normed, norm_two_back = jax.vjp(layer_norm, hidden + ffn_out, gain_two, shift_two)
        layer_rows.append((normed * row_mask).astype(jnp.bfloat16))
        weights_full = unpack(
            (
                lax.all_gather(w_qkv, "shard", axis=0, tiled=True),
                lax.all_gather(bias_q, "shard", axis=0, tiled=True),
                lax.all_gather(bias_v, "shard", axis=0, tiled=True),
                lax.all_gather(w_out, "shard", axis=0, tiled=True),
                lax.all_gather(bias_out, "shard", axis=0, tiled=True),
                lax.all_gather(gain_attn, "shard", axis=0, tiled=True),
                lax.all_gather(shift_attn, "shard", axis=0, tiled=True),
                lax.all_gather(w_up, "shard", axis=0, tiled=True),
                lax.all_gather(bias_up, "shard", axis=0, tiled=True),
                lax.all_gather(w_down, "shard", axis=0, tiled=True),
                lax.all_gather(bias_down, "shard", axis=0, tiled=True),
                lax.all_gather(gain_ffn, "shard", axis=0, tiled=True),
                lax.all_gather(shift_ffn, "shard", axis=0, tiled=True),
            )
        )
        (
            qkv_weight,
            query_bias,
            value_bias,
            out_weight,
            out_bias,
            gain_one,
            shift_one,
            up_weight,
            up_bias,
            down_weight,
            down_bias,
            gain_two,
            shift_two,
        ) = weights_full
        grad_out = cotangent[batch_idx].astype(jnp.float32) * row_mask
        grad_res_two, grad_gain_two, grad_shift_two = norm_two_back(grad_out)
        grad_ffn_low = grad_res_two.astype(jnp.bfloat16)
        grad_act = contract_cols(grad_ffn_low, down_weight)
        (grad_up,) = gelu_back(grad_act)
        grad_up_low = grad_up.astype(jnp.bfloat16)
        grad_hidden = grad_res_two + contract_cols(grad_up_low, up_weight)
        grad_res_one, grad_gain_one, grad_shift_one = norm_one_back(grad_hidden)
        grad_attn_low = grad_res_one.astype(jnp.bfloat16)
        grad_ctx_low = contract_cols(grad_attn_low, out_weight).astype(jnp.bfloat16)
        keys_all, values_all = (
            lax.all_gather(key_part, "shard", axis=0, tiled=True),
            lax.all_gather(value_part, "shard", axis=0, tiled=True),
        )
        grad_q, grad_keys_all, grad_values_all = attend_backward(
            queries, keys_all, values_all, key_mask, lse_rows, grad_ctx_low
        )
        grad_keys, grad_values = (
            lax.psum_scatter(
                grad_keys_all.astype(jnp.bfloat16), "shard", scatter_dimension=0, tiled=True
            ).astype(jnp.float32),
            lax.psum_scatter(
                grad_values_all.astype(jnp.bfloat16), "shard", scatter_dimension=0, tiled=True
            ).astype(jnp.float32),
        )
        grad_qkv_low = jnp.concatenate([grad_q, grad_keys, grad_values], axis=1).astype(
            jnp.bfloat16
        )
        grad_input = grad_res_one + contract_cols(grad_qkv_low, qkv_weight)
        grad_rows.append(grad_input.astype(jnp.bfloat16))
        terms = (
            contract_rows(seq_in, grad_qkv_low),
            column_sums(grad_qkv_low[:, :width]),
            column_sums(grad_qkv_low[:, 2 * width :]),
            contract_rows(context_low, grad_attn_low),
            column_sums(grad_attn_low),
            grad_gain_one,
            grad_shift_one,
            contract_rows(hidden_low, grad_up_low),
            column_sums(grad_up_low),
            contract_rows(act_low, grad_ffn_low),
            column_sums(grad_ffn_low),
            grad_gain_two,
            grad_shift_two,
        )
        totals = [running + fresh for running, fresh in zip(totals, terms)]
    grad_local = (
        lax.psum_scatter(
            totals[0].astype(jnp.bfloat16), "shard", scatter_dimension=0, tiled=True
        ).astype(jnp.float32),
        lax.psum_scatter(
            totals[1].astype(jnp.bfloat16), "shard", scatter_dimension=0, tiled=True
        ).astype(jnp.float32),
        lax.psum_scatter(
            totals[2].astype(jnp.bfloat16), "shard", scatter_dimension=0, tiled=True
        ).astype(jnp.float32),
        lax.psum_scatter(
            totals[3].astype(jnp.bfloat16), "shard", scatter_dimension=0, tiled=True
        ).astype(jnp.float32),
        lax.psum_scatter(
            totals[4].astype(jnp.bfloat16), "shard", scatter_dimension=0, tiled=True
        ).astype(jnp.float32),
        lax.psum_scatter(
            totals[5].astype(jnp.bfloat16), "shard", scatter_dimension=0, tiled=True
        ).astype(jnp.float32),
        lax.psum_scatter(
            totals[6].astype(jnp.bfloat16), "shard", scatter_dimension=0, tiled=True
        ).astype(jnp.float32),
        lax.psum_scatter(
            totals[7].astype(jnp.bfloat16), "shard", scatter_dimension=0, tiled=True
        ).astype(jnp.float32),
        lax.psum_scatter(
            totals[8].astype(jnp.bfloat16), "shard", scatter_dimension=0, tiled=True
        ).astype(jnp.float32),
        lax.psum_scatter(
            totals[9].astype(jnp.bfloat16), "shard", scatter_dimension=0, tiled=True
        ).astype(jnp.float32),
        lax.psum_scatter(
            totals[10].astype(jnp.bfloat16), "shard", scatter_dimension=0, tiled=True
        ).astype(jnp.float32),
        lax.psum_scatter(
            totals[11].astype(jnp.bfloat16), "shard", scatter_dimension=0, tiled=True
        ).astype(jnp.float32),
        lax.psum_scatter(
            totals[12].astype(jnp.bfloat16), "shard", scatter_dimension=0, tiled=True
        ).astype(jnp.float32),
    )
    grad_total = (
        lax.psum(grad_local[0].astype(jnp.bfloat16), "grp").astype(jnp.float32),
        lax.psum(grad_local[1].astype(jnp.bfloat16), "grp").astype(jnp.float32),
        lax.psum(grad_local[2].astype(jnp.bfloat16), "grp").astype(jnp.float32),
        lax.psum(grad_local[3].astype(jnp.bfloat16), "grp").astype(jnp.float32),
        lax.psum(grad_local[4].astype(jnp.bfloat16), "grp").astype(jnp.float32),
        lax.psum(grad_local[5].astype(jnp.bfloat16), "grp").astype(jnp.float32),
        lax.psum(grad_local[6].astype(jnp.bfloat16), "grp").astype(jnp.float32),
        lax.psum(grad_local[7].astype(jnp.bfloat16), "grp").astype(jnp.float32),
        lax.psum(grad_local[8].astype(jnp.bfloat16), "grp").astype(jnp.float32),
        lax.psum(grad_local[9].astype(jnp.bfloat16), "grp").astype(jnp.float32),
        lax.psum(grad_local[10].astype(jnp.bfloat16), "grp").astype(jnp.float32),
        lax.psum(grad_local[11].astype(jnp.bfloat16), "grp").astype(jnp.float32),
        lax.psum(grad_local[12].astype(jnp.bfloat16), "grp").astype(jnp.float32),
    )
    return (
        jnp.stack(layer_rows),
        jnp.stack(grad_rows),
        grad_total[0],
        grad_total[1],
        grad_total[2],
        grad_total[3],
        grad_total[4],
        grad_total[5],
        grad_total[6],
        grad_total[7],
        grad_total[8],
        grad_total[9],
        grad_total[10],
        grad_total[11],
        grad_total[12],
    )


BF = jnp.bfloat16
GRANT = 60 << 20
COST = pl.CostEstimate(flops=1024, bytes_accessed=1024, transcendentals=0)
F32 = jnp.float32


def swap_core(value):
    return lax.ppermute(value, "grp", [(i, i ^ 1) for i in range(8)])


def swap_x(value):
    return lax.ppermute(value, "grp", [(i, i ^ 2) for i in range(8)])


def swap_y(value):
    return lax.ppermute(value, "grp", [(i, i ^ 4) for i in range(8)])


def swap_z(value, flip):
    return lax.ppermute(value, "shard", [(i, i ^ flip) for i in range(4)])


def swap_xy(value):
    return lax.ppermute(value, "grp", [(i, i ^ 6) for i in range(8)])


def dot32(left_mat, right_mat):
    return jnp.dot(left_mat, right_mat, preferred_element_type=F32)


def after(values, *others):
    return lax.optimization_barrier((values, others))[0]


def sequence_perm(flip):
    pairs = []
    for grp in range(8):
        for line in range(4):
            dst_grp = (grp & 6) | (line // 2)
            dst_line = 2 * (grp & 1) + ((line % 2) ^ flip)
            pairs.append((grp * 4 + line, dst_grp * 4 + dst_line))
    return pairs


def send_first(block):
    return lax.ppermute(block, ("grp", "shard"), sequence_perm(0))


def send_second(block):
    return lax.ppermute(block, ("grp", "shard"), sequence_perm(1))


def send_rows(first, second):
    return send_first(first), send_second(second)


def return_block(block, flip):
    return lax.ppermute(block, ("grp", "shard"), [(dst, src) for src, dst in sequence_perm(flip)])


def return_rows(first, second):
    return return_block(first, 0), return_block(second, 1)


def join_rows(first, second, parity):
    return jnp.where(parity == 0, jnp.stack([first, second]), jnp.stack([second, first]))


CORE, PLANE, LINE, PARITY = range(4)


def start_moves(moves, where_ref, sources, targets, sems):
    where = [where_ref[idx] for idx in range(4)]
    place = lambda at, unit: at if isinstance(at, int) else pl.multiple_of(at(*where), unit)
    copies = []
    for idx, (src, src_row, src_col, rows, cols, dst, dst_row, dst_col) in enumerate(moves):
        copies.append(
            pltpu.make_async_copy(
                sources[src].at[pl.ds(place(src_row, 8), rows), pl.ds(place(src_col, 128), cols)],
                targets[dst].at[pl.ds(place(dst_row, 8), rows), pl.ds(place(dst_col, 128), cols)],
                sems.at[idx],
            )
        )
    for copy in copies:
        copy.start()
    return copies


def move_kernel(count, moves, where_ref, *refs):
    for copy in start_moves(moves, where_ref, refs[:count], refs[count:-1], refs[-1]):
        copy.wait()


def move_blocks(where, sources, moves, shapes, grant=16 << 20):
    moved = sum(move[3] * move[4] for move in moves) * 2
    return pl.pallas_call(
        functools.partial(move_kernel, len(sources), moves),
        out_shape=[jax.ShapeDtypeStruct(shape, sources[0].dtype) for shape in shapes],
        in_specs=[pl.BlockSpec(memory_space=pltpu.SMEM)]
        + [pl.BlockSpec(memory_space=pl.ANY)] * len(sources),
        out_specs=[pl.BlockSpec(memory_space=pltpu.VMEM)] * len(shapes),
        scratch_shapes=[pltpu.SemaphoreType.DMA((len(moves),))],
        cost_estimate=COST,
        compiler_params=pltpu.CompilerParams(vmem_limit_bytes=grant),
    )(where, *sources)


def join_blocks(where, parts):
    moves, at = [], 0
    for idx, part in enumerate(parts):
        moves.append((idx, 0, 0, part.shape[0], part.shape[1], 0, at, 0))
        at += part.shape[0]
    return move_blocks(where, list(parts), moves, [(at, parts[0].shape[1])])[0]


def along_line(piece):
    return [swap_z(piece, flip) for flip in (1, 2, 3)]


def across_plane(came):
    return [swap_x(came), swap_y(came), swap_xy(came)]


def placed_moves(first_src, height, piece_rows, col, cols, dst):
    moves = []
    for flip in range(4):
        for step in range(1, 4):
            at = lambda core, plane, line, parity, flip=flip, step=step: (
                (line ^ step) * (4 * piece_rows) + (plane ^ flip) * piece_rows
            )
            moves.append((first_src + flip, (step - 1) * height, col, piece_rows, cols, dst, at, 0))
    return moves


def pick(arr, idx, axis):
    return lax.dynamic_index_in_dim(arr, idx, axis, keepdims=False)


def add_low(left, right):
    return (left.astype(F32) + right.astype(F32)).astype(BF)


def reduce_first(grads, cut, col, row):
    join = lambda arrs: arrs[0] if len(arrs) == 1 else jnp.concatenate(arrs, axis=-1)
    low_part = lambda idx: join([pick(grad[:, :, :, :cut], idx, 2) for grad in grads])
    high_part = lambda idx: join([pick(grad[:, :, :, cut:], idx, 1) for grad in grads])
    sent = (low_part(1 - col), high_part(1 - row))
    return (low_part(col), high_part(row), swap_x(sent[0]), swap_y(sent[1])), sent


def reduce_second(state, col, row):
    low, high, low_got, high_got = state
    low, high = add_low(low, low_got), add_low(high, high_got)
    sent = (pick(low, 1 - row, 1), pick(high, 1 - col, 1))
    return (pick(low, row, 1), pick(high, col, 1), swap_y(sent[0]), swap_x(sent[1])), sent


def reduce_near(states, line):
    mine = [
        jnp.concatenate([add_low(low, low_got), add_low(high, high_got)], axis=1)
        for low, high, low_got, high_got in states
    ]
    mine = mine[0] if len(mine) == 1 else jnp.concatenate(mine, axis=-1)
    pairs = mine.reshape((2, 2) + mine.shape[1:])
    sent = pick(pairs, 1 - line % 2, 1)
    return (pick(pairs, line % 2, 1), swap_z(sent, 1)), sent


def reduce_far(state, line):
    mine = add_low(*state)
    sent = pick(mine, 1 - line // 2, 0)
    return (pick(mine, line // 2, 0), swap_z(sent, 2)), sent


def direct_spread(state):
    piece = sum(part.astype(F32) for part in state).astype(BF)
    return [piece] + across_plane(piece), piece


def final_kernel(layout, rows, extra, flips, where_ref, mine_ref, other_ref, *outs):
    plane = where_ref[PLANE]
    height = mine_ref.shape[0] // 4

    low = where_ref[CORE] == 0
    for half in range(2):
        for at in range(4):
            part = plane ^ flips[at]
            for src_col, cols, dst, row_of, dst_col in layout(half):
                row = pl.multiple_of(row_of(part), 16)
                here = (pl.ds(at * height, rows), pl.ds(src_col, cols))
                mine, other = mine_ref[here], other_ref[here]
                value = jnp.where(low, mine, other) if half == 0 else jnp.where(low, other, mine)
                outs[dst][pl.ds(row, rows), pl.ds(dst_col, cols)] = value.astype(F32)
    if extra is not None:
        vecs = outs[-9:]
        slab = vecs[0].shape[0]
        for at in range(4):

            @pl.when(plane == flips[at])
            def _(at=at):
                begin, end = [
                    mine_ref[here, pl.ds(extra, 128)].astype(F32) + other_ref[here, pl.ds(extra, 128)].astype(F32)
                    for here in (pl.ds(at * height, 16), pl.ds(at * height + 16, 16))
                ]
                both = jnp.concatenate([begin, end], axis=1)
                for idx in range(8):
                    vecs[idx][...] = both[idx : idx + 1, :slab].reshape(slab)
                spread = jnp.concatenate([both, jnp.zeros((16, 4 * slab - 256), F32)], axis=1)
                lane = lax.broadcasted_iota(jnp.int32, spread.shape, 1)
                spread = jnp.where(lane < slab, spread, 0.0)
                wide = spread[8:9]
                for part in range(1, 4):
                    wide += pltpu.roll(spread[8 + part : 9 + part], part * slab, 1)
                vecs[8][...] = wide.reshape(4 * slab)


def spread_first(state, through_x):
    piece = add_low(*state)
    return piece, (swap_x if through_x else swap_y)(piece)


def spread_second(state, through_x):
    both = jnp.concatenate(state, axis=0)
    return both, (swap_y if through_x else swap_x)(both)


def spread_core(state):
    mine = jnp.concatenate(state, axis=0)
    return mine, swap_core(mine)


def finish_grad(where, state, through_x, layout, rows, shapes, extra=None):
    mine, other = state
    mine_flips = (0, 1, 2, 3) if through_x else (0, 2, 1, 3)
    shapes = list(shapes) + ([] if extra is None else [(shapes[0][0],)] * 8 + [(4 * shapes[0][0],)])
    vmem = pl.BlockSpec(memory_space=pltpu.VMEM)
    return pl.pallas_call(
        functools.partial(final_kernel, layout, rows, extra, mine_flips),
        out_shape=[jax.ShapeDtypeStruct(shape, F32) for shape in shapes],
        in_specs=[pl.BlockSpec(memory_space=pltpu.SMEM), vmem, vmem],
        out_specs=[vmem] * len(shapes),
        cost_estimate=COST,
        compiler_params=pltpu.CompilerParams(vmem_limit_bytes=16 << 20),
    )(where, mine, other)


ROWS = 256


def row_spec(width, shift=0, steps=1, block=ROWS):
    if shift:
        return pl.BlockSpec((block, width), lambda blk: ((blk + shift) % steps, 0))
    return pl.BlockSpec((block, width), lambda blk: (blk, 0))


def whole_spec(rows, width):
    return pl.BlockSpec((rows, width), lambda blk: (0, 0))


def mean_last(values):
    return jnp.mean(values, axis=-1, keepdims=True)


def norm_parts(values):
    centered = values - mean_last(values)
    scale = lax.rsqrt(mean_last(centered * centered) + eps)
    return centered * scale, scale


def norm_back(grad_normed, normed, scale):
    return scale * (grad_normed - mean_last(grad_normed) - normed * mean_last(grad_normed * normed))


def up_kernel(part_ref, got_ref, tok_ref, vec_ref, bias_ref, w_ref, low_ref, n_ref, r_ref, act_ref, slope_ref):
    vec = vec_ref[...]
    attn_out = part_ref[...].astype(F32) + got_ref[...].astype(F32) + vec[0:1]
    normed, scale = norm_parts(tok_ref[...].astype(F32) + attn_out)
    hidden = (normed * vec[1:2] + vec[2:3]).astype(BF)
    n_ref[...] = normed
    r_ref[...] = jnp.broadcast_to(scale, r_ref.shape)
    low_ref[...] = hidden
    for at in range(0, w_ref.shape[1], 384):
        cols = pl.ds(at, 384)
        up = dot32(hidden, w_ref[:, cols]) + bias_ref[:, cols]
        cdf = 0.5 + 0.5 * lax.erf(up * 0.5**0.5)
        act_ref[:, cols] = (up * cdf).astype(BF)
        slope = cdf + up * (jnp.exp(up * up * -0.5) * (2 * math.pi) ** -0.5)
        slope_ref[:, cols] = slope.astype(BF)


def ffn_up(part, got, tokens, vectors, up_bias, weight):
    rows, width = part.shape
    units = weight.shape[1]
    block = ROWS // 2
    steps = rows // block
    return pl.pallas_call(
        up_kernel,
        grid=(steps,),
        out_shape=[
            jax.ShapeDtypeStruct((rows, width), BF),
            jax.ShapeDtypeStruct((rows, width), F32),
            jax.ShapeDtypeStruct((rows, 128), F32),
            jax.ShapeDtypeStruct((rows, units), BF),
            jax.ShapeDtypeStruct((rows, units), BF),
        ],
        in_specs=[
            row_spec(width, block=block),
            row_spec(width, steps // 2, steps, block=block),
            row_spec(width, block=block),
            whole_spec(8, width),
            whole_spec(1, units),
            whole_spec(width, units),
        ],
        out_specs=[row_spec(width, block=block), row_spec(width, block=block), row_spec(128, block=block), row_spec(units, block=block), row_spec(units, block=block)],
        cost_estimate=COST,
        compiler_params=pltpu.CompilerParams(vmem_limit_bytes=20 << 20),
    )(part, got, tokens, vectors, up_bias, weight)


def turn_kernel(
    half_steps, part_ref, got_ref, n_ref, cot_ref, bias_ref, vec_ref, first_ref, second_ref, dr_ref, low_ref, sum_ref
):
    blk = pl.program_id(0)
    vec = vec_ref[...]
    hidden = n_ref[...] * vec[1:2] + vec[2:3]
    ffn_out = part_ref[...].astype(F32) + got_ref[...].astype(F32) + vec[3:4]
    normed, scale = norm_parts(hidden + ffn_out)
    mask = jnp.where(bias_ref[:, 0:1] < 0.0, 0.0, 1.0)
    result = ((normed * vec[4:5] + vec[5:6]) * mask).astype(BF)
    dy = cot_ref[...].astype(F32) * mask
    dr = norm_back(dy * vec[4:5], normed, scale)
    dr_low = dr.astype(BF)
    dr_ref[...] = dr
    low_ref[...] = dr_low

    @pl.when(blk == 0)
    def _():
        sum_ref[...] = jnp.zeros_like(sum_ref)
        first_ref[...] = result

    @pl.when(blk == 1)
    def _():
        second_ref[...] = result

    @pl.when(blk < half_steps)
    def _():
        sum_ref[0:1] += jnp.sum(dy * normed, axis=0, keepdims=True)
        sum_ref[1:2] += jnp.sum(dy, axis=0, keepdims=True)
        sum_ref[2:3] += jnp.sum(dr_low.astype(F32), axis=0, keepdims=True)


def norm_turn(part, got, n_one, cot, bias, vectors):
    rows, width = part.shape
    steps = rows // ROWS
    return pl.pallas_call(
        functools.partial(turn_kernel, steps // 2),
        grid=(steps,),
        out_shape=[jax.ShapeDtypeStruct((ROWS, width), BF)] * 2
        + [
            jax.ShapeDtypeStruct((rows, width), F32),
            jax.ShapeDtypeStruct((rows, width), BF),
            jax.ShapeDtypeStruct((8, width), F32),
        ],
        in_specs=[
            row_spec(width),
            row_spec(width, steps // 2, steps),
            row_spec(width),
            row_spec(width),
            row_spec(128),
            whole_spec(8, width),
        ],
        out_specs=[whole_spec(ROWS, width)] * 2 + [row_spec(width), row_spec(width), whole_spec(8, width)],
        cost_estimate=COST,
        compiler_params=pltpu.CompilerParams(vmem_limit_bytes=28 << 20),
    )(part, got, n_one, cot, bias, vectors)


def ffn_back_kernel(dffn_ref, down_ref, slope_ref, up_ref, dup_ref, part_ref, sum_ref):
    @pl.when(pl.program_id(0) == 0)
    def _():
        sum_ref[...] = jnp.zeros_like(sum_ref)

    total = jnp.zeros(part_ref.shape, F32)
    dffn = dffn_ref[...]
    for at in range(0, dup_ref.shape[1], 512):
        here = pl.ds(at, 512)
        dup = (contract_cols(dffn, down_ref[here, :]) * slope_ref[:, here].astype(F32)).astype(BF)
        dup_ref[:, here] = dup
        sum_ref[:, here] += jnp.sum(dup.astype(F32), axis=0, keepdims=True)
        total += contract_cols(dup, up_ref[:, here])
    part_ref[...] = total.astype(BF)


def ffn_back(dffn, down_weight, slope, up_weight):
    rows, width = dffn.shape
    units = slope.shape[1]
    return pl.pallas_call(
        ffn_back_kernel,
        grid=(rows // ROWS,),
        out_shape=[
            jax.ShapeDtypeStruct((rows, units), BF),
            jax.ShapeDtypeStruct((rows, width), BF),
            jax.ShapeDtypeStruct((1, units), F32),
        ],
        in_specs=[row_spec(width), whole_spec(units, width), row_spec(units), whole_spec(width, units)],
        out_specs=[row_spec(units), row_spec(width), whole_spec(1, units)],
        cost_estimate=COST,
        compiler_params=pltpu.CompilerParams(vmem_limit_bytes=20 << 20),
    )(dffn, down_weight, slope, up_weight)


def back_kernel(
    half_steps, where_ref, dr_ref, part_ref, got_ref, n_ref, r_ref, vec_ref, own_ref, low_ref, part_low_ref, sum_ref
):
    blk = pl.program_id(0)
    vec = vec_ref[...]
    normed = n_ref[...]
    dhidden = dr_ref[...] + (part_ref[...].astype(F32) + got_ref[...].astype(F32))
    dr = norm_back(dhidden * vec[1:2], normed, r_ref[:, 0:1])
    dr_low = dr.astype(BF)
    low_ref[...] = dr_low
    half = dr.shape[1] // 2
    part_low_ref[...] = jnp.where(where_ref[CORE] == 0, dr_low[:, :half], dr_low[:, half:])

    @pl.when(blk == 0)
    def _():
        sum_ref[...] = jnp.zeros_like(sum_ref)

    @pl.when(blk < half_steps)
    def _():
        own_ref[...] = dr
        sum_ref[0:1] += jnp.sum(dhidden * normed, axis=0, keepdims=True)
        sum_ref[1:2] += jnp.sum(dhidden, axis=0, keepdims=True)
        sum_ref[2:3] += jnp.sum(dr_low.astype(F32), axis=0, keepdims=True)


def norm_one_back(where, dr_two, part, got, n_one, r_one, vectors):
    rows, width = part.shape
    steps = rows // ROWS
    return pl.pallas_call(
        functools.partial(back_kernel, steps // 2),
        grid=(steps,),
        out_shape=[
            jax.ShapeDtypeStruct((rows // 2, width), F32),
            jax.ShapeDtypeStruct((rows, width), BF),
            jax.ShapeDtypeStruct((rows, width // 2), BF),
            jax.ShapeDtypeStruct((8, width), F32),
        ],
        in_specs=[
            pl.BlockSpec(memory_space=pltpu.SMEM),
            row_spec(width),
            row_spec(width),
            row_spec(width, steps // 2, steps),
            row_spec(width),
            row_spec(128),
            whole_spec(8, width),
        ],
        out_specs=[
            pl.BlockSpec((ROWS, width), lambda blk: (jnp.minimum(blk, steps // 2 - 1), 0)),
            row_spec(width),
            row_spec(width // 2),
            whole_spec(8, width),
        ],
        cost_estimate=COST,
        compiler_params=pltpu.CompilerParams(vmem_limit_bytes=28 << 20),
    )(where, dr_two, part, got, n_one, r_one, vectors)


Q_BLOCK = 512
PAIR = 128


def contract_last(left_mat, right_mat):
    return lax.dot_general(
        left_mat, right_mat, (((1,), (1,)), ((), ())), preferred_element_type=F32
    )


def head_lanes(block, head):
    lane = lax.broadcasted_iota(jnp.int32, block.shape, 1)
    return jnp.where((lane // HD) == head, block, jnp.zeros_like(block))


def attend_fwd_kernel(q_ref, k_ref, v_ref, bias_ref, ctx_ref, lse_ref, vt_ref, out_ref):
    vt_ref[...] = v_ref[...].T

    @pl.loop(0, q_ref.shape[0] // Q_BLOCK)
    def _(blk):
        at = pl.multiple_of(blk * Q_BLOCK, Q_BLOCK)

        @pl.loop(0, 2)
        def _(head):
            q_blk = q_ref[pl.ds(at, Q_BLOCK), :] * jnp.asarray(HD ** (-0.5), BF)
            here = pl.ds(pl.multiple_of(head * HD, HD), HD)
            scores = contract_last(k_ref[...], head_lanes(q_blk, head))
            scores = scores + jnp.concatenate([bias_ref[...]] * (Q_BLOCK // 128), axis=1)
            top = jnp.max(scores, axis=0, keepdims=True)
            exps = jnp.exp(scores - top)
            total = jnp.sum(exps, axis=0, keepdims=True)
            out_ref[here, :] = dot32(vt_ref[here, :], exps.astype(BF)) * (1.0 / total)
            lse_ref[0, pl.ds(head, 1), pl.ds(at, Q_BLOCK)] = top + jnp.log(total)

        ctx_ref[pl.ds(at, Q_BLOCK), :] = out_ref[...].T.astype(BF)


def attend_bwd_kernel(
    q_ref, k_ref, v_ref, bias_ref, lse_ref, grad_ref, dq_ref, dk_ref, dv_ref, kt_ref, dk_acc, dv_acc, out_ref
):
    kt_ref[...] = k_ref[...].T
    dk_acc[...] = jnp.zeros_like(dk_acc)
    dv_acc[...] = jnp.zeros_like(dv_acc)

    @pl.loop(0, q_ref.shape[0] // Q_BLOCK)
    def _(blk):
        at = pl.multiple_of(blk * Q_BLOCK, Q_BLOCK)

        @pl.loop(0, 2)
        def _(head):
            q_head = head_lanes(q_ref[pl.ds(at, Q_BLOCK), :] * jnp.asarray(HD ** (-0.5), BF), head)
            grad_head = head_lanes(grad_ref[pl.ds(at, Q_BLOCK), :], head)
            here = pl.ds(pl.multiple_of(head * HD, HD), HD)
            scores = contract_last(k_ref[...], q_head)
            scores = scores + jnp.concatenate([bias_ref[...]] * (Q_BLOCK // 128), axis=1)
            probs = jnp.exp(scores - lse_ref[0, pl.ds(head, 1), pl.ds(at, Q_BLOCK)])
            weighed = probs * contract_last(v_ref[...], grad_head)
            delta = jnp.sum(weighed, axis=0, keepdims=True)
            grad_scores = (weighed - probs * delta).astype(BF)
            dk_acc[...] += dot32(grad_scores, q_head)
            dv_acc[...] += dot32(probs.astype(BF), grad_head)
            out_ref[here, :] = dot32(kt_ref[here, :], grad_scores)

        dq_ref[pl.ds(at, Q_BLOCK), :] = (out_ref[...].T * (HD ** (-0.5))).astype(BF)

    dk_ref[...] = dk_acc[...].astype(BF)
    dv_ref[...] = dv_acc[...].astype(BF)


def column_spec(rows, first):
    return pl.BlockSpec((rows, PAIR), lambda pair: (0, first + pair))


def attend_chip_forward(qkv, bias, pair):
    rows, half = qkv.shape[0], qkv.shape[1] // 3
    pairs = half // PAIR
    return pl.pallas_call(
        attend_fwd_kernel,
        grid=(1,),
        out_shape=[
            jax.ShapeDtypeStruct((rows, PAIR), BF),
            jax.ShapeDtypeStruct((1, 2, rows), F32),
        ],
        in_specs=[column_spec(rows, idx * pairs + pair) for idx in range(3)]
        + [pl.BlockSpec((rows, 128), lambda step: (0, 0))],
        out_specs=[column_spec(rows, 0), pl.BlockSpec((1, 2, rows), lambda step: (0, 0, 0))],
        scratch_shapes=[pltpu.VMEM((PAIR, rows), BF), pltpu.VMEM((PAIR, Q_BLOCK), F32)],
        cost_estimate=COST,
        compiler_params=pltpu.CompilerParams(vmem_limit_bytes=28 << 20),
    )(qkv, qkv, qkv, bias)


def attend_chip_backward(qkv, bias, lse, grad_ctx, pair):
    rows, half = qkv.shape[0], qkv.shape[1] // 3
    pairs = half // PAIR
    return pl.pallas_call(
        attend_bwd_kernel,
        grid=(1,),
        out_shape=[jax.ShapeDtypeStruct((rows, PAIR), BF)] * 3,
        in_specs=[column_spec(rows, idx * pairs + pair) for idx in range(3)]
        + [
            pl.BlockSpec((rows, 128), lambda step: (0, 0)),
            pl.BlockSpec((1, 2, rows), lambda step: (0, 0, 0)),
            column_spec(rows, pair),
        ],
        out_specs=[column_spec(rows, 0)] * 3,
        scratch_shapes=[
            pltpu.VMEM((PAIR, rows), BF),
            pltpu.VMEM((rows, PAIR), F32),
            pltpu.VMEM((rows, PAIR), F32),
            pltpu.VMEM((PAIR, Q_BLOCK), F32),
        ],
        cost_estimate=COST,
        compiler_params=pltpu.CompilerParams(vmem_limit_bytes=32 << 20),
    )(qkv, qkv, qkv, bias, lse, grad_ctx)


def pack_kernel(count, moves, vec_at, slab, where_ref, *refs):
    sources, vecs = refs[:count], refs[count : count + 9]
    targets, sems = refs[count + 9 : -1], refs[-1]
    copies = start_moves(moves, where_ref, sources, targets, sems)
    dst, row = vec_at
    width = targets[dst].shape[1]
    rows = [vec[...].reshape(1, slab).astype(F32) for vec in vecs[:8]]
    wide = vecs[8][...].reshape(1, -1).astype(F32)
    count_wide = wide.shape[1] // slab
    rows += [wide[:, :slab]]
    rows += [pltpu.roll(wide, wide.shape[1] - idx * slab, 1)[:, :slab] for idx in range(1, count_wide)]
    rows += [jnp.zeros((4, slab), F32)]
    block = jnp.concatenate(rows, axis=0)
    targets[dst][pl.ds(row, 16), :] = jnp.concatenate(
        [block, jnp.zeros((16, width - slab), F32)], axis=1
    ).astype(BF)
    for copy in copies:
        copy.wait()


def pack_blocks(where, sources, vecs, moves, shapes, vec_at, slab):
    return pl.pallas_call(
        functools.partial(pack_kernel, len(sources), moves, vec_at, slab),
        out_shape=[jax.ShapeDtypeStruct(shape, BF) for shape in shapes],
        in_specs=[pl.BlockSpec(memory_space=pltpu.SMEM)]
        + [pl.BlockSpec(memory_space=pl.ANY)] * len(sources)
        + [pl.BlockSpec(memory_space=pltpu.VMEM)] * len(vecs),
        out_specs=[pl.BlockSpec(memory_space=pltpu.VMEM)] * len(shapes),
        scratch_shapes=[pltpu.SemaphoreType.DMA((len(moves),))],
        cost_estimate=COST,
        compiler_params=pltpu.CompilerParams(vmem_limit_bytes=60 << 20),
    )(where, *sources, *vecs)


def vector_kernel(height, at, slab, where_ref, own_ref, came_ref, block_ref, qkv_ref, up_ref, buf, sems):
    line = where_ref[LINE]
    copies = [pltpu.make_async_copy(own_ref.at[pl.ds(at, 16)], buf.at[line], sems.at[0])]
    for step in range(1, 4):
        copies.append(
            pltpu.make_async_copy(
                came_ref.at[pl.ds((step - 1) * height + at, 16)], buf.at[line ^ step], sems.at[step]
            )
        )
    for copy in copies:
        copy.start()
    for copy in copies:
        copy.wait()
    width = block_ref.shape[1]
    half = width // 2
    joined = jnp.zeros((16, width), F32)
    lane = lax.broadcasted_iota(jnp.int32, (16, width), 1)
    wide = []
    for idx in range(4):
        rows = jnp.where(lane < slab, buf[idx, :, :width].astype(F32), 0.0)
        joined += rows if idx == 0 else pltpu.roll(rows, idx * slab, 1)
        row = rows[8:9]
        for part in range(1, 4):
            row += pltpu.roll(rows[8 + part : 9 + part], part * slab, 1)
        wide.append(row)
    low = where_ref[CORE] == 0
    pick_half = lambda row: jnp.where(low, row[:, :half], row[:, half:])
    block_ref[...] = jnp.concatenate([joined[2:8], jnp.zeros((2, width), F32)], axis=0)
    qkv_ref[...] = jnp.concatenate(
        [pick_half(joined[0:1]), jnp.zeros((1, half), F32), pick_half(joined[1:2])], axis=1
    )
    up_ref[...] = jnp.concatenate([pick_half(row) for row in wide], axis=1)


def join_vectors(where, own, came, at, slab, width):
    height = came.shape[0] // 3
    return pl.pallas_call(
        functools.partial(vector_kernel, height, at, slab),
        out_shape=[
            jax.ShapeDtypeStruct((8, width), F32),
            jax.ShapeDtypeStruct((1, 3 * width // 2), F32),
            jax.ShapeDtypeStruct((1, 2 * width), F32),
        ],
        in_specs=[pl.BlockSpec(memory_space=pltpu.SMEM)] + [pl.BlockSpec(memory_space=pl.ANY)] * 2,
        out_specs=[pl.BlockSpec(memory_space=pltpu.VMEM)] * 3,
        scratch_shapes=[pltpu.VMEM((4, 16, own.shape[1]), BF), pltpu.SemaphoreType.DMA((4,))],
        cost_estimate=COST,
        compiler_params=pltpu.CompilerParams(vmem_limit_bytes=4 << 20),
    )(where, own, came)


def small_kernel(slab, where_ref, one_ref, two_ref, up_ref, qkv_ref, out_ref):
    width = one_ref.shape[1]
    half = width // 2
    low = where_ref[CORE] == 0
    zero = jnp.zeros((1, half), F32)
    on_core = lambda row: jnp.where(
        low, jnp.concatenate([row, zero], axis=1), jnp.concatenate([zero, row], axis=1)
    )
    one, two = one_ref[...], two_ref[...]
    rows = jnp.concatenate(
        [
            on_core(qkv_ref[:, :half]),
            on_core(qkv_ref[:, 2 * half :]),
            one[2:3],
            one[0:1],
            one[1:2],
            two[2:3],
            two[0:1],
            two[1:2],
        ],
        axis=0,
    )
    out_ref[...] = jnp.zeros_like(out_ref)
    for idx in range(4):
        wide = on_core(up_ref[:, idx * half : (idx + 1) * half])
        at = lambda row, part: row if part == 0 else pltpu.roll(row, width - part * slab, 1)
        parts = [at(wide, part)[:, :256] for part in range(4)]
        block = jnp.concatenate([at(rows, idx)[:, :256]] + parts + [jnp.zeros((4, 256), F32)], axis=0)
        lane = lax.broadcasted_iota(jnp.int32, block.shape, 1)
        block = jnp.where(lane < slab, block, 0.0).astype(BF)
        out_ref[idx, 0:16, :] = block[:, :128]
        out_ref[idx, 16:32, :] = block[:, 128:]


def small_grads(where, sums_one, sums_two, up_sums, qkv_sums, slab):
    vmem = pl.BlockSpec(memory_space=pltpu.VMEM)
    return pl.pallas_call(
        functools.partial(small_kernel, slab),
        out_shape=jax.ShapeDtypeStruct((4, slab // 4, 128), BF),
        in_specs=[pl.BlockSpec(memory_space=pltpu.SMEM)] + [vmem] * 4,
        out_specs=vmem,
        compiler_params=pltpu.CompilerParams(vmem_limit_bytes=4 << 20),
    )(where, sums_one, sums_two, up_sums, qkv_sums)


def per_device_chip(
    tokens,
    cotangent,
    lengths,
    w_qkv,
    bias_q,
    bias_v,
    w_out,
    bias_out,
    gain_attn,
    shift_attn,
    w_up,
    bias_up,
    w_down,
    bias_down,
    gain_ffn,
    shift_ffn,
):
    quarter, width = tokens.shape[1:]
    half_rows = 2 * quarter
    units = w_up.shape[1] // 2
    slab = w_qkv.shape[0]
    wide = w_down.shape[0]
    half = width // 2
    slab_part, wide_part = slab // 4, wide // 8
    vec_rows = 16
    group = lax.axis_index("grp")
    line = lax.axis_index("shard")
    core = group % 2
    plane = group // 2
    col, row = plane % 2, plane // 2
    parity = line % 2
    where = jnp.stack([core, plane, line, parity]).astype(jnp.int32)

    vecs = [bias_q, bias_v, bias_out, gain_attn, shift_attn, bias_down, gain_ffn, shift_ffn, bias_up]
    moves = []
    slab_at = lambda c, p, z, e: p * slab_part
    for idx in range(3):
        at = lambda c, p, z, e, idx=idx: idx * width + c * half
        moves.append((0, slab_at, at, slab_part, half, 0, 0, idx * half))
    (qkv_piece,) = pack_blocks(
        where, [w_qkv], vecs, moves, [(slab_part + vec_rows, 3 * half)], (0, slab_part), slab
    )
    qkv_parts = along_line(qkv_piece)
    moves = []
    for idx in range(2):
        moves.append((idx, lambda c, p, z, e: e * quarter, 0, quarter, width, 2 * idx, 0, 0))
        moves.append((idx, lambda c, p, z, e: (1 - e) * quarter, 0, quarter, width, 2 * idx + 1, 0, 0))
    for idx in range(4):
        at = lambda c, p, z, e, idx=idx: idx * wide + c * (wide // 2)
        moves.append((2, slab_at, at, slab_part, wide // 2, 4, 0, idx * (wide // 2)))
    moves.append((3, slab_at, lambda c, p, z, e: c * half, slab_part, half, 4, 0, units))
    moves.append((4, lambda c, p, z, e: c * (wide // 2) + p * wide_part, 0, wide_part, width, 5, 0, 0))
    tok_first, tok_second, cot_first, cot_second, up_piece, down_piece = move_blocks(
        where,
        [after(tokens.reshape(half_rows, width), qkv_parts[0]), cotangent.reshape(half_rows, width), w_up, w_out, w_down],
        moves,
        [(quarter, width)] * 4 + [(slab_part, units + half), (wide_part, width)],
        grant=GRANT,
    )
    slab_start = lambda c, p, z, e: z * slab

    stack = lambda parts: join_blocks(where, parts)
    len_other = swap_core(lengths)
    len_all = jnp.where(core == 0, jnp.concatenate([lengths, len_other]), jnp.concatenate([len_other, lengths]))
    seq_len = len_all[line]
    place = lax.broadcasted_iota(jnp.int32, (4 * quarter, 128), 0)
    place = ((place // quarter) ^ (2 * core + parity)) * quarter + place % quarter
    bias = jnp.where(place < seq_len, 0.0, masked_score).astype(F32)
    tok_first, tok_second = send_rows(tok_first, tok_second)
    qkv_came = stack(after(qkv_parts, bias, down_piece))
    qkv_plane = across_plane(qkv_came)
    vec_block, qkv_bias, up_bias = join_vectors(where, qkv_piece, qkv_came, slab_part, slab, width)
    tok_own = stack(after([tok_first, tok_second], vec_block, *qkv_plane))
    up_parts = along_line(after(up_piece, tok_own))
    tok_all = stack([tok_own, swap_core(tok_own)])

    moves = []
    for idx in range(3):
        at = lambda c, p, z, e, idx=idx: idx * width + c * half
        moves.append((0, 0, at, slab, half, 0, slab_start, idx * half))
    moves += placed_moves(1, slab_part + vec_rows, slab_part, 0, 3 * half, 0)
    (qkv_weight,) = move_blocks(
        where, [w_qkv, after(qkv_came, vec_block)] + qkv_plane, moves, [(width, 3 * half)]
    )

    qkv = (dot32(tok_all, qkv_weight) + qkv_bias).astype(BF)
    pairs = half // PAIR
    contexts, lses = [], []
    for pair in range(pairs):
        qkv_in = after(qkv, contexts[-1]) if contexts else qkv
        if pair == 1:
            up_came = stack(after(up_parts, contexts[0]))
            up_plane = across_plane(up_came)
            down_far = swap_z(after(down_piece, up_came), 2)
            cot_first = send_first(after(cot_first, up_came))
            qkv_in = after(qkv, up_came)
        elif pair == 2:
            down_two = stack(after([down_piece, down_far], contexts[1]))
            down_near = swap_z(down_two, 1)
            cot_second = send_second(after(cot_second, down_two))
            qkv_in = after(qkv, down_two)
        got = attend_chip_forward(qkv_in, bias, pair)
        contexts.append(got[0])
        lses.append(got[1])
    context = jnp.concatenate(contexts, axis=1)
    down_near = after(down_near, context)
    down_came = stack([down_near[:wide_part], down_far, down_near[wide_part:]])
    cot_own = stack(after([cot_first, cot_second], down_came))

    moves = []
    for idx in range(4):
        at = lambda c, p, z, e, idx=idx: idx * wide + c * (wide // 2)
        moves.append((0, 0, at, slab, wide // 2, 0, slab_start, idx * (wide // 2)))
    moves.append((1, 0, lambda c, p, z, e: c * half, slab, half, 1, slab_start, 0))
    moves += placed_moves(2, slab_part, slab_part, 0, units, 0)
    moves += placed_moves(2, slab_part, slab_part, units, half, 1)
    up_weight, out_half = move_blocks(
        where,
        [w_up, w_out, after(up_came, down_came, cot_own)] + up_plane,
        moves,
        [(width, units), (width, half)],
    )
    out_got = swap_core(out_half)
    down_plane = across_plane(after(down_came, out_half))
    moves = [
        (0, lambda c, p, z, e: c * half, 0, half, half, 0, 0, lambda c, p, z, e: c * half),
        (1, lambda c, p, z, e: c * half, 0, half, half, 0, 0, lambda c, p, z, e: (1 - c) * half),
    ]
    (out_weight,) = move_blocks(where, [out_half, out_got], moves, [(half, width)])
    part = dot32(context, out_weight).astype(BF)
    got = swap_core(part)
    hidden_low, n_one, r_one, act, slope = ffn_up(part, got, tok_all, vec_block, up_bias, up_weight)

    cot_all = stack([cot_own, swap_core(cot_own)])
    moves = [
        (0, 0, 0, 4 * quarter, half, 0, 0, lambda c, p, z, e: c * half),
        (1, 0, 0, half_rows, half, 0, half_rows, lambda c, p, z, e: (1 - c) * half),
        (1, half_rows, 0, half_rows, half, 0, 0, lambda c, p, z, e: (1 - c) * half),
    ]
    (context_all,) = move_blocks(
        where, [context, swap_core(after(context, cot_own))], moves, [(4 * quarter, width)]
    )
    moves = [(0, lambda c, p, z, e: c * (wide // 2), 0, wide // 2, width, 0, lambda c, p, z, e: z * (wide // 2), 0)]
    moves += placed_moves(1, wide_part, wide_part, 0, width, 0)
    (down_weight,) = move_blocks(where, [w_down, after(down_came, act, cot_all, context_all)] + down_plane, moves, [(units, width)])
    part = dot32(act, down_weight).astype(BF)
    out_first, out_second, dr_two, dffn, sums_two = norm_turn(
        part, swap_core(part), n_one, cot_all, bias, vec_block
    )

    blocks = lambda grad: grad.reshape(4, 2, 2, grad.shape[0] // 16, grad.shape[1])
    g_down = contract_rows(act, dffn).astype(BF)
    down_state, sent = reduce_first([blocks(g_down)], wide_part // 2, col, row)
    dffn = after(dffn, sent)
    dup, part, up_sums = ffn_back(dffn, down_weight, slope, up_weight)
    got = swap_core(part)
    dup_late = after(dup, part)
    g_up = contract_rows(hidden_low, dup_late).astype(BF)
    up_state, sent_up = reduce_first([blocks(g_up)], slab_part // 2, col, row)
    dr_one, dattn, dattn_part, sums_one = norm_one_back(
        where, dr_two, part, after(got, sent_up), n_one, r_one, vec_block
    )
    grad_ctx = contract_cols(dattn, out_weight).astype(BF)
    g_out = contract_rows(context_all, after(dattn_part, grad_ctx)).astype(BF)
    down_state, sent = reduce_second(after(down_state, g_out), col, row)
    layer_first = return_block(after(out_first, g_down), 0)
    layer_second = return_block(after(out_second, layer_first, g_out), 1)

    dqkv = []
    side = lambda parts: jnp.concatenate(parts, axis=1)
    qkv_in = after(qkv, sent)
    dqkv.append(attend_chip_backward(qkv_in, bias, lses[0], grad_ctx, 0))
    layer_out = join_rows(*after((layer_first, layer_second), dqkv[-1]), parity)
    down_state, sent = reduce_near([after(down_state, layer_out)], line)
    up_state, sent_up = reduce_second(after(up_state, sent), col, row)
    qkv_in = after(qkv, sent_up)
    for pair in range(1, pairs - 1):
        dqkv.append(attend_chip_backward(qkv_in, bias, lses[pair], grad_ctx, pair))
    most = side([part[idx] for idx in range(3) for part in dqkv])
    g_most = contract_rows(tok_all, most).astype(BF)
    most_state, sent = reduce_first([blocks(g_most), blocks(g_out)], slab_part // 2, col, row)
    down_state, sent = reduce_far(after(down_state, sent), line)
    up_state, sent_up = reduce_near([after(up_state, sent)], line)
    qkv_in = after(qkv, sent_up)
    dqkv.append(attend_chip_backward(qkv_in, bias, lses[-1], grad_ctx, pairs - 1))
    most_state, sent = reduce_second(after(most_state, dqkv[-1]), col, row)
    last = side(dqkv[-1])
    g_last = contract_rows(tok_all, after(last, sent)).astype(BF)
    dqkv = side([part[idx] for idx in range(3) for part in dqkv])
    qkv_sums = jnp.sum(dqkv.astype(F32), axis=0, keepdims=True)
    small = small_grads(where, sums_one, sums_two, up_sums, qkv_sums, slab)
    small = jnp.pad(small[:, None, None], ((0, 0), (0, 1), (0, 1), (0, 0), (0, 0)))
    last_state, sent = reduce_first([blocks(g_last), small], slab_part // 2, col, row)
    down_state = spread_first(after(down_state, sent), True)
    up_state, sent_up = reduce_far(after(up_state, down_state[0]), line)
    dqkv = after(dqkv, sent_up)
    dtok_low = contract_cols(dqkv[half_rows:], qkv_weight).astype(BF)
    dtok_got = swap_core(dtok_low)
    grad_tok = contract_cols(after(dqkv[:half_rows], dtok_low), qkv_weight) + dr_one
    last_state, sent = reduce_second(after(last_state, grad_tok), col, row)
    down_state = spread_second(after(down_state, sent), True)
    grad_tok = (after(grad_tok, down_state[0]) + dtok_got.astype(F32)).astype(BF)
    back_first = return_block(grad_tok[:quarter], 0)
    up_state = spread_first(after(up_state, grad_tok), False)
    attn_state, sent = reduce_near([most_state, after(last_state, up_state[0])], line)
    down_state = spread_core(after(down_state, sent))
    up_state = spread_second(after(up_state, down_state[0]), False)
    attn_state, sent = reduce_far(after(attn_state, up_state[0], back_first), line)
    back_second = return_block(after(grad_tok[quarter:], sent), 1)
    up_state = spread_core(after(up_state, sent))
    down_layout = lambda half_at: [(0, width, 0, lambda part: half_at * (wide // 2) + part * wide_part, 0)]
    (grad_down,) = finish_grad(where, after(down_state, up_state[0]), True, down_layout, wide_part, [(wide, width)])
    slab_row = lambda part: part * slab_part
    up_layout = lambda half_at: [
        (idx * (wide // 2), wide // 2, 0, slab_row, idx * wide + half_at * (wide // 2)) for idx in range(4)
    ]
    (grad_up,) = finish_grad(
        where, after(up_state, grad_down), False, up_layout, slab_part, [(slab, 2 * units)]
    )
    attn_state, sent = direct_spread(after(attn_state, grad_up))
    attn_state = spread_core(attn_state)
    span = half - PAIR
    attn_layout = lambda half_at: (
        [(idx * span, span, 0, slab_row, idx * width + half_at * half) for idx in range(3)]
        + [(3 * span, half, 1, slab_row, half_at * half)]
        + [
            (3 * span + half + idx * PAIR, PAIR, 0, slab_row, idx * width + half_at * half + span)
            for idx in range(3)
        ]
    )
    grad_qkv, grad_out, *vec_grads = finish_grad(
        where, after(attn_state, grad_up), True, attn_layout, slab_part, [(slab, 3 * width), (slab, width)], 4 * half
    )
    grad_tokens = join_rows(*after((back_first, back_second), grad_qkv), parity)
    vec_of = lambda idx: vec_grads[idx]
    return (
        layer_out,
        grad_tokens,
        grad_qkv,
        vec_of(0),
        vec_of(1),
        grad_out,
        vec_of(2),
        vec_of(3),
        vec_of(4),
        grad_up,
        vec_of(8),
        grad_down,
        vec_of(5),
        vec_of(6),
        vec_of(7),
    )


def solution(mesh):
    placed = (
        P("grp", "shard", None),
        P("grp", "shard", None),
        P("grp"),
        P("shard", None),
        P("shard"),
        P("shard"),
        P("shard", None),
        P("shard"),
        P("shard"),
        P("shard"),
        P("shard", None),
        P("shard"),
        P("shard", None),
        P("shard"),
        P("shard"),
        P("shard"),
    )
    plan = per_device_chip if dict(mesh.shape) == {"grp": 8, "shard": 4} else per_device
    return jax.shard_map(
        plan,
        mesh=mesh,
        in_specs=placed,
        out_specs=(
            P("grp", "shard", None),
            P("grp", "shard", None),
            P("shard", None),
            P("shard"),
            P("shard"),
            P("shard", None),
            P("shard"),
            P("shard"),
            P("shard"),
            P("shard", None),
            P("shard"),
            P("shard", None),
            P("shard"),
            P("shard"),
            P("shard"),
        ),
        check_vma=False,
    )
```

profile of v0, /device:TPU:1, one launch (start us, length us, event | category | flops | bytes accessed | tf_op | source)
XLA Modules:
  0.0 298.1 jit_solution(10823434297649857211)
XLA Ops:
  1.3 2.3 shard_map.271.own_ref
  3.6 2.2 collective-permute-start
  5.8 2.3 collective-permute-start.3
  13.2 3.6 %shard_map.272 = (bf16[256,768]{1,0:T(8,128)(2,1)}, bf16[256,768]{1,0:T(8,128)(2,1)}, bf16[256,768]{1,0:T(8,128)(2,1)}, bf16[256,768]{1,0:T(8,128)(2,1)}, bf16[4...) custom-call(s32[4]{0:T(128)} %pad_add_fusion.where_ref, bf16[512,768]{1,0:T(8,128)(2,1)} %bitcast.196, ...), custom_call_target="tpu_custom_call" | custom-call | flops 1024 | bytes 1024 | tf_op jit(solution)/shard_map/pallas_call | solution.py:498
  21.7 8.8 %collective-permute-start.1 = (bf16[256,768]{1,0:T(8,128)(2,1)}, bf16[256,768]{1,0:T(8,128)(2,1)S(1)}, u32[]{:S(2)}, u32[]{:S(2)}) collective-permute-start(bf16[256,768]{1,0:T(8,128)(2,1)} %get-tuple-element.167), channel_id=1, source_target_pairs={{0,0},{1,1},{2,4},{3,5},{4,2},{5,3},{6,6},{7,7},{8,8},{9,9},{10,12... | collective-permute-start | bytes 1179656 | tf_op jit(solution)/shard_map/ppermute | solution.py:448
  31.5 12.6 %collective-permute-done.1.refs_0_ = bf16[256,768]{1,0:T(8,128)(2,1)S(1)} collective-permute-done((bf16[256,768]{1,0:T(8,128)(2,1)}, bf16[256,768]{1,0:T(8,128)(2,1)S(1)}, u32[]{:S(2)}, u32[]{:S(2)}) %collective-permute-start.1) | collective-permute-done | bytes 393248 | tf_op jit(solution)/shard_map/ppermute | solution.py:448
  46.6 4.6 %collective-permute-start.10 = (bf16[48,1920]{1,0:T(8,128)(2,1)}, bf16[48,1920]{1,0:T(8,128)(2,1)S(1)}, u32[]{:S(2)}, u32[]{:S(2)}) collective-permute-start(bf16[48,1920]{1,0:T(8,128)(2,1)} %get-tuple-element.180), channel_id=1, source_target_pairs={{0,1},{1,0},{2,3},{3,2},{4,5},{5,4},{6,7},{7,6},{8,9},{9,8},{10,11... | collective-permute-start | bytes 552968 | tf_op jit(solution)/shard_map/ppermute | solution.py:422
  55.5 2.5 shard_map.277
  59.8 2.2 add_convert_fusion.q_ref.k_ref.v_ref
  62.0 4.4 %shard_map.278 = (bf16[1024,128]{1,0:T(8,128)(2,1)S(1)}, f32[1,2,1024]{2,1,0:T(2,128)S(1)}) custom-call(bf16[1024,1152]{1,0:T(8,128)(2,1)S(1)} %add_convert_fusion.q_ref.k_ref.v_ref, bf16[1024,1152]{1,0:T(8,128)(2,1)S(1)} %add_convert_fusion.q_ref.k_ref.v_ref, bf16[1024,1152]{1,0:T(8,128)(2,1)S(1)} %add_convert_fusion.q_ref.k_ref.v_ref, ...), custom_call_target="tpu_custom_call" | custom-call | flops 1024 | bytes 1024 | tf_op jit(solution)/shard_map/pallas_call | solution.py:947
  67.8 5.1 %collective-permute-start.13 = (bf16[96,768]{1,0:T(8,128)(2,1)S(1)}, bf16[96,768]{1,0:T(8,128)(2,1)S(1)}, u32[]{:S(2)}, u32[]{:S(2)}) collective-permute-start(bf16[96,768]{1,0:T(8,128)(2,1)S(1)} %copy-done.29), channel_id=1, source_target_pairs={{0,2},{1,3},{2,0},{3,1},{4,6},{5,7},{6,4},{7,5},{8,10},{9,11},{10,... | collective-permute-start | bytes 442376 | tf_op jit(solution)/shard_map/ppermute | solution.py:422
  72.9 4.4 %shard_map.280 = (bf16[1024,128]{1,0:T(8,128)(2,1)S(1)}, f32[1,2,1024]{2,1,0:T(2,128)S(1)}) custom-call(bf16[1024,1152]{1,0:T(8,128)(2,1)S(1)} %add_convert_fusion.q_ref.k_ref.v_ref, bf16[1024,1152]{1,0:T(8,128)(2,1)S(1)} %add_convert_fusion.q_ref.k_ref.v_ref, bf16[1024,1152]{1,0:T(8,128)(2,1)S(1)} %add_convert_fusion.q_ref.k_ref.v_ref, ...), custom_call_target="tpu_custom_call" | custom-call | flops 1024 | bytes 1024 | tf_op jit(solution)/shard_map/pallas_call | solution.py:947
  77.3 2.6 collective-permute-done.13.refs_1_
  83.6 5.0 %collective-permute-start.15 = (bf16[256,768]{1,0:T(8,128)(2,1)S(1)}, bf16[256,768]{1,0:T(8,128)(2,1)S(1)}, u32[]{:S(2)}, u32[]{:S(2)}) collective-permute-start(bf16[256,768]{1,0:T(8,128)(2,1)S(1)} %copy-done.35), channel_id=1, source_target_pairs={{0,0},{1,1},{2,4},{3,5},{4,2},{5,3},{6,6},{7,7},{8,8},{9,9},{10,12... | collective-permute-start | bytes 1179656 | tf_op jit(solution)/shard_map/ppermute | solution.py:448
  89.6 4.4 %shard_map.282 = (bf16[1024,128]{1,0:T(8,128)(2,1)S(1)}, f32[1,2,1024]{2,1,0:T(2,128)S(1)}) custom-call(bf16[1024,1152]{1,0:T(8,128)(2,1)S(1)} %add_convert_fusion.q_ref.k_ref.v_ref, bf16[1024,1152]{1,0:T(8,128)(2,1)S(1)} %add_convert_fusion.q_ref.k_ref.v_ref, bf16[1024,1152]{1,0:T(8,128)(2,1)S(1)} %add_convert_fusion.q_ref.k_ref.v_ref, ...), custom_call_target="tpu_custom_call" | custom-call | flops 1024 | bytes 1024 | tf_op jit(solution)/shard_map/pallas_call | solution.py:947
  95.3 2.0 collective-permute-done.15.refs_0_
  97.3 5.2 %collective-permute-done.16.refs_1_ = bf16[256,768]{1,0:T(8,128)(2,1)S(1)} collective-permute-done((bf16[256,768]{1,0:T(8,128)(2,1)S(1)}, bf16[256,768]{1,0:T(8,128)(2,1)S(1)}, u32[]{:S(2)}, u32[]{:S(2)}) %collective-permute-start.16) | collective-permute-done | bytes 393248 | tf_op jit(solution)/shard_map/ppermute | solution.py:452
  103.4 3.3 %collective-permute-done.19.refs_5_ = bf16[144,1920]{1,0:T(8,128)(2,1)S(1)} collective-permute-done((bf16[144,1920]{1,0:T(8,128)(2,1)S(1)}, bf16[144,1920]{1,0:T(8,128)(2,1)S(1)}, u32[]{:S(2)}, u32[]{:S(2)}) %collective-permute-start.19) | collective-permute-done | bytes 552992 | tf_op jit(solution)/shard_map/ppermute | solution.py:426
  108.3 2.2 collective-permute-start.20
  116.2 2.2 collective-permute-done.22.refs_1_
  122.2 7.0 %shard_map.287 = (bf16[1024,768]{1,0:T(8,128)(2,1)S(1)}, f32[1024,768]{1,0:T(8,128)S(1)}, f32[1024,128]{1,0:T(8,128)S(1)}, bf16[1024,1536]{1,0:T(8,128)(2,1)S(1)}, bf16[1024,1536]{1,0:T(8,128)(2,1)S(1)}) custom-call(bf16[1024,768]{1,0:T(8,128)(2,1)S(1)} %convolution_convert_fusion.2.part_ref, bf16[1024,768]{1,0:T(8,128)(2,1)S(1)} %collective-permute-done.21.got_ref, ...), custom_call_target="tpu_custom_call" | custom-call | flops 1024 | bytes 1024 | tf_op jit(solution)/shard_map/pallas_call | solution.py:698
  132.0 4.7 %collective-permute-done.26.refs_4_ = bf16[288,768]{1,0:T(8,128)(2,1)S(1)} collective-permute-done((bf16[288,768]{1,0:T(8,128)(2,1)S(1)}, bf16[288,768]{1,0:T(8,128)(2,1)S(1)}, u32[]{:S(2)}, u32[]{:S(2)}) %collective-permute-start.26) | collective-permute-done | bytes 442400 | tf_op jit(solution)/shard_map/ppermute | solution.py:426
  136.8 3.1 %shard_map.290.down_ref = bf16[1536,768]{1,0:T(8,128)(2,1)S(1)} custom-call(s32[4]{0:T(128)S(1)} %copy-done.28, bf16[768,768]{1,0:T(8,128)(2,1)S(1)} %copy-done.12, bf16[288,768]{1,0:T(8,128)(2,1)S(1)} %shard_map.283.refs_1_, bf16[288,768]{1,0:T(8,128)(2,1)S(1)} %collective-permute-done.24.refs_2_, bf16[288,768]{1,0:T(8,128)(2,1)S(1)} %collective-permute-done.25.refs_3_, ...), custom_call_target="tpu_custom_call" | custom-call | flops 1024 | bytes 1024 | tf_op jit(solution)/shard_map/pallas_call | solution.py:498
  139.9 3.7 %convolution_convert_fusion.3.part_ref = bf16[1024,768]{1,0:T(8,128)(2,1)} fusion(bf16[1024,1536]{1,0:T(8,128)(2,1)S(1)} %get-tuple-element.202, bf16[1536,768]{1,0:T(8,128)(2,1)S(1)} %shard_map.290.down_ref), kind=kOutput, calls=%fused_computation.5 | convolution fusion | flops 2416705536 | bytes 7077888 | tf_op jit(solution)/shard_map/dot_general | solution.py:430
  144.6 3.4 %collective-permute-done.27.got_ref = bf16[1024,768]{1,0:T(8,128)(2,1)} collective-permute-done((bf16[1024,768]{1,0:T(8,128)(2,1)}, bf16[1024,768]{1,0:T(8,128)(2,1)}, u32[]{:S(2)}, u32[]{:S(2)}) %collective-permute-start.27) | collective-permute-done | bytes 1572896 | tf_op jit(solution)/shard_map/ppermute | solution.py:410
  147.9 1.9 copy-done.1
  151.2 5.4 %shard_map.291 = (bf16[256,768]{1,0:T(8,128)(2,1)S(1)}, bf16[256,768]{1,0:T(8,128)(2,1)S(1)}, f32[1024,768]{1,0:T(8,128)S(1)}, bf16[1024,768]{1,0:T(8,128)(2,1)S(1)}, f32[8,768]{1,0:T(8,128)S(1)}) custom-call(bf16[1024,768]{1,0:T(8,128)(2,1)} %convolution_convert_fusion.3.part_ref, bf16[1024,768]{1,0:T(8,128)(2,1)} %collective-permute-done.27.got_ref, ...), custom_call_target="tpu_custom_call" | custom-call | flops 1024 | bytes 1024 | tf_op jit(solution)/shard_map/pallas_call | solution.py:757
  156.7 2.9 convolution_convert_fusion.1
  161.9 2.9 collective-permute-start.28
  164.8 6.7 %shard_map.292 = (bf16[1024,1536]{1,0:T(8,128)(2,1)S(1)}, bf16[1024,768]{1,0:T(8,128)(2,1)S(1)}, f32[1,1536]{1,0:T(1,128)S(1)}) custom-call(bf16[1024,768]{1,0:T(8,128)(2,1)S(1)} %get-tuple-element.212.dffn_ref, bf16[1536,768]{1,0:T(8,128)(2,1)S(1)} %copy-done.6, bf16[1024,1536]{1,0:T(8,128)(2,1)S(1)} %copy-done.15, bf16[768,1536]{1,0:T(8,128)(2,1)S(1)} %copy-done.4), custom_call_target="tpu_custom_call" | custom-call | flops 1024 | bytes 1024 | tf_op jit(solution)/shard_map/pallas_call | solution.py:799
  171.6 3.0 convolution_convert_fusion
  176.9 3.1 %shard_map.293 = (f32[512,768]{1,0:T(8,128)S(1)}, bf16[1024,768]{1,0:T(8,128)(2,1)S(1)}, bf16[1024,384]{1,0:T(8,128)(2,1)S(1)}, f32[8,768]{1,0:T(8,128)S(1)}) custom-call(s32[4]{0:T(128)S(1)} %copy-done.28, f32[1024,768]{1,0:T(8,128)S(1)} %get-tuple-element.211.dr_ref, bf16[1024,768]{1,0:T(8,128)(2,1)S(1)} %get-tuple-element.214.part_ref, ...), custom_call_target="tpu_custom_call" | custom-call | flops 1024 | bytes 1024 | tf_op jit(solution)/shard_map/pallas_call | solution.py:842
  182.5 3.3 %collective-permute-start.30 = (bf16[256,768]{1,0:T(8,128)(2,1)S(1)}, bf16[256,768]{1,0:T(8,128)(2,1)S(1)}, u32[]{:S(2)}, u32[]{:S(2)}) collective-permute-start(bf16[256,768]{1,0:T(8,128)(2,1)S(1)} %get-tuple-element.223), channel_id=1, source_target_pairs={{1,0},{0,1},{5,2},{4,3},{3,4},{2,5},{7,6},{6,7},{9,8},{8,9},{13,10... | collective-permute-start | bytes 1179656 | tf_op jit(solution)/shard_map/ppermute | solution.py:460
  188.2 7.4 %shard_map.294 = (bf16[1024,128]{1,0:T(8,128)(2,1)S(1)}, bf16[1024,128]{1,0:T(8,128)(2,1)S(1)}, bf16[1024,128]{1,0:T(8,128)(2,1)S(1)}) custom-call(bf16[1024,1152]{1,0:T(8,128)(2,1)S(1)} %add_convert_fusion.q_ref.k_ref.v_ref, bf16[1024,1152]{1,0:T(8,128)(2,1)S(1)} %add_convert_fusion.q_ref.k_ref.v_ref, ...), custom_call_target="tpu_custom_call" | custom-call | flops 1024 | bytes 1024 | tf_op jit(solution)/shard_map/pallas_call | solution.py:966
  199.0 7.7 %shard_map.295 = (bf16[1024,128]{1,0:T(8,128)(2,1)S(1)}, bf16[1024,128]{1,0:T(8,128)(2,1)S(1)}, bf16[1024,128]{1,0:T(8,128)(2,1)S(1)}) custom-call(bf16[1024,1152]{1,0:T(8,128)(2,1)S(1)} %add_convert_fusion.q_ref.k_ref.v_ref, bf16[1024,1152]{1,0:T(8,128)(2,1)S(1)} %add_convert_fusion.q_ref.k_ref.v_ref, ...), custom_call_target="tpu_custom_call" | custom-call | flops 1024 | bytes 1024 | tf_op jit(solution)/shard_map/pallas_call | solution.py:966
  215.3 7.4 %shard_map.296 = (bf16[1024,128]{1,0:T(8,128)(2,1)S(1)}, bf16[1024,128]{1,0:T(8,128)(2,1)S(1)}, bf16[1024,128]{1,0:T(8,128)(2,1)S(1)}) custom-call(bf16[1024,1152]{1,0:T(8,128)(2,1)S(1)} %add_convert_fusion.q_ref.k_ref.v_ref, bf16[1024,1152]{1,0:T(8,128)(2,1)S(1)} %add_convert_fusion.q_ref.k_ref.v_ref, ...), custom_call_target="tpu_custom_call" | custom-call | flops 1024 | bytes 1024 | tf_op jit(solution)/shard_map/pallas_call | solution.py:966
  234.7 4.6 %collective-permute-start.47 = (bf16[512,768]{1,0:T(8,128)(2,1)S(1)}, bf16[512,768]{1,0:T(8,128)(2,1)S(1)}, u32[]{:S(2)}, u32[]{:S(2)}) collective-permute-start(bf16[512,768]{1,0:T(8,128)(2,1)S(1)} %convolution_convert_fusion.6), channel_id=1, source_target_pairs={{0,4},{4,0},{8,12},{12,8},{16,20},{20,16},{24,28},{28,24},{1,5},{5... | collective-permute-start | bytes 2359304 | tf_op jit(solution)/shard_map/ppermute | solution.py:410
  243.1 4.4 %collective-permute-start.48 = (bf16[256,768]{1,0:T(8,128)(2,1)S(1)}, bf16[256,768]{1,0:T(8,128)(2,1)S(1)}, u32[]{:S(2)}, u32[]{:S(2)}) collective-permute-start(bf16[256,768]{1,0:T(8,128)(2,1)S(1)} %get-tuple-element.332), channel_id=1, source_target_pairs={{0,0},{1,1},{4,2},{5,3},{2,4},{3,5},{6,6},{7,7},{8,8},{9,9},{12,10... | collective-permute-start | bytes 1179656 | tf_op jit(solution)/shard_map/ppermute | solution.py:460
  251.6 1.8 collective-permute-done.55
  254.2 7.7 %collective-permute-done.54 = bf16[2,48,1664]{2,1,0:T(8,128)(2,1)S(1)} collective-permute-done((bf16[2,48,1664]{2,1,0:T(8,128)(2,1)S(1)}, bf16[2,48,1664]{2,1,0:T(8,128)(2,1)S(1)}, u32[]{:S(2)}, u32[]{:S(2)}) %collective-permute-start.54) | collective-permute-done | bytes 319520 | tf_op jit(solution)/shard_map/ppermute | solution.py:422
  265.1 2.2 shard_map.298
  267.3 2.1 shard_map.299
  269.5 4.0 %collective-permute-done.58 = bf16[48,1664]{1,0:T(8,128)(2,1)S(1)} collective-permute-done((bf16[48,1664]{1,0:T(8,128)(2,1)S(1)}, bf16[48,1664]{1,0:T(8,128)(2,1)S(1)}, u32[]{:S(2)}, u32[]{:S(2)}) %collective-permute-start.58) | collective-permute-done | bytes 159776 | tf_op jit(solution)/shard_map/ppermute | solution.py:422
  276.2 3.1 %collective-permute-done.64 = bf16[48,1664]{1,0:T(8,128)(2,1)S(1)} collective-permute-done((bf16[48,1664]{1,0:T(8,128)(2,1)S(1)}, bf16[48,1664]{1,0:T(8,128)(2,1)S(1)}, u32[]{:S(2)}, u32[]{:S(2)}) %collective-permute-start.64) | collective-permute-done | bytes 159776 | tf_op jit(solution)/shard_map/ppermute | solution.py:426
  279.3 4.1 %collective-permute-done.63 = bf16[48,1664]{1,0:T(8,128)(2,1)S(1)} collective-permute-done((bf16[48,1664]{1,0:T(8,128)(2,1)S(1)}, bf16[48,1664]{1,0:T(8,128)(2,1)S(1)}, u32[]{:S(2)}, u32[]{:S(2)}) %collective-permute-start.63) | collective-permute-done | bytes 159776 | tf_op jit(solution)/shard_map/ppermute | solution.py:418
  284.3 2.9 collective-permute-start.57
  287.2 2.2 shard_map.300
  289.5 7.2 %collective-permute-done.57 = bf16[256,768]{1,0:T(8,128)(2,1)S(1)} collective-permute-done((bf16[256,768]{1,0:T(8,128)(2,1)S(1)}, bf16[256,768]{1,0:T(8,128)(2,1)S(1)}, u32[]{:S(2)}, u32[]{:S(2)}) %collective-permute-start.57) | collective-permute-done | bytes 393248 | tf_op jit(solution)/shard_map/ppermute | solution.py:460
  (312 shorter events, 93.6 us)
Async XLA Ops:
  3.6 9.6 %collective-permute-start = (bf16[64,1152]{1,0:T(8,128)(2,1)}, bf16[64,1152]{1,0:T(8,128)(2,1)S(1)}, u32[]{:S(2)}, u32[]{:S(2)}) collective-permute-start(bf16[64,1152]{1,0:T(8,128)(2,1)} %shard_map.271.own_ref), channel_id=1, source_target_pairs={{0,1},{1,0},{2,3},{3,2},{4,5},{5,4},{6,7},{7,6},{8,9},{9,8},{10,11... | collective-permute-start | bytes 442376 | tf_op jit(solution)/shard_map/ppermute | solution.py:422
  5.8 11.1 %collective-permute-start.3 = (bf16[64,1152]{1,0:T(8,128)(2,1)}, bf16[64,1152]{1,0:T(8,128)(2,1)S(1)}, u32[]{:S(2)}, u32[]{:S(2)}) collective-permute-start(bf16[64,1152]{1,0:T(8,128)(2,1)} %shard_map.271.own_ref), channel_id=1, source_target_pairs={{0,2},{1,3},{2,0},{3,1},{4,6},{5,7},{6,4},{7,5},{8,10},{9,11},{10,... | collective-permute-start | bytes 442376 | tf_op jit(solution)/shard_map/ppermute | solution.py:422
  8.1 9.7 %collective-permute-start.4 = (bf16[64,1152]{1,0:T(8,128)(2,1)}, bf16[64,1152]{1,0:T(8,128)(2,1)S(1)}, u32[]{:S(2)}, u32[]{:S(2)}) collective-permute-start(bf16[64,1152]{1,0:T(8,128)(2,1)} %shard_map.271.own_ref), channel_id=1, source_target_pairs={{0,3},{1,2},{2,1},{3,0},{4,7},{5,6},{6,5},{7,4},{8,11},{9,10},{10,... | collective-permute-start | bytes 442376 | tf_op jit(solution)/shard_map/ppermute | solution.py:422
  19.0 25.1 %collective-permute-start.6 = (bf16[192,1152]{1,0:T(8,128)(2,1)S(1)}, bf16[192,1152]{1,0:T(8,128)(2,1)S(1)}, u32[]{:S(2)}, u32[]{:S(2)}) collective-permute-start(bf16[192,1152]{1,0:T(8,128)(2,1)S(1)} %shard_map.273.came_ref.refs_1_), channel_id=1, source_target_pairs={{0,8},{4,12},{8,0},{12,4},{16,24},{20,28},{24,16},{28,20},{1,9},{5... | collective-permute-start | bytes 1327112 | tf_op jit(solution)/shard_map/ppermute | solution.py:414
  20.2 23.8 %collective-permute-start.7 = (bf16[192,1152]{1,0:T(8,128)(2,1)S(1)}, bf16[192,1152]{1,0:T(8,128)(2,1)S(1)}, u32[]{:S(2)}, u32[]{:S(2)}) collective-permute-start(bf16[192,1152]{1,0:T(8,128)(2,1)S(1)} %shard_map.273.came_ref.refs_1_), channel_id=1, source_target_pairs={{0,16},{4,20},{8,24},{12,28},{16,0},{20,4},{24,8},{28,12},{1,17},{... | collective-permute-start | bytes 1327112 | tf_op jit(solution)/shard_map/ppermute | solution.py:418
  21.5 23.3 %collective-permute-start.8 = (bf16[192,1152]{1,0:T(8,128)(2,1)S(1)}, bf16[192,1152]{1,0:T(8,128)(2,1)S(1)}, u32[]{:S(2)}, u32[]{:S(2)}) collective-permute-start(bf16[192,1152]{1,0:T(8,128)(2,1)S(1)} %shard_map.273.came_ref.refs_1_), channel_id=1, source_target_pairs={{0,24},{4,28},{8,16},{12,20},{16,8},{20,12},{24,0},{28,4},{1,25},{... | collective-permute-start | bytes 1327112 | tf_op jit(solution)/shard_map/ppermute | solution.py:426
  21.7 22.3 %collective-permute-start.1 = (bf16[256,768]{1,0:T(8,128)(2,1)}, bf16[256,768]{1,0:T(8,128)(2,1)S(1)}, u32[]{:S(2)}, u32[]{:S(2)}) collective-permute-start(bf16[256,768]{1,0:T(8,128)(2,1)} %get-tuple-element.167), channel_id=1, source_target_pairs={{0,0},{1,1},{2,4},{3,5},{4,2},{5,3},{6,6},{7,7},{8,8},{9,9},{10,12... | collective-permute-start | bytes 1179656 | tf_op jit(solution)/shard_map/ppermute | solution.py:448
  30.5 13.5 %collective-permute-start.2 = (bf16[256,768]{1,0:T(8,128)(2,1)}, bf16[256,768]{1,0:T(8,128)(2,1)S(1)}, u32[]{:S(2)}, u32[]{:S(2)}) collective-permute-start(bf16[256,768]{1,0:T(8,128)(2,1)} %get-tuple-element.168), channel_id=1, source_target_pairs={{0,1},{1,0},{2,5},{3,4},{4,3},{5,2},{6,7},{7,6},{8,9},{9,8},{10,13... | collective-permute-start | bytes 1179656 | tf_op jit(solution)/shard_map/ppermute | solution.py:452
  46.5 11.5 %collective-permute-start.9 = (bf16[512,768]{1,0:T(8,128)(2,1)S(1)}, bf16[512,768]{1,0:T(8,128)(2,1)}, u32[]{:S(2)}, u32[]{:S(2)}) collective-permute-start(bf16[512,768]{1,0:T(8,128)(2,1)S(1)} %shard_map.275.refs_0_), channel_id=1, source_target_pairs={{0,4},{4,0},{8,12},{12,8},{16,20},{20,16},{24,28},{28,24},{1,5},{5... | collective-permute-start | bytes 2359304 | tf_op jit(solution)/shard_map/ppermute | solution.py:410
  46.6 19.8 %collective-permute-start.10 = (bf16[48,1920]{1,0:T(8,128)(2,1)}, bf16[48,1920]{1,0:T(8,128)(2,1)S(1)}, u32[]{:S(2)}, u32[]{:S(2)}) collective-permute-start(bf16[48,1920]{1,0:T(8,128)(2,1)} %get-tuple-element.180), channel_id=1, source_target_pairs={{0,1},{1,0},{2,3},{3,2},{4,5},{5,4},{6,7},{7,6},{8,9},{9,8},{10,11... | collective-permute-start | bytes 552968 | tf_op jit(solution)/shard_map/ppermute | solution.py:422
  51.2 15.2 %collective-permute-start.11 = (bf16[48,1920]{1,0:T(8,128)(2,1)}, bf16[48,1920]{1,0:T(8,128)(2,1)S(1)}, u32[]{:S(2)}, u32[]{:S(2)}) collective-permute-start(bf16[48,1920]{1,0:T(8,128)(2,1)} %get-tuple-element.180), channel_id=1, source_target_pairs={{0,2},{1,3},{2,0},{3,1},{4,6},{5,7},{6,4},{7,5},{8,10},{9,11},{10,... | collective-permute-start | bytes 552968 | tf_op jit(solution)/shard_map/ppermute | solution.py:422
  52.3 14.1 %collective-permute-start.12 = (bf16[48,1920]{1,0:T(8,128)(2,1)}, bf16[48,1920]{1,0:T(8,128)(2,1)S(1)}, u32[]{:S(2)}, u32[]{:S(2)}) collective-permute-start(bf16[48,1920]{1,0:T(8,128)(2,1)} %get-tuple-element.180), channel_id=1, source_target_pairs={{0,3},{1,2},{2,1},{3,0},{4,7},{5,6},{6,5},{7,4},{8,11},{9,10},{10,... | collective-permute-start | bytes 552968 | tf_op jit(solution)/shard_map/ppermute | solution.py:422
  67.8 12.1 %collective-permute-start.13 = (bf16[96,768]{1,0:T(8,128)(2,1)S(1)}, bf16[96,768]{1,0:T(8,128)(2,1)S(1)}, u32[]{:S(2)}, u32[]{:S(2)}) collective-permute-start(bf16[96,768]{1,0:T(8,128)(2,1)S(1)} %copy-done.29), channel_id=1, source_target_pairs={{0,2},{1,3},{2,0},{3,1},{4,6},{5,7},{6,4},{7,5},{8,10},{9,11},{10,... | collective-permute-start | bytes 442376 | tf_op jit(solution)/shard_map/ppermute | solution.py:422
  80.9 22.6 %collective-permute-start.17 = (bf16[144,1920]{1,0:T(8,128)(2,1)S(1)}, bf16[144,1920]{1,0:T(8,128)(2,1)S(1)}, u32[]{:S(2)}, u32[]{:S(2)}) collective-permute-start(bf16[144,1920]{1,0:T(8,128)(2,1)S(1)} %shard_map.279.refs_2_), channel_id=1, source_target_pairs={{0,8},{4,12},{8,0},{12,4},{16,24},{20,28},{24,16},{28,20},{1,9},{5... | collective-permute-start | bytes 1658888 | tf_op jit(solution)/shard_map/ppermute | solution.py:414
  82.1 21.3 %collective-permute-start.18 = (bf16[144,1920]{1,0:T(8,128)(2,1)S(1)}, bf16[144,1920]{1,0:T(8,128)(2,1)S(1)}, u32[]{:S(2)}, u32[]{:S(2)}) collective-permute-start(bf16[144,1920]{1,0:T(8,128)(2,1)S(1)} %shard_map.279.refs_2_), channel_id=1, source_target_pairs={{0,16},{4,20},{8,24},{12,28},{16,0},{20,4},{24,8},{28,12},{1,17},{... | collective-permute-start | bytes 1658888 | tf_op jit(solution)/shard_map/ppermute | solution.py:418
  83.4 23.4 %collective-permute-start.19 = (bf16[144,1920]{1,0:T(8,128)(2,1)S(1)}, bf16[144,1920]{1,0:T(8,128)(2,1)S(1)}, u32[]{:S(2)}, u32[]{:S(2)}) collective-permute-start(bf16[144,1920]{1,0:T(8,128)(2,1)S(1)} %shard_map.279.refs_2_), channel_id=1, source_target_pairs={{0,24},{4,28},{8,16},{12,20},{16,8},{20,12},{24,0},{28,4},{1,25},{... | collective-permute-start | bytes 1658888 | tf_op jit(solution)/shard_map/ppermute | solution.py:426
  83.6 13.7 %collective-permute-start.15 = (bf16[256,768]{1,0:T(8,128)(2,1)S(1)}, bf16[256,768]{1,0:T(8,128)(2,1)S(1)}, u32[]{:S(2)}, u32[]{:S(2)}) collective-permute-start(bf16[256,768]{1,0:T(8,128)(2,1)S(1)} %copy-done.35), channel_id=1, source_target_pairs={{0,0},{1,1},{2,4},{3,5},{4,2},{5,3},{6,6},{7,7},{8,8},{9,9},{10,12... | collective-permute-start | bytes 1179656 | tf_op jit(solution)/shard_map/ppermute | solution.py:448
  88.6 13.8 %collective-permute-start.16 = (bf16[256,768]{1,0:T(8,128)(2,1)S(1)}, bf16[256,768]{1,0:T(8,128)(2,1)S(1)}, u32[]{:S(2)}, u32[]{:S(2)}) collective-permute-start(bf16[256,768]{1,0:T(8,128)(2,1)S(1)} %copy-done.34), channel_id=1, source_target_pairs={{0,1},{1,0},{2,5},{3,4},{4,3},{5,2},{6,7},{7,6},{8,9},{9,8},{10,13... | collective-permute-start | bytes 1179656 | tf_op jit(solution)/shard_map/ppermute | solution.py:452
  114.7 17.3 %collective-permute-start.24 = (bf16[288,768]{1,0:T(8,128)(2,1)S(1)}, bf16[288,768]{1,0:T(8,128)(2,1)S(1)}, u32[]{:S(2)}, u32[]{:S(2)}) collective-permute-start(bf16[288,768]{1,0:T(8,128)(2,1)S(1)} %shard_map.283.refs_1_), channel_id=1, source_target_pairs={{0,8},{4,12},{8,0},{12,4},{16,24},{20,28},{24,16},{28,20},{1,9},{5... | collective-permute-start | bytes 1327112 | tf_op jit(solution)/shard_map/ppermute | solution.py:414
  115.6 16.4 %collective-permute-start.25 = (bf16[288,768]{1,0:T(8,128)(2,1)S(1)}, bf16[288,768]{1,0:T(8,128)(2,1)S(1)}, u32[]{:S(2)}, u32[]{:S(2)}) collective-permute-start(bf16[288,768]{1,0:T(8,128)(2,1)S(1)} %shard_map.283.refs_1_), channel_id=1, source_target_pairs={{0,16},{4,20},{8,24},{12,28},{16,0},{20,4},{24,8},{28,12},{1,17},{... | collective-permute-start | bytes 1327112 | tf_op jit(solution)/shard_map/ppermute | solution.py:418
  118.3 18.4 %collective-permute-start.26 = (bf16[288,768]{1,0:T(8,128)(2,1)S(1)}, bf16[288,768]{1,0:T(8,128)(2,1)S(1)}, u32[]{:S(2)}, u32[]{:S(2)}) collective-permute-start(bf16[288,768]{1,0:T(8,128)(2,1)S(1)} %shard_map.283.refs_1_), channel_id=1, source_target_pairs={{0,24},{4,28},{8,16},{12,20},{16,8},{20,12},{24,0},{28,4},{1,25},{... | collective-permute-start | bytes 1327112 | tf_op jit(solution)/shard_map/ppermute | solution.py:426
  159.9 25.8 %collective-permute-start.31 = (bf16[4,2,48,768]{3,2,1,0:T(8,128)(2,1)S(1)}, bf16[4,2,48,768]{3,2,1,0:T(8,128)(2,1)S(1)}, u32[]{:S(2)}, u32[]{:S(2)}) collective-permute-start(bf16[4,2,48,768]{3,2,1,0:T(8,128)(2,1)S(1)} %get-tuple-element.330), channel_id=1, source_target_pairs={{0,8},{4,12},{8,0},{12,4},{16,24},{20,28},{24,16},{28,20},{1,9},{5... | collective-permute-start | bytes 1769480 | tf_op jit(solution)/shard_map/ppermute | solution.py:414
  160.6 25.2 %collective-permute-start.32 = (bf16[4,2,48,768]{3,2,1,0:T(8,128)(2,1)S(1)}, bf16[4,2,48,768]{3,2,1,0:T(8,128)(2,1)S(1)}, u32[]{:S(2)}, u32[]{:S(2)}) collective-permute-start(bf16[4,2,48,768]{3,2,1,0:T(8,128)(2,1)S(1)} %get-tuple-element.328), channel_id=1, source_target_pairs={{0,16},{4,20},{8,24},{12,28},{16,0},{20,4},{24,8},{28,12},{1,17},{... | collective-permute-start | bytes 1769480 | tf_op jit(solution)/shard_map/ppermute | solution.py:418
  161.9 20.6 %collective-permute-start.28 = (bf16[256,768]{1,0:T(8,128)(2,1)S(1)}, bf16[256,768]{1,0:T(8,128)(2,1)S(1)}, u32[]{:S(2)}, u32[]{:S(2)}) collective-permute-start(bf16[256,768]{1,0:T(8,128)(2,1)S(1)} %get-tuple-element.209), channel_id=1, source_target_pairs={{0,0},{1,1},{4,2},{5,3},{2,4},{3,5},{6,6},{7,7},{8,8},{9,9},{12,10... | collective-permute-start | bytes 1179656 | tf_op jit(solution)/shard_map/ppermute | solution.py:460
  175.0 22.2 %collective-permute-start.33 = (bf16[4,2,24,1536]{3,2,1,0:T(8,128)(2,1)S(1)}, bf16[4,2,24,1536]{3,2,1,0:T(8,128)(2,1)S(1)}, u32[]{:S(2)}, u32[]{:S(2)}) collective-permute-start(bf16[4,2,24,1536]{3,2,1,0:T(8,128)(2,1)S(1)} %get-tuple-element.326), channel_id=1, source_target_pairs={{0,8},{4,12},{8,0},{12,4},{16,24},{20,28},{24,16},{28,20},{1,9},{5... | collective-permute-start | bytes 1769480 | tf_op jit(solution)/shard_map/ppermute | solution.py:414
  176.4 20.8 %collective-permute-start.34 = (bf16[4,2,24,1536]{3,2,1,0:T(8,128)(2,1)S(1)}, bf16[4,2,24,1536]{3,2,1,0:T(8,128)(2,1)S(1)}, u32[]{:S(2)}, u32[]{:S(2)}) collective-permute-start(bf16[4,2,24,1536]{3,2,1,0:T(8,128)(2,1)S(1)} %get-tuple-element.324), channel_id=1, source_target_pairs={{0,16},{4,20},{8,24},{12,28},{16,0},{20,4},{24,8},{28,12},{1,17},{... | collective-permute-start | bytes 1769480 | tf_op jit(solution)/shard_map/ppermute | solution.py:418
  182.5 13.2 %collective-permute-start.30 = (bf16[256,768]{1,0:T(8,128)(2,1)S(1)}, bf16[256,768]{1,0:T(8,128)(2,1)S(1)}, u32[]{:S(2)}, u32[]{:S(2)}) collective-permute-start(bf16[256,768]{1,0:T(8,128)(2,1)S(1)} %get-tuple-element.223), channel_id=1, source_target_pairs={{1,0},{0,1},{5,2},{4,3},{3,4},{2,5},{7,6},{6,7},{9,8},{8,9},{13,10... | collective-permute-start | bytes 1179656 | tf_op jit(solution)/shard_map/ppermute | solution.py:460
  186.2 10.7 %collective-permute-start.35 = (bf16[4,48,768]{2,1,0:T(8,128)(2,1)S(1)}, bf16[4,48,768]{2,1,0:T(8,128)(2,1)S(1)}, u32[]{:S(2)}, u32[]{:S(2)}) collective-permute-start(bf16[4,48,768]{2,1,0:T(8,128)(2,1)S(1)} %get-tuple-element.354), channel_id=1, source_target_pairs={{0,16},{4,20},{8,24},{12,28},{16,0},{20,4},{24,8},{28,12},{1,17},{... | collective-permute-start | bytes 884744 | tf_op jit(solution)/shard_map/ppermute | solution.py:418
  186.8 10.1 %collective-permute-start.36 = (bf16[4,48,768]{2,1,0:T(8,128)(2,1)S(1)}, bf16[4,48,768]{2,1,0:T(8,128)(2,1)S(1)}, u32[]{:S(2)}, u32[]{:S(2)}) collective-permute-start(bf16[4,48,768]{2,1,0:T(8,128)(2,1)S(1)} %get-tuple-element.352), channel_id=1, source_target_pairs={{0,8},{4,12},{8,0},{12,4},{16,24},{20,28},{24,16},{28,20},{1,9},{5... | collective-permute-start | bytes 884744 | tf_op jit(solution)/shard_map/ppermute | solution.py:414
  197.6 14.3 %collective-permute-start.37 = (bf16[4,24,1536]{2,1,0:T(8,128)(2,1)S(1)}, bf16[4,24,1536]{2,1,0:T(8,128)(2,1)S(1)}, u32[]{:S(2)}, u32[]{:S(2)}) collective-permute-start(bf16[4,24,1536]{2,1,0:T(8,128)(2,1)S(1)} %get-tuple-element.350), channel_id=1, source_target_pairs={{0,16},{4,20},{8,24},{12,28},{16,0},{20,4},{24,8},{28,12},{1,17},{... | collective-permute-start | bytes 884744 | tf_op jit(solution)/shard_map/ppermute | solution.py:418
  197.9 14.0 %collective-permute-start.38 = (bf16[4,24,1536]{2,1,0:T(8,128)(2,1)S(1)}, bf16[4,24,1536]{2,1,0:T(8,128)(2,1)S(1)}, u32[]{:S(2)}, u32[]{:S(2)}) collective-permute-start(bf16[4,24,1536]{2,1,0:T(8,128)(2,1)S(1)} %get-tuple-element.348), channel_id=1, source_target_pairs={{0,8},{4,12},{8,0},{12,4},{16,24},{20,28},{24,16},{28,20},{1,9},{5... | collective-permute-start | bytes 884744 | tf_op jit(solution)/shard_map/ppermute | solution.py:414
  199.0 12.8 %collective-permute-start.39 = (bf16[2,96,768]{2,1,0:T(8,128)(2,1)S(1)}, bf16[2,96,768]{2,1,0:T(8,128)(2,1)S(1)}, u32[]{:S(2)}, u32[]{:S(2)}) collective-permute-start(bf16[2,96,768]{2,1,0:T(8,128)(2,1)S(1)} %get-tuple-element.346), channel_id=1, source_target_pairs={{0,1},{1,0},{2,3},{3,2},{4,5},{5,4},{6,7},{7,6},{8,9},{9,8},{10,11... | collective-permute-start | bytes 884744 | tf_op jit(solution)/shard_map/ppermute | solution.py:422
  209.9 14.7 %collective-permute-start.42 = (bf16[4,2,24,1152]{3,2,1,0:T(8,128)(2,1)S(1)}, bf16[4,2,24,1152]{3,2,1,0:T(8,128)(2,1)S(1)}, u32[]{:S(2)}, u32[]{:S(2)}) collective-permute-start(bf16[4,2,24,1152]{3,2,1,0:T(8,128)(2,1)S(1)} %pad_maximum_fusion.4), channel_id=1, source_target_pairs={{0,8},{4,12},{8,0},{12,4},{16,24},{20,28},{24,16},{28,20},{1,9},{5... | collective-permute-start | bytes 1327112 | tf_op jit(solution)/shard_map/ppermute | solution.py:414
  210.9 13.7 %collective-permute-start.43 = (bf16[4,2,24,1152]{3,2,0,1:T(8,128)(2,1)S(1)}, bf16[4,2,24,1152]{3,2,0,1:T(8,128)(2,1)S(1)}, u32[]{:S(2)}, u32[]{:S(2)}) collective-permute-start(bf16[4,2,24,1152]{3,2,0,1:T(8,128)(2,1)S(1)} %pad_maximum_fusion.5), channel_id=1, source_target_pairs={{0,16},{4,20},{8,24},{12,28},{16,0},{20,4},{24,8},{28,12},{1,17},{... | collective-permute-start | bytes 1327112 | tf_op jit(solution)/shard_map/ppermute | solution.py:418
  212.2 17.2 %collective-permute-start.40 = (bf16[2,48,1536]{2,1,0:T(8,128)(2,1)S(1)}, bf16[2,48,1536]{2,1,0:T(8,128)(2,1)S(1)}, u32[]{:S(2)}, u32[]{:S(2)}) collective-permute-start(bf16[2,48,1536]{2,1,0:T(8,128)(2,1)S(1)} %get-tuple-element.342), channel_id=1, source_target_pairs={{0,1},{1,0},{2,3},{3,2},{4,5},{5,4},{6,7},{7,6},{8,9},{9,8},{10,11... | collective-permute-start | bytes 884744 | tf_op jit(solution)/shard_map/ppermute | solution.py:422
  213.7 14.9 %collective-permute-start.41 = (bf16[96,768]{1,0:T(8,128)(2,1)S(1)}, bf16[96,768]{1,0:T(8,128)(2,1)S(1)}, u32[]{:S(2)}, u32[]{:S(2)}) collective-permute-start(bf16[96,768]{1,0:T(8,128)(2,1)S(1)} %get-tuple-element.368), channel_id=1, source_target_pairs={{0,2},{1,3},{2,0},{3,1},{4,6},{5,7},{6,4},{7,5},{8,10},{9,11},{10,... | collective-permute-start | bytes 442376 | tf_op jit(solution)/shard_map/ppermute | solution.py:422
  224.9 16.0 %collective-permute-start.50 = (bf16[4,24,1152]{2,1,0:T(8,128)(2,1)S(1)}, bf16[4,24,1152]{2,1,0:T(8,128)(2,1)S(1)}, u32[]{:S(2)}, u32[]{:S(2)}) collective-permute-start(bf16[4,24,1152]{2,1,0:T(8,128)(2,1)S(1)} %dynamic-slice_bitcast_fusion.24), channel_id=1, source_target_pairs={{0,8},{4,12},{8,0},{12,4},{16,24},{20,28},{24,16},{28,20},{1,9},{5... | collective-permute-start | bytes 663560 | tf_op jit(solution)/shard_map/ppermute | solution.py:414
  226.2 15.5 %collective-permute-start.49 = (bf16[4,24,1152]{2,1,0:T(8,128)(2,1)S(1)}, bf16[4,24,1152]{2,1,0:T(8,128)(2,1)S(1)}, u32[]{:S(2)}, u32[]{:S(2)}) collective-permute-start(bf16[4,24,1152]{2,1,0:T(8,128)(2,1)S(1)} %dynamic-slice_bitcast_fusion.25), channel_id=1, source_target_pairs={{0,16},{4,20},{8,24},{12,28},{16,0},{20,4},{24,8},{28,12},{1,17},{... | collective-permute-start | bytes 663560 | tf_op jit(solution)/shard_map/ppermute | solution.py:418
  228.6 10.6 %collective-permute-start.46 = (bf16[4,2,24,512]{3,2,1,0:T(8,128)(2,1)S(1)}, bf16[4,2,24,512]{3,2,1,0:T(8,128)(2,1)S(1)}, u32[]{:S(2)}, u32[]{:S(2)}) collective-permute-start(bf16[4,2,24,512]{3,2,1,0:T(8,128)(2,1)S(1)} %pad_maximum_fusion.9), channel_id=1, source_target_pairs={{0,16},{4,20},{8,24},{12,28},{16,0},{20,4},{24,8},{28,12},{1,17},{... | collective-permute-start | bytes 589832 | tf_op jit(solution)/shard_map/ppermute | solution.py:418
  229.4 10.4 %collective-permute-start.44 = (bf16[96,768]{1,0:T(8,128)(2,1)S(1)}, bf16[96,768]{1,0:T(8,128)(2,1)S(1)}, u32[]{:S(2)}, u32[]{:S(2)}) collective-permute-start(bf16[96,768]{1,0:T(8,128)(2,1)S(1)} %add_convert_fusion.19), channel_id=1, source_target_pairs={{0,8},{4,12},{8,0},{12,4},{16,24},{20,28},{24,16},{28,20},{1,9},{5... | collective-permute-start | bytes 442376 | tf_op jit(solution)/shard_map/ppermute | solution.py:414
  239.2 9.5 %collective-permute-start.53 = (bf16[48,1536]{1,0:T(8,128)(2,1)S(1)}, bf16[48,1536]{1,0:T(8,128)(2,1)S(1)}, u32[]{:S(2)}, u32[]{:S(2)}) collective-permute-start(bf16[48,1536]{1,0:T(8,128)(2,1)S(1)} %get-tuple-element.358), channel_id=1, source_target_pairs={{0,2},{1,3},{2,0},{3,1},{4,6},{5,7},{6,4},{7,5},{8,10},{9,11},{10,... | collective-permute-start | bytes 442376 | tf_op jit(solution)/shard_map/ppermute | solution.py:422
  239.7 10.1 %collective-permute-start.51 = (bf16[4,24,512]{2,1,0:T(8,128)(2,1)S(1)}, bf16[4,24,512]{2,1,0:T(8,128)(2,1)S(1)}, u32[]{:S(2)}, u32[]{:S(2)}) collective-permute-start(bf16[4,24,512]{2,1,0:T(8,128)(2,1)S(1)} %get-tuple-element.378), channel_id=1, source_target_pairs={{0,16},{4,20},{8,24},{12,28},{16,0},{20,4},{24,8},{28,12},{1,17},{... | collective-permute-start | bytes 294920 | tf_op jit(solution)/shard_map/ppermute | solution.py:418
  243.1 18.9 %collective-permute-start.48 = (bf16[256,768]{1,0:T(8,128)(2,1)S(1)}, bf16[256,768]{1,0:T(8,128)(2,1)S(1)}, u32[]{:S(2)}, u32[]{:S(2)}) collective-permute-start(bf16[256,768]{1,0:T(8,128)(2,1)S(1)} %get-tuple-element.332), channel_id=1, source_target_pairs={{0,0},{1,1},{4,2},{5,3},{2,4},{3,5},{6,6},{7,7},{8,8},{9,9},{12,10... | collective-permute-start | bytes 1179656 | tf_op jit(solution)/shard_map/ppermute | solution.py:460
  250.0 11.9 %collective-permute-start.54 = (bf16[2,48,1664]{2,1,0:T(8,128)(2,1)S(1)}, bf16[2,48,1664]{2,1,0:T(8,128)(2,1)S(1)}, u32[]{:S(2)}, u32[]{:S(2)}) collective-permute-start(bf16[2,48,1664]{2,1,0:T(8,128)(2,1)S(1)} %get-tuple-element.333), channel_id=1, source_target_pairs={{0,1},{1,0},{2,3},{3,2},{4,5},{5,4},{6,7},{7,6},{8,9},{9,8},{10,11... | collective-permute-start | bytes 958472 | tf_op jit(solution)/shard_map/ppermute | solution.py:422
  250.2 14.9 %collective-permute-start.61 = (bf16[384,768]{1,0:T(8,128)(2,1)S(1)}, bf16[384,768]{1,0:T(8,128)(2,1)S(1)}, u32[]{:S(2)}, u32[]{:S(2)}) collective-permute-start(bf16[384,768]{1,0:T(8,128)(2,1)S(1)} %constant_dynamic-update-slice_fusion.20.mine_ref), channel_id=1, source_target_pairs={{0,4},{4,0},{8,12},{12,8},{16,20},{20,16},{24,28},{28,24},{1,5},{5... | collective-permute-start | bytes 1769480 | tf_op jit(solution)/shard_map/ppermute | solution.py:410
  263.4 10.0 %collective-permute-start.58 = (bf16[48,1664]{1,0:T(8,128)(2,1)S(1)}, bf16[48,1664]{1,0:T(8,128)(2,1)S(1)}, u32[]{:S(2)}, u32[]{:S(2)}) collective-permute-start(bf16[48,1664]{1,0:T(8,128)(2,1)S(1)} %get-tuple-element.356), channel_id=1, source_target_pairs={{0,2},{1,3},{2,0},{3,1},{4,6},{5,7},{6,4},{7,5},{8,10},{9,11},{10,... | collective-permute-start | bytes 479240 | tf_op jit(solution)/shard_map/ppermute | solution.py:422
  274.2 9.2 %collective-permute-start.63 = (bf16[48,1664]{1,0:T(8,128)(2,1)S(1)}, bf16[48,1664]{1,0:T(8,128)(2,1)S(1)}, u32[]{:S(2)}, u32[]{:S(2)}) collective-permute-start(bf16[48,1664]{1,0:T(8,128)(2,1)S(1)} %add_convert_fusion.17), channel_id=1, source_target_pairs={{0,16},{4,20},{8,24},{12,28},{16,0},{20,4},{24,8},{28,12},{1,17},{... | collective-permute-start | bytes 479240 | tf_op jit(solution)/shard_map/ppermute | solution.py:418
  284.3 12.3 %collective-permute-start.57 = (bf16[256,768]{1,0:T(8,128)(2,1)S(1)}, bf16[256,768]{1,0:T(8,128)(2,1)S(1)}, u32[]{:S(2)}, u32[]{:S(2)}) collective-permute-start(bf16[256,768]{1,0:T(8,128)(2,1)S(1)} %get-tuple-element.293), channel_id=1, source_target_pairs={{1,0},{0,1},{5,2},{4,3},{3,4},{2,5},{7,6},{6,7},{9,8},{8,9},{13,10... | collective-permute-start | bytes 1179656 | tf_op jit(solution)/shard_map/ppermute | solution.py:460
  (54 other events, 415.1 us)
where the time goes:
time: 304 us; the launch traced here: 298 us
  starting transfers between devices  91.9 us (30%)
  Pallas kernels  89.1 us (29%)
  waiting for transfers between devices  68.9 us (23%)
  matrix products  19.7 us (6%)
  local copies, waits for them, and re-layouts  17.9 us (6%)
  other arithmetic  7.82 us (3%)
    pallas_call x3, Pallas kernels, attend_chip_backward(): pl.pallas_call(attend_bwd_kernel, grid=(1,), out_shape=[jax.ShapeDtypeStr...  22.5 us
    ppermute x14, starting transfers between devices, swap_z(): return lax.ppermute(value, 'shard', [(i, i ^ flip) for i in range(4)])  21.7 us
    pallas_call x14, Pallas kernels, move_blocks(): pl.pallas_call(functools.partial(move_kernel, len(sources), moves), out_s...  20.8 us
    ppermute x14, waiting for transfers between devices, swap_z(): return lax.ppermute(value, 'shard', [(i, i ^ flip) for i in range(4)])  16.5 us
    ppermute x14, starting transfers between devices, swap_x(): return lax.ppermute(value, 'grp', [(i, i ^ 2) for i in range(8)])  14.9 us
    unnamed x89, local copies, waits for them, and re-layouts  14.8 us
    ppermute x2, waiting for transfers between devices, send_first(): return lax.ppermute(block, ('grp', 'shard'), sequence_perm(0))  14.6 us
    ppermute x2, starting transfers between devices, send_first(): return lax.ppermute(block, ('grp', 'shard'), sequence_perm(0))  13.8 us
  transfers between devices with their start and end apart: 66, of which 19 were waited for; matrix products, arithmetic and copies ran while one was open for 7% of the time, Pallas kernels for 24%

commit v1 on v0

--- a/solution.py
+++ b/solution.py
@@ -1336,7 +1336,8 @@
         where, after(up_state, grad_down), False, up_layout, slab_part, [(slab, 2 * units)]
     )
     attn_state, sent = direct_spread(after(attn_state, grad_up))
-    attn_state = spread_core(attn_state)
+    grad_tokens = join_rows(*after((back_first, back_second), attn_state[1]), parity)
+    attn_state = spread_core(after(attn_state, grad_tokens))
     span = half - PAIR
     attn_layout = lambda half_at: (
         [(idx * span, span, 0, slab_row, idx * width + half_at * half) for idx in range(3)]
@@ -1349,7 +1350,6 @@
     grad_qkv, grad_out, *vec_grads = finish_grad(
         where, after(attn_state, grad_up), True, attn_layout, slab_part, [(slab, 3 * width), (slab, width)], 4 * half
     )
-    grad_tokens = join_rows(*after((back_first, back_second), grad_qkv), parity)
     vec_of = lambda idx: vec_grads[idx]
     return (
         layer_out,

time: 304 us -> 297 us (0.977)
  the two profiles are of different devices: /device:TPU:1 before, /device:TPU:25 now
where the time goes in v1:
time: 297 us; the launch traced here: 291 us
  Pallas kernels  89 us (30%)
  starting transfers between devices  83.8 us (28%)
  waiting for transfers between devices  70 us (24%)
  matrix products  19.7 us (7%)
  local copies, waits for them, and re-layouts  18.3 us (6%)
  other arithmetic  7.77 us (3%)
    ppermute x12, starting transfers between devices, swap_core(): return lax.ppermute(value, 'grp', [(i, i ^ 1) for i in range(8)])  27.8 us
    pallas_call x3, Pallas kernels, attend_chip_backward(): pl.pallas_call(attend_bwd_kernel, grid=(1,), out_shape=[jax.ShapeDtypeStr...  22.5 us
    ppermute x14, waiting for transfers between devices, swap_z(): return lax.ppermute(value, 'shard', [(i, i ^ flip) for i in range(4)])  21 us
    pallas_call x14, Pallas kernels, move_blocks(): pl.pallas_call(functools.partial(move_kernel, len(sources), moves), out_s...  20.8 us
    ppermute x14, starting transfers between devices, swap_z(): return lax.ppermute(value, 'shard', [(i, i ^ flip) for i in range(4)])  19.8 us
    ppermute x4, waiting for transfers between devices, swap_xy(): return lax.ppermute(value, 'grp', [(i, i ^ 6) for i in range(8)])  19.2 us
    unnamed x92, local copies, waits for them, and re-layouts  15.1 us
    pallas_call x3, Pallas kernels, attend_chip_forward(): pl.pallas_call(attend_fwd_kernel, grid=(1,), out_shape=[jax.ShapeDtypeStr...  13.1 us
  transfers between devices with their start and end apart: 66, of which 20 were waited for; matrix products, arithmetic and copies ran while one was open for 8% of the time, Pallas kernels for 24%

profile of v1, /device:TPU:25, one launch (start us, length us, event | category | flops | bytes accessed | tf_op | source)
XLA Modules:
  0.0 291.4 jit_solution(18029853329217554798)
XLA Ops:
  1.3 2.3 shard_map.271.own_ref
  3.8 3.4 %collective-permute-start.4 = (bf16[64,1152]{1,0:T(8,128)(2,1)}, bf16[64,1152]{1,0:T(8,128)(2,1)S(1)}, u32[]{:S(2)}, u32[]{:S(2)}) collective-permute-start(bf16[64,1152]{1,0:T(8,128)(2,1)} %shard_map.271.own_ref), channel_id=1, source_target_pairs={{0,3},{1,2},{2,1},{3,0},{4,7},{5,6},{6,5},{7,4},{8,11},{9,10},{10,... | collective-permute-start | bytes 442376 | tf_op jit(solution)/shard_map/ppermute | solution.py:422
  12.6 3.6 %shard_map.272 = (bf16[256,768]{1,0:T(8,128)(2,1)}, bf16[256,768]{1,0:T(8,128)(2,1)}, bf16[256,768]{1,0:T(8,128)(2,1)}, bf16[256,768]{1,0:T(8,128)(2,1)}, bf16[4...) custom-call(s32[4]{0:T(128)} %pad_add_fusion.where_ref, bf16[512,768]{1,0:T(8,128)(2,1)} %bitcast.196, ...), custom_call_target="tpu_custom_call" | custom-call | flops 1024 | bytes 1024 | tf_op jit(solution)/shard_map/pallas_call | solution.py:498
  21.8 3.1 %collective-permute-start.2 = (bf16[256,768]{1,0:T(8,128)(2,1)}, bf16[256,768]{1,0:T(8,128)(2,1)S(1)}, u32[]{:S(2)}, u32[]{:S(2)}) collective-permute-start(bf16[256,768]{1,0:T(8,128)(2,1)} %get-tuple-element.172), channel_id=1, source_target_pairs={{0,1},{1,0},{2,5},{3,4},{4,3},{5,2},{6,7},{7,6},{8,9},{9,8},{10,13... | collective-permute-start | bytes 1179656 | tf_op jit(solution)/shard_map/ppermute | solution.py:452
  25.8 8.0 %collective-permute-done.2.refs_1_ = bf16[256,768]{1,0:T(8,128)(2,1)S(1)} collective-permute-done((bf16[256,768]{1,0:T(8,128)(2,1)}, bf16[256,768]{1,0:T(8,128)(2,1)S(1)}, u32[]{:S(2)}, u32[]{:S(2)}) %collective-permute-start.2) | collective-permute-done | bytes 393248 | tf_op jit(solution)/shard_map/ppermute | solution.py:452
  34.6 2.5 collective-permute-done.8.refs_4_
  38.8 7.2 %collective-permute-start.9 = (bf16[512,768]{1,0:T(8,128)(2,1)S(1)}, bf16[512,768]{1,0:T(8,128)(2,1)}, u32[]{:S(2)}, u32[]{:S(2)}) collective-permute-start(bf16[512,768]{1,0:T(8,128)(2,1)S(1)} %shard_map.275.refs_0_), channel_id=1, source_target_pairs={{0,4},{4,0},{8,12},{12,8},{16,20},{20,16},{24,28},{28,24},{1,5},{5... | collective-permute-start | bytes 2359304 | tf_op jit(solution)/shard_map/ppermute | solution.py:410
  46.0 3.3 %collective-permute-start.10 = (bf16[48,1920]{1,0:T(8,128)(2,1)}, bf16[48,1920]{1,0:T(8,128)(2,1)S(1)}, u32[]{:S(2)}, u32[]{:S(2)}) collective-permute-start(bf16[48,1920]{1,0:T(8,128)(2,1)} %get-tuple-element.184), channel_id=1, source_target_pairs={{0,1},{1,0},{2,3},{3,2},{4,5},{5,4},{6,7},{7,6},{8,9},{9,8},{10,11... | collective-permute-start | bytes 552968 | tf_op jit(solution)/shard_map/ppermute | solution.py:422
  49.3 2.2 collective-permute-start.12
  53.5 2.5 shard_map.277
  57.8 2.2 add_convert_fusion.q_ref.k_ref.v_ref
  60.0 4.4 %shard_map.278 = (bf16[1024,128]{1,0:T(8,128)(2,1)S(1)}, f32[1,2,1024]{2,1,0:T(2,128)S(1)}) custom-call(bf16[1024,1152]{1,0:T(8,128)(2,1)S(1)} %add_convert_fusion.q_ref.k_ref.v_ref, bf16[1024,1152]{1,0:T(8,128)(2,1)S(1)} %add_convert_fusion.q_ref.k_ref.v_ref, bf16[1024,1152]{1,0:T(8,128)(2,1)S(1)} %add_convert_fusion.q_ref.k_ref.v_ref, ...), custom_call_target="tpu_custom_call" | custom-call | flops 1024 | bytes 1024 | tf_op jit(solution)/shard_map/pallas_call | solution.py:947
  65.8 3.5 %collective-permute-start.13 = (bf16[96,768]{1,0:T(8,128)(2,1)S(1)}, bf16[96,768]{1,0:T(8,128)(2,1)S(1)}, u32[]{:S(2)}, u32[]{:S(2)}) collective-permute-start(bf16[96,768]{1,0:T(8,128)(2,1)S(1)} %copy-done.29), channel_id=1, source_target_pairs={{0,2},{1,3},{2,0},{3,1},{4,6},{5,7},{6,4},{7,5},{8,10},{9,11},{10,... | collective-permute-start | bytes 442376 | tf_op jit(solution)/shard_map/ppermute | solution.py:422
  69.2 4.3 %shard_map.280 = (bf16[1024,128]{1,0:T(8,128)(2,1)S(1)}, f32[1,2,1024]{2,1,0:T(2,128)S(1)}) custom-call(bf16[1024,1152]{1,0:T(8,128)(2,1)S(1)} %add_convert_fusion.q_ref.k_ref.v_ref, bf16[1024,1152]{1,0:T(8,128)(2,1)S(1)} %add_convert_fusion.q_ref.k_ref.v_ref, bf16[1024,1152]{1,0:T(8,128)(2,1)S(1)} %add_convert_fusion.q_ref.k_ref.v_ref, ...), custom_call_target="tpu_custom_call" | custom-call | flops 1024 | bytes 1024 | tf_op jit(solution)/shard_map/pallas_call | solution.py:947
  74.5 2.6 collective-permute-start.14
  82.4 2.2 collective-permute-start.16
  84.7 4.4 %shard_map.282 = (bf16[1024,128]{1,0:T(8,128)(2,1)S(1)}, f32[1,2,1024]{2,1,0:T(2,128)S(1)}) custom-call(bf16[1024,1152]{1,0:T(8,128)(2,1)S(1)} %add_convert_fusion.q_ref.k_ref.v_ref, bf16[1024,1152]{1,0:T(8,128)(2,1)S(1)} %add_convert_fusion.q_ref.k_ref.v_ref, bf16[1024,1152]{1,0:T(8,128)(2,1)S(1)} %add_convert_fusion.q_ref.k_ref.v_ref, ...), custom_call_target="tpu_custom_call" | custom-call | flops 1024 | bytes 1024 | tf_op jit(solution)/shard_map/pallas_call | solution.py:947
  90.3 2.5 collective-permute-done.16.refs_1_
  93.8 8.9 %collective-permute-done.19.refs_5_ = bf16[144,1920]{1,0:T(8,128)(2,1)S(1)} collective-permute-done((bf16[144,1920]{1,0:T(8,128)(2,1)S(1)}, bf16[144,1920]{1,0:T(8,128)(2,1)S(1)}, u32[]{:S(2)}, u32[]{:S(2)}) %collective-permute-start.19) | collective-permute-done | bytes 552992 | tf_op jit(solution)/shard_map/ppermute | solution.py:426
  104.2 2.6 collective-permute-start.20
  112.4 2.2 collective-permute-done.22.refs_1_
  118.4 7.0 %shard_map.287 = (bf16[1024,768]{1,0:T(8,128)(2,1)S(1)}, f32[1024,768]{1,0:T(8,128)S(1)}, f32[1024,128]{1,0:T(8,128)S(1)}, bf16[1024,1536]{1,0:T(8,128)(2,1)S(1)}, bf16[1024,1536]{1,0:T(8,128)(2,1)S(1)}) custom-call(bf16[1024,768]{1,0:T(8,128)(2,1)S(1)} %convolution_convert_fusion.2.part_ref, bf16[1024,768]{1,0:T(8,128)(2,1)S(1)} %collective-permute-done.21.got_ref, ...), custom_call_target="tpu_custom_call" | custom-call | flops 1024 | bytes 1024 | tf_op jit(solution)/shard_map/pallas_call | solution.py:698
  128.3 4.7 %collective-permute-done.26.refs_4_ = bf16[288,768]{1,0:T(8,128)(2,1)S(1)} collective-permute-done((bf16[288,768]{1,0:T(8,128)(2,1)S(1)}, bf16[288,768]{1,0:T(8,128)(2,1)S(1)}, u32[]{:S(2)}, u32[]{:S(2)}) %collective-permute-start.26) | collective-permute-done | bytes 442400 | tf_op jit(solution)/shard_map/ppermute | solution.py:426
  133.0 3.1 %shard_map.290.down_ref = bf16[1536,768]{1,0:T(8,128)(2,1)S(1)} custom-call(s32[4]{0:T(128)S(1)} %copy-done.28, bf16[768,768]{1,0:T(8,128)(2,1)S(1)} %copy-done.12, bf16[288,768]{1,0:T(8,128)(2,1)S(1)} %shard_map.283.refs_1_, bf16[288,768]{1,0:T(8,128)(2,1)S(1)} %collective-permute-done.24.refs_2_, bf16[288,768]{1,0:T(8,128)(2,1)S(1)} %collective-permute-done.25.refs_3_, ...), custom_call_target="tpu_custom_call" | custom-call | flops 1024 | bytes 1024 | tf_op jit(solution)/shard_map/pallas_call | solution.py:498
  136.1 3.7 %convolution_convert_fusion.3.part_ref = bf16[1024,768]{1,0:T(8,128)(2,1)} fusion(bf16[1024,1536]{1,0:T(8,128)(2,1)S(1)} %get-tuple-element.206, bf16[1536,768]{1,0:T(8,128)(2,1)S(1)} %shard_map.290.down_ref), kind=kOutput, calls=%fused_computation.5 | convolution fusion | flops 2416705536 | bytes 7077888 | tf_op jit(solution)/shard_map/dot_general | solution.py:430
  140.8 3.4 %collective-permute-done.27.got_ref = bf16[1024,768]{1,0:T(8,128)(2,1)} collective-permute-done((bf16[1024,768]{1,0:T(8,128)(2,1)}, bf16[1024,768]{1,0:T(8,128)(2,1)}, u32[]{:S(2)}, u32[]{:S(2)}) %collective-permute-start.27) | collective-permute-done | bytes 1572896 | tf_op jit(solution)/shard_map/ppermute | solution.py:410
  147.5 5.4 %shard_map.291 = (bf16[256,768]{1,0:T(8,128)(2,1)S(1)}, bf16[256,768]{1,0:T(8,128)(2,1)S(1)}, f32[1024,768]{1,0:T(8,128)S(1)}, bf16[1024,768]{1,0:T(8,128)(2,1)S(1)}, f32[8,768]{1,0:T(8,128)S(1)}) custom-call(bf16[1024,768]{1,0:T(8,128)(2,1)} %convolution_convert_fusion.3.part_ref, bf16[1024,768]{1,0:T(8,128)(2,1)} %collective-permute-done.27.got_ref, ...), custom_call_target="tpu_custom_call" | custom-call | flops 1024 | bytes 1024 | tf_op jit(solution)/shard_map/pallas_call | solution.py:757
  152.9 2.9 %convolution_convert_fusion.1 = bf16[1536,768]{1,0:T(8,128)(2,1)S(1)} fusion(bf16[1024,1536]{1,0:T(8,128)(2,1)S(1)} %copy-done.31, bf16[1024,768]{1,0:T(8,128)(2,1)S(1)} %get-tuple-element.216.dffn_ref), kind=kOutput, calls=%fused_computation.3 | convolution fusion | flops 2417098752 | bytes 7077888 | tf_op jit(solution)/shard_map/dot_general | solution.py:38
  159.2 6.7 %shard_map.292 = (bf16[1024,1536]{1,0:T(8,128)(2,1)S(1)}, bf16[1024,768]{1,0:T(8,128)(2,1)S(1)}, f32[1,1536]{1,0:T(1,128)S(1)}) custom-call(bf16[1024,768]{1,0:T(8,128)(2,1)S(1)} %get-tuple-element.216.dffn_ref, bf16[1536,768]{1,0:T(8,128)(2,1)S(1)} %copy-done.6, bf16[1024,1536]{1,0:T(8,128)(2,1)S(1)} %copy-done.15, bf16[768,1536]{1,0:T(8,128)(2,1)S(1)} %copy-done.4), custom_call_target="tpu_custom_call" | custom-call | flops 1024 | bytes 1024 | tf_op jit(solution)/shard_map/pallas_call | solution.py:799
  165.9 4.8 %collective-permute-start.29 = (bf16[1024,768]{1,0:T(8,128)(2,1)S(1)}, bf16[1024,768]{1,0:T(8,128)(2,1)S(1)}, u32[]{:S(2)}, u32[]{:S(2)}) collective-permute-start(bf16[1024,768]{1,0:T(8,128)(2,1)S(1)} %get-tuple-element.218.part_ref), channel_id=1, source_target_pairs={{0,4},{4,0},{8,12},{12,8},{16,20},{20,16},{24,28},{28,24},{1,5},{5... | collective-permute-start | bytes 4718600 | tf_op jit(solution)/shard_map/ppermute | solution.py:410
  170.7 3.0 %convolution_convert_fusion = bf16[768,1536]{1,0:T(8,128)(2,1)S(1)} fusion(bf16[1024,768]{1,0:T(8,128)(2,1)S(1)} %copy-done.33, bf16[1024,1536]{1,0:T(8,128)(2,1)S(1)} %get-tuple-element.221), kind=kOutput, calls=%fused_computation.2 | convolution fusion | flops 2417098752 | bytes 7077888 | tf_op jit(solution)/shard_map/dot_general | solution.py:38
  175.9 3.1 %shard_map.293 = (f32[512,768]{1,0:T(8,128)S(1)}, bf16[1024,768]{1,0:T(8,128)(2,1)S(1)}, bf16[1024,384]{1,0:T(8,128)(2,1)S(1)}, f32[8,768]{1,0:T(8,128)S(1)}) custom-call(s32[4]{0:T(128)S(1)} %copy-done.28, f32[1024,768]{1,0:T(8,128)S(1)} %get-tuple-element.215.dr_ref, bf16[1024,768]{1,0:T(8,128)(2,1)S(1)} %get-tuple-element.218.part_ref, ...), custom_call_target="tpu_custom_call" | custom-call | flops 1024 | bytes 1024 | tf_op jit(solution)/shard_map/pallas_call | solution.py:842
  183.6 7.4 %shard_map.294 = (bf16[1024,128]{1,0:T(8,128)(2,1)S(1)}, bf16[1024,128]{1,0:T(8,128)(2,1)S(1)}, bf16[1024,128]{1,0:T(8,128)(2,1)S(1)}) custom-call(bf16[1024,1152]{1,0:T(8,128)(2,1)S(1)} %add_convert_fusion.q_ref.k_ref.v_ref, bf16[1024,1152]{1,0:T(8,128)(2,1)S(1)} %add_convert_fusion.q_ref.k_ref.v_ref, ...), custom_call_target="tpu_custom_call" | custom-call | flops 1024 | bytes 1024 | tf_op jit(solution)/shard_map/pallas_call | solution.py:966
  192.2 3.3 %collective-permute-done.35 = bf16[4,48,768]{2,1,0:T(8,128)(2,1)S(1)} collective-permute-done((bf16[4,48,768]{2,1,0:T(8,128)(2,1)S(1)}, bf16[4,48,768]{2,1,0:T(8,128)(2,1)S(1)}, u32[]{:S(2)}, u32[]{:S(2)}) %collective-permute-start.35) | collective-permute-done | bytes 294944 | tf_op jit(solution)/shard_map/ppermute | solution.py:418
  197.8 7.7 %shard_map.295 = (bf16[1024,128]{1,0:T(8,128)(2,1)S(1)}, bf16[1024,128]{1,0:T(8,128)(2,1)S(1)}, bf16[1024,128]{1,0:T(8,128)(2,1)S(1)}) custom-call(bf16[1024,1152]{1,0:T(8,128)(2,1)S(1)} %add_convert_fusion.q_ref.k_ref.v_ref, bf16[1024,1152]{1,0:T(8,128)(2,1)S(1)} %add_convert_fusion.q_ref.k_ref.v_ref, ...), custom_call_target="tpu_custom_call" | custom-call | flops 1024 | bytes 1024 | tf_op jit(solution)/shard_map/pallas_call | solution.py:966
  212.3 7.4 %shard_map.296 = (bf16[1024,128]{1,0:T(8,128)(2,1)S(1)}, bf16[1024,128]{1,0:T(8,128)(2,1)S(1)}, bf16[1024,128]{1,0:T(8,128)(2,1)S(1)}) custom-call(bf16[1024,1152]{1,0:T(8,128)(2,1)S(1)} %add_convert_fusion.q_ref.k_ref.v_ref, bf16[1024,1152]{1,0:T(8,128)(2,1)S(1)} %add_convert_fusion.q_ref.k_ref.v_ref, ...), custom_call_target="tpu_custom_call" | custom-call | flops 1024 | bytes 1024 | tf_op jit(solution)/shard_map/pallas_call | solution.py:966
  231.6 4.3 %collective-permute-start.47 = (bf16[512,768]{1,0:T(8,128)(2,1)S(1)}, bf16[512,768]{1,0:T(8,128)(2,1)S(1)}, u32[]{:S(2)}, u32[]{:S(2)}) collective-permute-start(bf16[512,768]{1,0:T(8,128)(2,1)S(1)} %convolution_convert_fusion.6), channel_id=1, source_target_pairs={{0,4},{4,0},{8,12},{12,8},{16,20},{20,16},{24,28},{28,24},{1,5},{5... | collective-permute-start | bytes 2359304 | tf_op jit(solution)/shard_map/ppermute | solution.py:410
  235.9 2.7 collective-permute-start.53
  242.2 3.7 %collective-permute-done.53 = bf16[48,1536]{1,0:T(8,128)(2,1)S(1)} collective-permute-done((bf16[48,1536]{1,0:T(8,128)(2,1)S(1)}, bf16[48,1536]{1,0:T(8,128)(2,1)S(1)}, u32[]{:S(2)}, u32[]{:S(2)}) %collective-permute-start.53) | collective-permute-done | bytes 147488 | tf_op jit(solution)/shard_map/ppermute | solution.py:422
  247.2 2.1 collective-permute-done.56
  252.6 6.7 %collective-permute-done.54 = bf16[2,48,1664]{2,1,0:T(8,128)(2,1)S(1)} collective-permute-done((bf16[2,48,1664]{2,1,0:T(8,128)(2,1)S(1)}, bf16[2,48,1664]{2,1,0:T(8,128)(2,1)S(1)}, u32[]{:S(2)}, u32[]{:S(2)}) %collective-permute-start.54) | collective-permute-done | bytes 319520 | tf_op jit(solution)/shard_map/ppermute | solution.py:422
  259.9 2.1 collective-permute-start.60
  262.9 2.2 shard_map.298
  265.1 2.1 shard_map.299
  267.2 8.9 %collective-permute-done.58 = bf16[48,1664]{1,0:T(8,128)(2,1)S(1)} collective-permute-done((bf16[48,1664]{1,0:T(8,128)(2,1)S(1)}, bf16[48,1664]{1,0:T(8,128)(2,1)S(1)}, u32[]{:S(2)}, u32[]{:S(2)}) %collective-permute-start.58) | collective-permute-done | bytes 159776 | tf_op jit(solution)/shard_map/ppermute | solution.py:422
  278.9 2.4 collective-permute-done.62
  282.3 3.0 %collective-permute-done.64 = bf16[48,1664]{1,0:T(8,128)(2,1)S(1)} collective-permute-done((bf16[48,1664]{1,0:T(8,128)(2,1)S(1)}, bf16[48,1664]{1,0:T(8,128)(2,1)S(1)}, u32[]{:S(2)}, u32[]{:S(2)}) %collective-permute-start.64) | collective-permute-done | bytes 159776 | tf_op jit(solution)/shard_map/ppermute | solution.py:426
  288.7 2.2 shard_map.300
  (315 shorter events, 94.9 us)
Async XLA Ops:
  3.6 9.0 %collective-permute-start = (bf16[64,1152]{1,0:T(8,128)(2,1)}, bf16[64,1152]{1,0:T(8,128)(2,1)S(1)}, u32[]{:S(2)}, u32[]{:S(2)}) collective-permute-start(bf16[64,1152]{1,0:T(8,128)(2,1)} %shard_map.271.own_ref), channel_id=1, source_target_pairs={{0,1},{1,0},{2,3},{3,2},{4,5},{5,4},{6,7},{7,6},{8,9},{9,8},{10,11... | collective-permute-start | bytes 442376 | tf_op jit(solution)/shard_map/ppermute | solution.py:422
  3.8 12.4 %collective-permute-start.3 = (bf16[64,1152]{1,0:T(8,128)(2,1)}, bf16[64,1152]{1,0:T(8,128)(2,1)S(1)}, u32[]{:S(2)}, u32[]{:S(2)}) collective-permute-start(bf16[64,1152]{1,0:T(8,128)(2,1)} %shard_map.271.own_ref), channel_id=1, source_target_pairs={{0,2},{1,3},{2,0},{3,1},{4,6},{5,7},{6,4},{7,5},{8,10},{9,11},{10,... | collective-permute-start | bytes 442376 | tf_op jit(solution)/shard_map/ppermute | solution.py:422
  3.8 12.4 %collective-permute-start.4 = (bf16[64,1152]{1,0:T(8,128)(2,1)}, bf16[64,1152]{1,0:T(8,128)(2,1)S(1)}, u32[]{:S(2)}, u32[]{:S(2)}) collective-permute-start(bf16[64,1152]{1,0:T(8,128)(2,1)} %shard_map.271.own_ref), channel_id=1, source_target_pairs={{0,3},{1,2},{2,1},{3,0},{4,7},{5,6},{6,5},{7,4},{8,11},{9,10},{10,... | collective-permute-start | bytes 442376 | tf_op jit(solution)/shard_map/ppermute | solution.py:422
  17.4 16.4 %collective-permute-start.6 = (bf16[192,1152]{1,0:T(8,128)(2,1)S(1)}, bf16[192,1152]{1,0:T(8,128)(2,1)S(1)}, u32[]{:S(2)}, u32[]{:S(2)}) collective-permute-start(bf16[192,1152]{1,0:T(8,128)(2,1)S(1)} %shard_map.273.came_ref.refs_1_), channel_id=1, source_target_pairs={{0,8},{4,12},{8,0},{12,4},{16,24},{20,28},{24,16},{28,20},{1,9},{5... | collective-permute-start | bytes 1327112 | tf_op jit(solution)/shard_map/ppermute | solution.py:414
  18.7 15.1 %collective-permute-start.7 = (bf16[192,1152]{1,0:T(8,128)(2,1)S(1)}, bf16[192,1152]{1,0:T(8,128)(2,1)S(1)}, u32[]{:S(2)}, u32[]{:S(2)}) collective-permute-start(bf16[192,1152]{1,0:T(8,128)(2,1)S(1)} %shard_map.273.came_ref.refs_1_), channel_id=1, source_target_pairs={{0,16},{4,20},{8,24},{12,28},{16,0},{20,4},{24,8},{28,12},{1,17},{... | collective-permute-start | bytes 1327112 | tf_op jit(solution)/shard_map/ppermute | solution.py:418
  19.9 17.2 %collective-permute-start.8 = (bf16[192,1152]{1,0:T(8,128)(2,1)S(1)}, bf16[192,1152]{1,0:T(8,128)(2,1)S(1)}, u32[]{:S(2)}, u32[]{:S(2)}) collective-permute-start(bf16[192,1152]{1,0:T(8,128)(2,1)S(1)} %shard_map.273.came_ref.refs_1_), channel_id=1, source_target_pairs={{0,24},{4,28},{8,16},{12,20},{16,8},{20,12},{24,0},{28,4},{1,25},{... | collective-permute-start | bytes 1327112 | tf_op jit(solution)/shard_map/ppermute | solution.py:426
  21.8 12.0 %collective-permute-start.2 = (bf16[256,768]{1,0:T(8,128)(2,1)}, bf16[256,768]{1,0:T(8,128)(2,1)S(1)}, u32[]{:S(2)}, u32[]{:S(2)}) collective-permute-start(bf16[256,768]{1,0:T(8,128)(2,1)} %get-tuple-element.172), channel_id=1, source_target_pairs={{0,1},{1,0},{2,5},{3,4},{4,3},{5,2},{6,7},{7,6},{8,9},{9,8},{10,13... | collective-permute-start | bytes 1179656 | tf_op jit(solution)/shard_map/ppermute | solution.py:452
  38.8 17.2 %collective-permute-start.9 = (bf16[512,768]{1,0:T(8,128)(2,1)S(1)}, bf16[512,768]{1,0:T(8,128)(2,1)}, u32[]{:S(2)}, u32[]{:S(2)}) collective-permute-start(bf16[512,768]{1,0:T(8,128)(2,1)S(1)} %shard_map.275.refs_0_), channel_id=1, source_target_pairs={{0,4},{4,0},{8,12},{12,8},{16,20},{20,16},{24,28},{28,24},{1,5},{5... | collective-permute-start | bytes 2359304 | tf_op jit(solution)/shard_map/ppermute | solution.py:410
  46.0 18.4 %collective-permute-start.10 = (bf16[48,1920]{1,0:T(8,128)(2,1)}, bf16[48,1920]{1,0:T(8,128)(2,1)S(1)}, u32[]{:S(2)}, u32[]{:S(2)}) collective-permute-start(bf16[48,1920]{1,0:T(8,128)(2,1)} %get-tuple-element.184), channel_id=1, source_target_pairs={{0,1},{1,0},{2,3},{3,2},{4,5},{5,4},{6,7},{7,6},{8,9},{9,8},{10,11... | collective-permute-start | bytes 552968 | tf_op jit(solution)/shard_map/ppermute | solution.py:422
  49.3 15.1 %collective-permute-start.11 = (bf16[48,1920]{1,0:T(8,128)(2,1)}, bf16[48,1920]{1,0:T(8,128)(2,1)S(1)}, u32[]{:S(2)}, u32[]{:S(2)}) collective-permute-start(bf16[48,1920]{1,0:T(8,128)(2,1)} %get-tuple-element.184), channel_id=1, source_target_pairs={{0,2},{1,3},{2,0},{3,1},{4,6},{5,7},{6,4},{7,5},{8,10},{9,11},{10,... | collective-permute-start | bytes 552968 | tf_op jit(solution)/shard_map/ppermute | solution.py:422
  49.3 15.1 %collective-permute-start.12 = (bf16[48,1920]{1,0:T(8,128)(2,1)}, bf16[48,1920]{1,0:T(8,128)(2,1)S(1)}, u32[]{:S(2)}, u32[]{:S(2)}) collective-permute-start(bf16[48,1920]{1,0:T(8,128)(2,1)} %get-tuple-element.184), channel_id=1, source_target_pairs={{0,3},{1,2},{2,1},{3,0},{4,7},{5,6},{6,5},{7,4},{8,11},{9,10},{10,... | collective-permute-start | bytes 552968 | tf_op jit(solution)/shard_map/ppermute | solution.py:422
  77.1 16.6 %collective-permute-start.17 = (bf16[144,1920]{1,0:T(8,128)(2,1)S(1)}, bf16[144,1920]{1,0:T(8,128)(2,1)S(1)}, u32[]{:S(2)}, u32[]{:S(2)}) collective-permute-start(bf16[144,1920]{1,0:T(8,128)(2,1)S(1)} %shard_map.279.refs_2_), channel_id=1, source_target_pairs={{0,8},{4,12},{8,0},{12,4},{16,24},{20,28},{24,16},{28,20},{1,9},{5... | collective-permute-start | bytes 1658888 | tf_op jit(solution)/shard_map/ppermute | solution.py:414
  78.3 15.4 %collective-permute-start.18 = (bf16[144,1920]{1,0:T(8,128)(2,1)S(1)}, bf16[144,1920]{1,0:T(8,128)(2,1)S(1)}, u32[]{:S(2)}, u32[]{:S(2)}) collective-permute-start(bf16[144,1920]{1,0:T(8,128)(2,1)S(1)} %shard_map.279.refs_2_), channel_id=1, source_target_pairs={{0,16},{4,20},{8,24},{12,28},{16,0},{20,4},{24,8},{28,12},{1,17},{... | collective-permute-start | bytes 1658888 | tf_op jit(solution)/shard_map/ppermute | solution.py:418
  79.6 23.1 %collective-permute-start.19 = (bf16[144,1920]{1,0:T(8,128)(2,1)S(1)}, bf16[144,1920]{1,0:T(8,128)(2,1)S(1)}, u32[]{:S(2)}, u32[]{:S(2)}) collective-permute-start(bf16[144,1920]{1,0:T(8,128)(2,1)S(1)} %shard_map.279.refs_2_), channel_id=1, source_target_pairs={{0,24},{4,28},{8,16},{12,20},{16,8},{20,12},{24,0},{28,4},{1,25},{... | collective-permute-start | bytes 1658888 | tf_op jit(solution)/shard_map/ppermute | solution.py:426
  79.8 10.5 %collective-permute-start.15 = (bf16[256,768]{1,0:T(8,128)(2,1)S(1)}, bf16[256,768]{1,0:T(8,128)(2,1)S(1)}, u32[]{:S(2)}, u32[]{:S(2)}) collective-permute-start(bf16[256,768]{1,0:T(8,128)(2,1)S(1)} %copy-done.35), channel_id=1, source_target_pairs={{0,0},{1,1},{2,4},{3,5},{4,2},{5,3},{6,6},{7,7},{8,8},{9,9},{10,12... | collective-permute-start | bytes 1179656 | tf_op jit(solution)/shard_map/ppermute | solution.py:448
  82.4 10.4 %collective-permute-start.16 = (bf16[256,768]{1,0:T(8,128)(2,1)S(1)}, bf16[256,768]{1,0:T(8,128)(2,1)S(1)}, u32[]{:S(2)}, u32[]{:S(2)}) collective-permute-start(bf16[256,768]{1,0:T(8,128)(2,1)S(1)} %copy-done.34), channel_id=1, source_target_pairs={{0,1},{1,0},{2,5},{3,4},{4,3},{5,2},{6,7},{7,6},{8,9},{9,8},{10,13... | collective-permute-start | bytes 1179656 | tf_op jit(solution)/shard_map/ppermute | solution.py:452
  110.0 8.4 %collective-permute-start.21 = (bf16[1024,768]{1,0:T(8,128)(2,1)S(1)}, bf16[1024,768]{1,0:T(8,128)(2,1)S(1)}, u32[]{:S(2)}, u32[]{:S(2)}) collective-permute-start(bf16[1024,768]{1,0:T(8,128)(2,1)S(1)} %convolution_convert_fusion.2.part_ref), channel_id=1, source_target_pairs={{0,4},{4,0},{8,12},{12,8},{16,20},{20,16},{24,28},{28,24},{1,5},{5... | collective-permute-start | bytes 4718600 | tf_op jit(solution)/shard_map/ppermute | solution.py:410
  110.9 17.3 %collective-permute-start.24 = (bf16[288,768]{1,0:T(8,128)(2,1)S(1)}, bf16[288,768]{1,0:T(8,128)(2,1)S(1)}, u32[]{:S(2)}, u32[]{:S(2)}) collective-permute-start(bf16[288,768]{1,0:T(8,128)(2,1)S(1)} %shard_map.283.refs_1_), channel_id=1, source_target_pairs={{0,8},{4,12},{8,0},{12,4},{16,24},{20,28},{24,16},{28,20},{1,9},{5... | collective-permute-start | bytes 1327112 | tf_op jit(solution)/shard_map/ppermute | solution.py:414
  111.9 16.4 %collective-permute-start.25 = (bf16[288,768]{1,0:T(8,128)(2,1)S(1)}, bf16[288,768]{1,0:T(8,128)(2,1)S(1)}, u32[]{:S(2)}, u32[]{:S(2)}) collective-permute-start(bf16[288,768]{1,0:T(8,128)(2,1)S(1)} %shard_map.283.refs_1_), channel_id=1, source_target_pairs={{0,16},{4,20},{8,24},{12,28},{16,0},{20,4},{24,8},{28,12},{1,17},{... | collective-permute-start | bytes 1327112 | tf_op jit(solution)/shard_map/ppermute | solution.py:418
  114.6 18.4 %collective-permute-start.26 = (bf16[288,768]{1,0:T(8,128)(2,1)S(1)}, bf16[288,768]{1,0:T(8,128)(2,1)S(1)}, u32[]{:S(2)}, u32[]{:S(2)}) collective-permute-start(bf16[288,768]{1,0:T(8,128)(2,1)S(1)} %shard_map.283.refs_1_), channel_id=1, source_target_pairs={{0,24},{4,28},{8,16},{12,20},{16,8},{20,12},{24,0},{28,4},{1,25},{... | collective-permute-start | bytes 1327112 | tf_op jit(solution)/shard_map/ppermute | solution.py:426
  156.2 25.5 %collective-permute-start.31 = (bf16[4,2,48,768]{3,2,1,0:T(8,128)(2,1)S(1)}, bf16[4,2,48,768]{3,2,1,0:T(8,128)(2,1)S(1)}, u32[]{:S(2)}, u32[]{:S(2)}) collective-permute-start(bf16[4,2,48,768]{3,2,1,0:T(8,128)(2,1)S(1)} %get-tuple-element.338), channel_id=1, source_target_pairs={{0,8},{4,12},{8,0},{12,4},{16,24},{20,28},{24,16},{28,20},{1,9},{5... | collective-permute-start | bytes 1769480 | tf_op jit(solution)/shard_map/ppermute | solution.py:414
  156.8 24.8 %collective-permute-start.32 = (bf16[4,2,48,768]{3,2,1,0:T(8,128)(2,1)S(1)}, bf16[4,2,48,768]{3,2,1,0:T(8,128)(2,1)S(1)}, u32[]{:S(2)}, u32[]{:S(2)}) collective-permute-start(bf16[4,2,48,768]{3,2,1,0:T(8,128)(2,1)S(1)} %get-tuple-element.336), channel_id=1, source_target_pairs={{0,16},{4,20},{8,24},{12,28},{16,0},{20,4},{24,8},{28,12},{1,17},{... | collective-permute-start | bytes 1769480 | tf_op jit(solution)/shard_map/ppermute | solution.py:418
  158.1 23.4 %collective-permute-start.28 = (bf16[256,768]{1,0:T(8,128)(2,1)S(1)}, bf16[256,768]{1,0:T(8,128)(2,1)S(1)}, u32[]{:S(2)}, u32[]{:S(2)}) collective-permute-start(bf16[256,768]{1,0:T(8,128)(2,1)S(1)} %get-tuple-element.213), channel_id=1, source_target_pairs={{0,0},{1,1},{4,2},{5,3},{2,4},{3,5},{6,6},{7,7},{8,8},{9,9},{12,10... | collective-permute-start | bytes 1179656 | tf_op jit(solution)/shard_map/ppermute | solution.py:460
  165.9 8.6 %collective-permute-start.29 = (bf16[1024,768]{1,0:T(8,128)(2,1)S(1)}, bf16[1024,768]{1,0:T(8,128)(2,1)S(1)}, u32[]{:S(2)}, u32[]{:S(2)}) collective-permute-start(bf16[1024,768]{1,0:T(8,128)(2,1)S(1)} %get-tuple-element.218.part_ref), channel_id=1, source_target_pairs={{0,4},{4,0},{8,12},{12,8},{16,20},{20,16},{24,28},{28,24},{1,5},{5... | collective-permute-start | bytes 4718600 | tf_op jit(solution)/shard_map/ppermute | solution.py:410
  174.1 21.7 %collective-permute-start.33 = (bf16[4,2,24,1536]{3,2,1,0:T(8,128)(2,1)S(1)}, bf16[4,2,24,1536]{3,2,1,0:T(8,128)(2,1)S(1)}, u32[]{:S(2)}, u32[]{:S(2)}) collective-permute-start(bf16[4,2,24,1536]{3,2,1,0:T(8,128)(2,1)S(1)} %get-tuple-element.334), channel_id=1, source_target_pairs={{0,8},{4,12},{8,0},{12,4},{16,24},{20,28},{24,16},{28,20},{1,9},{5... | collective-permute-start | bytes 1769480 | tf_op jit(solution)/shard_map/ppermute | solution.py:414
  174.5 21.3 %collective-permute-start.34 = (bf16[4,2,24,1536]{3,2,1,0:T(8,128)(2,1)S(1)}, bf16[4,2,24,1536]{3,2,1,0:T(8,128)(2,1)S(1)}, u32[]{:S(2)}, u32[]{:S(2)}) collective-permute-start(bf16[4,2,24,1536]{3,2,1,0:T(8,128)(2,1)S(1)} %get-tuple-element.332), channel_id=1, source_target_pairs={{0,16},{4,20},{8,24},{12,28},{16,0},{20,4},{24,8},{28,12},{1,17},{... | collective-permute-start | bytes 1769480 | tf_op jit(solution)/shard_map/ppermute | solution.py:418
  181.5 9.7 %collective-permute-start.30 = (bf16[256,768]{1,0:T(8,128)(2,1)S(1)}, bf16[256,768]{1,0:T(8,128)(2,1)S(1)}, u32[]{:S(2)}, u32[]{:S(2)}) collective-permute-start(bf16[256,768]{1,0:T(8,128)(2,1)S(1)} %get-tuple-element.227), channel_id=1, source_target_pairs={{1,0},{0,1},{5,2},{4,3},{3,4},{2,5},{7,6},{6,7},{9,8},{8,9},{13,10... | collective-permute-start | bytes 1179656 | tf_op jit(solution)/shard_map/ppermute | solution.py:460
  182.1 13.4 %collective-permute-start.35 = (bf16[4,48,768]{2,1,0:T(8,128)(2,1)S(1)}, bf16[4,48,768]{2,1,0:T(8,128)(2,1)S(1)}, u32[]{:S(2)}, u32[]{:S(2)}) collective-permute-start(bf16[4,48,768]{2,1,0:T(8,128)(2,1)S(1)} %get-tuple-element.362), channel_id=1, source_target_pairs={{0,16},{4,20},{8,24},{12,28},{16,0},{20,4},{24,8},{28,12},{1,17},{... | collective-permute-start | bytes 884744 | tf_op jit(solution)/shard_map/ppermute | solution.py:418
  182.4 13.1 %collective-permute-start.36 = (bf16[4,48,768]{2,1,0:T(8,128)(2,1)S(1)}, bf16[4,48,768]{2,1,0:T(8,128)(2,1)S(1)}, u32[]{:S(2)}, u32[]{:S(2)}) collective-permute-start(bf16[4,48,768]{2,1,0:T(8,128)(2,1)S(1)} %get-tuple-element.360), channel_id=1, source_target_pairs={{0,8},{4,12},{8,0},{12,4},{16,24},{20,28},{24,16},{28,20},{1,9},{5... | collective-permute-start | bytes 884744 | tf_op jit(solution)/shard_map/ppermute | solution.py:414
  196.2 14.3 %collective-permute-start.37 = (bf16[4,24,1536]{2,1,0:T(8,128)(2,1)S(1)}, bf16[4,24,1536]{2,1,0:T(8,128)(2,1)S(1)}, u32[]{:S(2)}, u32[]{:S(2)}) collective-permute-start(bf16[4,24,1536]{2,1,0:T(8,128)(2,1)S(1)} %get-tuple-element.358), channel_id=1, source_target_pairs={{0,16},{4,20},{8,24},{12,28},{16,0},{20,4},{24,8},{28,12},{1,17},{... | collective-permute-start | bytes 884744 | tf_op jit(solution)/shard_map/ppermute | solution.py:418
  197.2 13.4 %collective-permute-start.38 = (bf16[4,24,1536]{2,1,0:T(8,128)(2,1)S(1)}, bf16[4,24,1536]{2,1,0:T(8,128)(2,1)S(1)}, u32[]{:S(2)}, u32[]{:S(2)}) collective-permute-start(bf16[4,24,1536]{2,1,0:T(8,128)(2,1)S(1)} %get-tuple-element.356), channel_id=1, source_target_pairs={{0,8},{4,12},{8,0},{12,4},{16,24},{20,28},{24,16},{28,20},{1,9},{5... | collective-permute-start | bytes 884744 | tf_op jit(solution)/shard_map/ppermute | solution.py:414
  197.7 12.7 %collective-permute-start.39 = (bf16[2,96,768]{2,1,0:T(8,128)(2,1)S(1)}, bf16[2,96,768]{2,1,0:T(8,128)(2,1)S(1)}, u32[]{:S(2)}, u32[]{:S(2)}) collective-permute-start(bf16[2,96,768]{2,1,0:T(8,128)(2,1)S(1)} %get-tuple-element.354), channel_id=1, source_target_pairs={{0,1},{1,0},{2,3},{3,2},{4,5},{5,4},{6,7},{7,6},{8,9},{9,8},{10,11... | collective-permute-start | bytes 884744 | tf_op jit(solution)/shard_map/ppermute | solution.py:422
  208.6 12.9 %collective-permute-start.42 = (bf16[4,2,24,1152]{3,2,1,0:T(8,128)(2,1)S(1)}, bf16[4,2,24,1152]{3,2,1,0:T(8,128)(2,1)S(1)}, u32[]{:S(2)}, u32[]{:S(2)}) collective-permute-start(bf16[4,2,24,1152]{3,2,1,0:T(8,128)(2,1)S(1)} %pad_maximum_fusion.3), channel_id=1, source_target_pairs={{0,8},{4,12},{8,0},{12,4},{16,24},{20,28},{24,16},{28,20},{1,9},{5... | collective-permute-start | bytes 1327112 | tf_op jit(solution)/shard_map/ppermute | solution.py:414
  209.7 11.8 %collective-permute-start.43 = (bf16[4,2,24,1152]{3,2,0,1:T(8,128)(2,1)S(1)}, bf16[4,2,24,1152]{3,2,0,1:T(8,128)(2,1)S(1)}, u32[]{:S(2)}, u32[]{:S(2)}) collective-permute-start(bf16[4,2,24,1152]{3,2,0,1:T(8,128)(2,1)S(1)} %pad_maximum_fusion.4), channel_id=1, source_target_pairs={{0,16},{4,20},{8,24},{12,28},{16,0},{20,4},{24,8},{28,12},{1,17},{... | collective-permute-start | bytes 1327112 | tf_op jit(solution)/shard_map/ppermute | solution.py:418
  210.8 15.5 %collective-permute-start.40 = (bf16[2,48,1536]{2,1,0:T(8,128)(2,1)S(1)}, bf16[2,48,1536]{2,1,0:T(8,128)(2,1)S(1)}, u32[]{:S(2)}, u32[]{:S(2)}) collective-permute-start(bf16[2,48,1536]{2,1,0:T(8,128)(2,1)S(1)} %get-tuple-element.350), channel_id=1, source_target_pairs={{0,1},{1,0},{2,3},{3,2},{4,5},{5,4},{6,7},{7,6},{8,9},{9,8},{10,11... | collective-permute-start | bytes 884744 | tf_op jit(solution)/shard_map/ppermute | solution.py:422
  212.3 13.3 %collective-permute-start.41 = (bf16[96,768]{1,0:T(8,128)(2,1)S(1)}, bf16[96,768]{1,0:T(8,128)(2,1)S(1)}, u32[]{:S(2)}, u32[]{:S(2)}) collective-permute-start(bf16[96,768]{1,0:T(8,128)(2,1)S(1)} %get-tuple-element.376), channel_id=1, source_target_pairs={{0,2},{1,3},{2,0},{3,1},{4,6},{5,7},{6,4},{7,5},{8,10},{9,11},{10,... | collective-permute-start | bytes 442376 | tf_op jit(solution)/shard_map/ppermute | solution.py:422
  221.8 17.9 %collective-permute-start.50 = (bf16[4,24,1152]{2,1,0:T(8,128)(2,1)S(1)}, bf16[4,24,1152]{2,1,0:T(8,128)(2,1)S(1)}, u32[]{:S(2)}, u32[]{:S(2)}) collective-permute-start(bf16[4,24,1152]{2,1,0:T(8,128)(2,1)S(1)} %dynamic-slice_bitcast_fusion.24), channel_id=1, source_target_pairs={{0,8},{4,12},{8,0},{12,4},{16,24},{20,28},{24,16},{28,20},{1,9},{5... | collective-permute-start | bytes 663560 | tf_op jit(solution)/shard_map/ppermute | solution.py:414
  223.1 17.1 %collective-permute-start.49 = (bf16[4,24,1152]{2,1,0:T(8,128)(2,1)S(1)}, bf16[4,24,1152]{2,1,0:T(8,128)(2,1)S(1)}, u32[]{:S(2)}, u32[]{:S(2)}) collective-permute-start(bf16[4,24,1152]{2,1,0:T(8,128)(2,1)S(1)} %dynamic-slice_bitcast_fusion.25), channel_id=1, source_target_pairs={{0,16},{4,20},{8,24},{12,28},{16,0},{20,4},{24,8},{28,12},{1,17},{... | collective-permute-start | bytes 663560 | tf_op jit(solution)/shard_map/ppermute | solution.py:418
  225.6 10.3 %collective-permute-start.46 = (bf16[4,2,24,512]{3,2,1,0:T(8,128)(2,1)S(1)}, bf16[4,2,24,512]{3,2,1,0:T(8,128)(2,1)S(1)}, u32[]{:S(2)}, u32[]{:S(2)}) collective-permute-start(bf16[4,2,24,512]{3,2,1,0:T(8,128)(2,1)S(1)} %pad_maximum_fusion.8), channel_id=1, source_target_pairs={{0,16},{4,20},{8,24},{12,28},{16,0},{20,4},{24,8},{28,12},{1,17},{... | collective-permute-start | bytes 589832 | tf_op jit(solution)/shard_map/ppermute | solution.py:418
  226.3 12.4 %collective-permute-start.44 = (bf16[96,768]{1,0:T(8,128)(2,1)S(1)}, bf16[96,768]{1,0:T(8,128)(2,1)S(1)}, u32[]{:S(2)}, u32[]{:S(2)}) collective-permute-start(bf16[96,768]{1,0:T(8,128)(2,1)S(1)} %add_convert_fusion.19), channel_id=1, source_target_pairs={{0,8},{4,12},{8,0},{12,4},{16,24},{20,28},{24,16},{28,20},{1,9},{5... | collective-permute-start | bytes 442376 | tf_op jit(solution)/shard_map/ppermute | solution.py:414
  231.6 9.6 %collective-permute-start.47 = (bf16[512,768]{1,0:T(8,128)(2,1)S(1)}, bf16[512,768]{1,0:T(8,128)(2,1)S(1)}, u32[]{:S(2)}, u32[]{:S(2)}) collective-permute-start(bf16[512,768]{1,0:T(8,128)(2,1)S(1)} %convolution_convert_fusion.6), channel_id=1, source_target_pairs={{0,4},{4,0},{8,12},{12,8},{16,20},{20,16},{24,28},{28,24},{1,5},{5... | collective-permute-start | bytes 2359304 | tf_op jit(solution)/shard_map/ppermute | solution.py:410
  235.9 10.0 %collective-permute-start.53 = (bf16[48,1536]{1,0:T(8,128)(2,1)S(1)}, bf16[48,1536]{1,0:T(8,128)(2,1)S(1)}, u32[]{:S(2)}, u32[]{:S(2)}) collective-permute-start(bf16[48,1536]{1,0:T(8,128)(2,1)S(1)} %get-tuple-element.366), channel_id=1, source_target_pairs={{0,2},{1,3},{2,0},{3,1},{4,6},{5,7},{6,4},{7,5},{8,10},{9,11},{10,... | collective-permute-start | bytes 442376 | tf_op jit(solution)/shard_map/ppermute | solution.py:422
  240.2 9.0 %collective-permute-start.56 = (bf16[192,768]{1,0:T(8,128)(2,1)S(1)}, bf16[192,768]{1,0:T(8,128)(2,1)S(1)}, u32[]{:S(2)}, u32[]{:S(2)}) collective-permute-start(bf16[192,768]{1,0:T(8,128)(2,1)S(1)} %constant_dynamic-update-slice_fusion.18), channel_id=1, source_target_pairs={{0,16},{4,20},{8,24},{12,28},{16,0},{20,4},{24,8},{28,12},{1,17},{... | collective-permute-start | bytes 884744 | tf_op jit(solution)/shard_map/ppermute | solution.py:418
  241.5 17.8 %collective-permute-start.48 = (bf16[256,768]{1,0:T(8,128)(2,1)S(1)}, bf16[256,768]{1,0:T(8,128)(2,1)S(1)}, u32[]{:S(2)}, u32[]{:S(2)}) collective-permute-start(bf16[256,768]{1,0:T(8,128)(2,1)S(1)} %get-tuple-element.340), channel_id=1, source_target_pairs={{0,0},{1,1},{4,2},{5,3},{2,4},{3,5},{6,6},{7,7},{8,8},{9,9},{12,10... | collective-permute-start | bytes 1179656 | tf_op jit(solution)/shard_map/ppermute | solution.py:460
  247.1 12.2 %collective-permute-start.54 = (bf16[2,48,1664]{2,1,0:T(8,128)(2,1)S(1)}, bf16[2,48,1664]{2,1,0:T(8,128)(2,1)S(1)}, u32[]{:S(2)}, u32[]{:S(2)}) collective-permute-start(bf16[2,48,1664]{2,1,0:T(8,128)(2,1)S(1)} %get-tuple-element.341), channel_id=1, source_target_pairs={{0,1},{1,0},{2,3},{3,2},{4,5},{5,4},{6,7},{7,6},{8,9},{9,8},{10,11... | collective-permute-start | bytes 958472 | tf_op jit(solution)/shard_map/ppermute | solution.py:422
  249.3 13.6 %collective-permute-start.61 = (bf16[384,768]{1,0:T(8,128)(2,1)S(1)}, bf16[384,768]{1,0:T(8,128)(2,1)S(1)}, u32[]{:S(2)}, u32[]{:S(2)}) collective-permute-start(bf16[384,768]{1,0:T(8,128)(2,1)S(1)} %constant_dynamic-update-slice_fusion.20.mine_ref), channel_id=1, source_target_pairs={{0,4},{4,0},{8,12},{12,8},{16,20},{20,16},{24,28},{28,24},{1,5},{5... | collective-permute-start | bytes 1769480 | tf_op jit(solution)/shard_map/ppermute | solution.py:410
  262.0 14.1 %collective-permute-start.58 = (bf16[48,1664]{1,0:T(8,128)(2,1)S(1)}, bf16[48,1664]{1,0:T(8,128)(2,1)S(1)}, u32[]{:S(2)}, u32[]{:S(2)}) collective-permute-start(bf16[48,1664]{1,0:T(8,128)(2,1)S(1)} %get-tuple-element.364), channel_id=1, source_target_pairs={{0,2},{1,3},{2,0},{3,1},{4,6},{5,7},{6,4},{7,5},{8,10},{9,11},{10,... | collective-permute-start | bytes 479240 | tf_op jit(solution)/shard_map/ppermute | solution.py:422
  262.5 16.4 %collective-permute-start.57 = (bf16[256,768]{1,0:T(8,128)(2,1)S(1)}, bf16[256,768]{1,0:T(8,128)(2,1)S(1)}, u32[]{:S(2)}, u32[]{:S(2)}) collective-permute-start(bf16[256,768]{1,0:T(8,128)(2,1)S(1)} %get-tuple-element.297), channel_id=1, source_target_pairs={{1,0},{0,1},{5,2},{4,3},{3,4},{2,5},{7,6},{6,7},{9,8},{8,9},{13,10... | collective-permute-start | bytes 1179656 | tf_op jit(solution)/shard_map/ppermute | solution.py:460
  (54 other events, 396.5 us)

commit v2 on v1

--- a/solution.py
+++ b/solution.py
@@ -1282,7 +1282,7 @@
     g_out = contract_rows(context_all, after(dattn_part, grad_ctx)).astype(BF)
     down_state, sent = reduce_second(after(down_state, g_out), col, row)
     layer_first = return_block(after(out_first, g_down), 0)
-    layer_second = return_block(after(out_second, layer_first, g_out), 1)
+    layer_second = return_block(after(out_second, layer_first, g_up), 1)
 
     dqkv = []
     side = lambda parts: jnp.concatenate(parts, axis=1)

time: 297 us -> 297 us (level)
  no operation moved by 1% of the time
where the time goes in v2:
time: 297 us; the launch traced here: 291 us
  Pallas kernels  89 us (30%)
  starting transfers between devices  83.8 us (28%)
  waiting for transfers between devices  70 us (24%)
  matrix products  19.7 us (7%)
  local copies, waits for them, and re-layouts  18.2 us (6%)
  other arithmetic  7.77 us (3%)
    ppermute x12, starting transfers between devices, swap_core(): return lax.ppermute(value, 'grp', [(i, i ^ 1) for i in range(8)])  27.8 us
    pallas_call x3, Pallas kernels, attend_chip_backward(): pl.pallas_call(attend_bwd_kernel, grid=(1,), out_shape=[jax.ShapeDtypeStr...  22.5 us
    ppermute x14, waiting for transfers between devices, swap_z(): return lax.ppermute(value, 'shard', [(i, i ^ flip) for i in range(4)])  21 us
    pallas_call x14, Pallas kernels, move_blocks(): pl.pallas_call(functools.partial(move_kernel, len(sources), moves), out_s...  20.8 us
    ppermute x14, starting transfers between devices, swap_z(): return lax.ppermute(value, 'shard', [(i, i ^ flip) for i in range(4)])  19.8 us
    ppermute x4, waiting for transfers between devices, swap_xy(): return lax.ppermute(value, 'grp', [(i, i ^ 6) for i in range(8)])  19.2 us
    unnamed x92, local copies, waits for them, and re-layouts  15.1 us
    pallas_call x3, Pallas kernels, attend_chip_forward(): pl.pallas_call(attend_fwd_kernel, grid=(1,), out_shape=[jax.ShapeDtypeStr...  13.1 us
  transfers between devices with their start and end apart: 66, of which 20 were waited for; matrix products, arithmetic and copies ran while one was open for 8% of the time, Pallas kernels for 24%

profile of v2, /device:TPU:25, one launch (start us, length us, event | category | flops | bytes accessed | tf_op | source)
XLA Modules:
  0.0 291.4 jit_solution(8738616438835581956)
XLA Ops:
  1.3 2.3 shard_map.271.own_ref
  3.8 3.4 %collective-permute-start.4 = (bf16[64,1152]{1,0:T(8,128)(2,1)}, bf16[64,1152]{1,0:T(8,128)(2,1)S(1)}, u32[]{:S(2)}, u32[]{:S(2)}) collective-permute-start(bf16[64,1152]{1,0:T(8,128)(2,1)} %shard_map.271.own_ref), channel_id=1, source_target_pairs={{0,3},{1,2},{2,1},{3,0},{4,7},{5,6},{6,5},{7,4},{8,11},{9,10},{10,... | collective-permute-start | bytes 442376 | tf_op jit(solution)/shard_map/ppermute | solution.py:422
  12.6 3.6 %shard_map.272 = (bf16[256,768]{1,0:T(8,128)(2,1)}, bf16[256,768]{1,0:T(8,128)(2,1)}, bf16[256,768]{1,0:T(8,128)(2,1)}, bf16[256,768]{1,0:T(8,128)(2,1)}, bf16[4...) custom-call(s32[4]{0:T(128)} %pad_add_fusion.where_ref, bf16[512,768]{1,0:T(8,128)(2,1)} %bitcast.196, ...), custom_call_target="tpu_custom_call" | custom-call | flops 1024 | bytes 1024 | tf_op jit(solution)/shard_map/pallas_call | solution.py:498
  21.8 3.1 %collective-permute-start.2 = (bf16[256,768]{1,0:T(8,128)(2,1)}, bf16[256,768]{1,0:T(8,128)(2,1)S(1)}, u32[]{:S(2)}, u32[]{:S(2)}) collective-permute-start(bf16[256,768]{1,0:T(8,128)(2,1)} %get-tuple-element.172), channel_id=1, source_target_pairs={{0,1},{1,0},{2,5},{3,4},{4,3},{5,2},{6,7},{7,6},{8,9},{9,8},{10,13... | collective-permute-start | bytes 1179656 | tf_op jit(solution)/shard_map/ppermute | solution.py:452
  25.8 8.0 %collective-permute-done.2.refs_1_ = bf16[256,768]{1,0:T(8,128)(2,1)S(1)} collective-permute-done((bf16[256,768]{1,0:T(8,128)(2,1)}, bf16[256,768]{1,0:T(8,128)(2,1)S(1)}, u32[]{:S(2)}, u32[]{:S(2)}) %collective-permute-start.2) | collective-permute-done | bytes 393248 | tf_op jit(solution)/shard_map/ppermute | solution.py:452
  34.6 2.5 collective-permute-done.8.refs_4_
  38.8 7.2 %collective-permute-start.9 = (bf16[512,768]{1,0:T(8,128)(2,1)S(1)}, bf16[512,768]{1,0:T(8,128)(2,1)}, u32[]{:S(2)}, u32[]{:S(2)}) collective-permute-start(bf16[512,768]{1,0:T(8,128)(2,1)S(1)} %shard_map.275.refs_0_), channel_id=1, source_target_pairs={{0,4},{4,0},{8,12},{12,8},{16,20},{20,16},{24,28},{28,24},{1,5},{5... | collective-permute-start | bytes 2359304 | tf_op jit(solution)/shard_map/ppermute | solution.py:410
  46.0 3.3 %collective-permute-start.10 = (bf16[48,1920]{1,0:T(8,128)(2,1)}, bf16[48,1920]{1,0:T(8,128)(2,1)S(1)}, u32[]{:S(2)}, u32[]{:S(2)}) collective-permute-start(bf16[48,1920]{1,0:T(8,128)(2,1)} %get-tuple-element.184), channel_id=1, source_target_pairs={{0,1},{1,0},{2,3},{3,2},{4,5},{5,4},{6,7},{7,6},{8,9},{9,8},{10,11... | collective-permute-start | bytes 552968 | tf_op jit(solution)/shard_map/ppermute | solution.py:422
  49.3 2.2 collective-permute-start.12
  53.5 2.5 shard_map.277
  57.8 2.2 add_convert_fusion.q_ref.k_ref.v_ref
  60.0 4.4 %shard_map.278 = (bf16[1024,128]{1,0:T(8,128)(2,1)S(1)}, f32[1,2,1024]{2,1,0:T(2,128)S(1)}) custom-call(bf16[1024,1152]{1,0:T(8,128)(2,1)S(1)} %add_convert_fusion.q_ref.k_ref.v_ref, bf16[1024,1152]{1,0:T(8,128)(2,1)S(1)} %add_convert_fusion.q_ref.k_ref.v_ref, bf16[1024,1152]{1,0:T(8,128)(2,1)S(1)} %add_convert_fusion.q_ref.k_ref.v_ref, ...), custom_call_target="tpu_custom_call" | custom-call | flops 1024 | bytes 1024 | tf_op jit(solution)/shard_map/pallas_call | solution.py:947
  65.8 3.5 %collective-permute-start.13 = (bf16[96,768]{1,0:T(8,128)(2,1)S(1)}, bf16[96,768]{1,0:T(8,128)(2,1)S(1)}, u32[]{:S(2)}, u32[]{:S(2)}) collective-permute-start(bf16[96,768]{1,0:T(8,128)(2,1)S(1)} %copy-done.29), channel_id=1, source_target_pairs={{0,2},{1,3},{2,0},{3,1},{4,6},{5,7},{6,4},{7,5},{8,10},{9,11},{10,... | collective-permute-start | bytes 442376 | tf_op jit(solution)/shard_map/ppermute | solution.py:422
  69.2 4.3 %shard_map.280 = (bf16[1024,128]{1,0:T(8,128)(2,1)S(1)}, f32[1,2,1024]{2,1,0:T(2,128)S(1)}) custom-call(bf16[1024,1152]{1,0:T(8,128)(2,1)S(1)} %add_convert_fusion.q_ref.k_ref.v_ref, bf16[1024,1152]{1,0:T(8,128)(2,1)S(1)} %add_convert_fusion.q_ref.k_ref.v_ref, bf16[1024,1152]{1,0:T(8,128)(2,1)S(1)} %add_convert_fusion.q_ref.k_ref.v_ref, ...), custom_call_target="tpu_custom_call" | custom-call | flops 1024 | bytes 1024 | tf_op jit(solution)/shard_map/pallas_call | solution.py:947
  74.5 2.6 collective-permute-start.14
  82.4 2.2 collective-permute-start.16
  84.7 4.4 %shard_map.282 = (bf16[1024,128]{1,0:T(8,128)(2,1)S(1)}, f32[1,2,1024]{2,1,0:T(2,128)S(1)}) custom-call(bf16[1024,1152]{1,0:T(8,128)(2,1)S(1)} %add_convert_fusion.q_ref.k_ref.v_ref, bf16[1024,1152]{1,0:T(8,128)(2,1)S(1)} %add_convert_fusion.q_ref.k_ref.v_ref, bf16[1024,1152]{1,0:T(8,128)(2,1)S(1)} %add_convert_fusion.q_ref.k_ref.v_ref, ...), custom_call_target="tpu_custom_call" | custom-call | flops 1024 | bytes 1024 | tf_op jit(solution)/shard_map/pallas_call | solution.py:947
  90.3 2.5 collective-permute-done.16.refs_1_
  93.8 8.9 %collective-permute-done.19.refs_5_ = bf16[144,1920]{1,0:T(8,128)(2,1)S(1)} collective-permute-done((bf16[144,1920]{1,0:T(8,128)(2,1)S(1)}, bf16[144,1920]{1,0:T(8,128)(2,1)S(1)}, u32[]{:S(2)}, u32[]{:S(2)}) %collective-permute-start.19) | collective-permute-done | bytes 552992 | tf_op jit(solution)/shard_map/ppermute | solution.py:426
  104.2 2.6 collective-permute-start.20
  112.4 2.2 collective-permute-done.22.refs_1_
  118.4 7.0 %shard_map.287 = (bf16[1024,768]{1,0:T(8,128)(2,1)S(1)}, f32[1024,768]{1,0:T(8,128)S(1)}, f32[1024,128]{1,0:T(8,128)S(1)}, bf16[1024,1536]{1,0:T(8,128)(2,1)S(1)}, bf16[1024,1536]{1,0:T(8,128)(2,1)S(1)}) custom-call(bf16[1024,768]{1,0:T(8,128)(2,1)S(1)} %convolution_convert_fusion.2.part_ref, bf16[1024,768]{1,0:T(8,128)(2,1)S(1)} %collective-permute-done.21.got_ref, ...), custom_call_target="tpu_custom_call" | custom-call | flops 1024 | bytes 1024 | tf_op jit(solution)/shard_map/pallas_call | solution.py:698
  128.3 4.7 %collective-permute-done.26.refs_4_ = bf16[288,768]{1,0:T(8,128)(2,1)S(1)} collective-permute-done((bf16[288,768]{1,0:T(8,128)(2,1)S(1)}, bf16[288,768]{1,0:T(8,128)(2,1)S(1)}, u32[]{:S(2)}, u32[]{:S(2)}) %collective-permute-start.26) | collective-permute-done | bytes 442400 | tf_op jit(solution)/shard_map/ppermute | solution.py:426
  133.0 3.1 %shard_map.290.down_ref = bf16[1536,768]{1,0:T(8,128)(2,1)S(1)} custom-call(s32[4]{0:T(128)S(1)} %copy-done.28, bf16[768,768]{1,0:T(8,128)(2,1)S(1)} %copy-done.12, bf16[288,768]{1,0:T(8,128)(2,1)S(1)} %shard_map.283.refs_1_, bf16[288,768]{1,0:T(8,128)(2,1)S(1)} %collective-permute-done.24.refs_2_, bf16[288,768]{1,0:T(8,128)(2,1)S(1)} %collective-permute-done.25.refs_3_, ...), custom_call_target="tpu_custom_call" | custom-call | flops 1024 | bytes 1024 | tf_op jit(solution)/shard_map/pallas_call | solution.py:498
  136.1 3.7 %convolution_convert_fusion.3.part_ref = bf16[1024,768]{1,0:T(8,128)(2,1)} fusion(bf16[1024,1536]{1,0:T(8,128)(2,1)S(1)} %get-tuple-element.206, bf16[1536,768]{1,0:T(8,128)(2,1)S(1)} %shard_map.290.down_ref), kind=kOutput, calls=%fused_computation.5 | convolution fusion | flops 2416705536 | bytes 7077888 | tf_op jit(solution)/shard_map/dot_general | solution.py:430
  140.8 3.4 %collective-permute-done.27.got_ref = bf16[1024,768]{1,0:T(8,128)(2,1)} collective-permute-done((bf16[1024,768]{1,0:T(8,128)(2,1)}, bf16[1024,768]{1,0:T(8,128)(2,1)}, u32[]{:S(2)}, u32[]{:S(2)}) %collective-permute-start.27) | collective-permute-done | bytes 1572896 | tf_op jit(solution)/shard_map/ppermute | solution.py:410
  147.5 5.4 %shard_map.291 = (bf16[256,768]{1,0:T(8,128)(2,1)S(1)}, bf16[256,768]{1,0:T(8,128)(2,1)S(1)}, f32[1024,768]{1,0:T(8,128)S(1)}, bf16[1024,768]{1,0:T(8,128)(2,1)S(1)}, f32[8,768]{1,0:T(8,128)S(1)}) custom-call(bf16[1024,768]{1,0:T(8,128)(2,1)} %convolution_convert_fusion.3.part_ref, bf16[1024,768]{1,0:T(8,128)(2,1)} %collective-permute-done.27.got_ref, ...), custom_call_target="tpu_custom_call" | custom-call | flops 1024 | bytes 1024 | tf_op jit(solution)/shard_map/pallas_call | solution.py:757
  152.9 2.9 %convolution_convert_fusion.1 = bf16[1536,768]{1,0:T(8,128)(2,1)S(1)} fusion(bf16[1024,1536]{1,0:T(8,128)(2,1)S(1)} %copy-done.31, bf16[1024,768]{1,0:T(8,128)(2,1)S(1)} %get-tuple-element.216.dffn_ref), kind=kOutput, calls=%fused_computation.3 | convolution fusion | flops 2417098752 | bytes 7077888 | tf_op jit(solution)/shard_map/dot_general | solution.py:38
  159.2 6.7 %shard_map.292 = (bf16[1024,1536]{1,0:T(8,128)(2,1)S(1)}, bf16[1024,768]{1,0:T(8,128)(2,1)S(1)}, f32[1,1536]{1,0:T(1,128)S(1)}) custom-call(bf16[1024,768]{1,0:T(8,128)(2,1)S(1)} %get-tuple-element.216.dffn_ref, bf16[1536,768]{1,0:T(8,128)(2,1)S(1)} %copy-done.6, bf16[1024,1536]{1,0:T(8,128)(2,1)S(1)} %copy-done.15, bf16[768,1536]{1,0:T(8,128)(2,1)S(1)} %copy-done.4), custom_call_target="tpu_custom_call" | custom-call | flops 1024 | bytes 1024 | tf_op jit(solution)/shard_map/pallas_call | solution.py:799
  165.9 4.8 %collective-permute-start.32 = (bf16[1024,768]{1,0:T(8,128)(2,1)S(1)}, bf16[1024,768]{1,0:T(8,128)(2,1)S(1)}, u32[]{:S(2)}, u32[]{:S(2)}) collective-permute-start(bf16[1024,768]{1,0:T(8,128)(2,1)S(1)} %get-tuple-element.219.part_ref), channel_id=1, source_target_pairs={{0,4},{4,0},{8,12},{12,8},{16,20},{20,16},{24,28},{28,24},{1,5},{5... | collective-permute-start | bytes 4718600 | tf_op jit(solution)/shard_map/ppermute | solution.py:410
  170.7 3.0 %convolution_convert_fusion = bf16[768,1536]{1,0:T(8,128)(2,1)S(1)} fusion(bf16[1024,768]{1,0:T(8,128)(2,1)S(1)} %copy-done.33, bf16[1024,1536]{1,0:T(8,128)(2,1)S(1)} %get-tuple-element.220), kind=kOutput, calls=%fused_computation.2 | convolution fusion | flops 2417098752 | bytes 7077888 | tf_op jit(solution)/shard_map/dot_general | solution.py:38
  175.9 3.1 %shard_map.293 = (f32[512,768]{1,0:T(8,128)S(1)}, bf16[1024,768]{1,0:T(8,128)(2,1)S(1)}, bf16[1024,384]{1,0:T(8,128)(2,1)S(1)}, f32[8,768]{1,0:T(8,128)S(1)}) custom-call(s32[4]{0:T(128)S(1)} %copy-done.28, f32[1024,768]{1,0:T(8,128)S(1)} %get-tuple-element.222.dr_ref, bf16[1024,768]{1,0:T(8,128)(2,1)S(1)} %get-tuple-element.219.part_ref, ...), custom_call_target="tpu_custom_call" | custom-call | flops 1024 | bytes 1024 | tf_op jit(solution)/shard_map/pallas_call | solution.py:842
  183.6 7.4 %shard_map.294 = (bf16[1024,128]{1,0:T(8,128)(2,1)S(1)}, bf16[1024,128]{1,0:T(8,128)(2,1)S(1)}, bf16[1024,128]{1,0:T(8,128)(2,1)S(1)}) custom-call(bf16[1024,1152]{1,0:T(8,128)(2,1)S(1)} %add_convert_fusion.q_ref.k_ref.v_ref, bf16[1024,1152]{1,0:T(8,128)(2,1)S(1)} %add_convert_fusion.q_ref.k_ref.v_ref, ...), custom_call_target="tpu_custom_call" | custom-call | flops 1024 | bytes 1024 | tf_op jit(solution)/shard_map/pallas_call | solution.py:966
  192.1 3.4 %collective-permute-done.35 = bf16[4,48,768]{2,1,0:T(8,128)(2,1)S(1)} collective-permute-done((bf16[4,48,768]{2,1,0:T(8,128)(2,1)S(1)}, bf16[4,48,768]{2,1,0:T(8,128)(2,1)S(1)}, u32[]{:S(2)}, u32[]{:S(2)}) %collective-permute-start.35) | collective-permute-done | bytes 294944 | tf_op jit(solution)/shard_map/ppermute | solution.py:418
  197.8 7.7 %shard_map.295 = (bf16[1024,128]{1,0:T(8,128)(2,1)S(1)}, bf16[1024,128]{1,0:T(8,128)(2,1)S(1)}, bf16[1024,128]{1,0:T(8,128)(2,1)S(1)}) custom-call(bf16[1024,1152]{1,0:T(8,128)(2,1)S(1)} %add_convert_fusion.q_ref.k_ref.v_ref, bf16[1024,1152]{1,0:T(8,128)(2,1)S(1)} %add_convert_fusion.q_ref.k_ref.v_ref, ...), custom_call_target="tpu_custom_call" | custom-call | flops 1024 | bytes 1024 | tf_op jit(solution)/shard_map/pallas_call | solution.py:966
  212.3 7.4 %shard_map.296 = (bf16[1024,128]{1,0:T(8,128)(2,1)S(1)}, bf16[1024,128]{1,0:T(8,128)(2,1)S(1)}, bf16[1024,128]{1,0:T(8,128)(2,1)S(1)}) custom-call(bf16[1024,1152]{1,0:T(8,128)(2,1)S(1)} %add_convert_fusion.q_ref.k_ref.v_ref, bf16[1024,1152]{1,0:T(8,128)(2,1)S(1)} %add_convert_fusion.q_ref.k_ref.v_ref, ...), custom_call_target="tpu_custom_call" | custom-call | flops 1024 | bytes 1024 | tf_op jit(solution)/shard_map/pallas_call | solution.py:966
  231.6 4.3 %collective-permute-start.47 = (bf16[512,768]{1,0:T(8,128)(2,1)S(1)}, bf16[512,768]{1,0:T(8,128)(2,1)S(1)}, u32[]{:S(2)}, u32[]{:S(2)}) collective-permute-start(bf16[512,768]{1,0:T(8,128)(2,1)S(1)} %convolution_convert_fusion.6), channel_id=1, source_target_pairs={{0,4},{4,0},{8,12},{12,8},{16,20},{20,16},{24,28},{28,24},{1,5},{5... | collective-permute-start | bytes 2359304 | tf_op jit(solution)/shard_map/ppermute | solution.py:410
  235.9 2.7 collective-permute-start.53
  242.2 3.7 %collective-permute-done.53 = bf16[48,1536]{1,0:T(8,128)(2,1)S(1)} collective-permute-done((bf16[48,1536]{1,0:T(8,128)(2,1)S(1)}, bf16[48,1536]{1,0:T(8,128)(2,1)S(1)}, u32[]{:S(2)}, u32[]{:S(2)}) %collective-permute-start.53) | collective-permute-done | bytes 147488 | tf_op jit(solution)/shard_map/ppermute | solution.py:422
  247.2 2.1 collective-permute-done.56
  252.6 6.7 %collective-permute-done.54 = bf16[2,48,1664]{2,1,0:T(8,128)(2,1)S(1)} collective-permute-done((bf16[2,48,1664]{2,1,0:T(8,128)(2,1)S(1)}, bf16[2,48,1664]{2,1,0:T(8,128)(2,1)S(1)}, u32[]{:S(2)}, u32[]{:S(2)}) %collective-permute-start.54) | collective-permute-done | bytes 319520 | tf_op jit(solution)/shard_map/ppermute | solution.py:422
  259.9 2.1 collective-permute-start.60
  262.9 2.2 shard_map.298
  265.1 2.1 shard_map.299
  267.2 8.9 %collective-permute-done.58 = bf16[48,1664]{1,0:T(8,128)(2,1)S(1)} collective-permute-done((bf16[48,1664]{1,0:T(8,128)(2,1)S(1)}, bf16[48,1664]{1,0:T(8,128)(2,1)S(1)}, u32[]{:S(2)}, u32[]{:S(2)}) %collective-permute-start.58) | collective-permute-done | bytes 159776 | tf_op jit(solution)/shard_map/ppermute | solution.py:422
  278.9 2.4 collective-permute-done.62
  282.3 3.0 %collective-permute-done.64 = bf16[48,1664]{1,0:T(8,128)(2,1)S(1)} collective-permute-done((bf16[48,1664]{1,0:T(8,128)(2,1)S(1)}, bf16[48,1664]{1,0:T(8,128)(2,1)S(1)}, u32[]{:S(2)}, u32[]{:S(2)}) %collective-permute-start.64) | collective-permute-done | bytes 159776 | tf_op jit(solution)/shard_map/ppermute | solution.py:426
  288.7 2.2 shard_map.300
  (315 shorter events, 94.8 us)
Async XLA Ops:
  3.6 9.0 %collective-permute-start = (bf16[64,1152]{1,0:T(8,128)(2,1)}, bf16[64,1152]{1,0:T(8,128)(2,1)S(1)}, u32[]{:S(2)}, u32[]{:S(2)}) collective-permute-start(bf16[64,1152]{1,0:T(8,128)(2,1)} %shard_map.271.own_ref), channel_id=1, source_target_pairs={{0,1},{1,0},{2,3},{3,2},{4,5},{5,4},{6,7},{7,6},{8,9},{9,8},{10,11... | collective-permute-start | bytes 442376 | tf_op jit(solution)/shard_map/ppermute | solution.py:422
  3.8 12.4 %collective-permute-start.3 = (bf16[64,1152]{1,0:T(8,128)(2,1)}, bf16[64,1152]{1,0:T(8,128)(2,1)S(1)}, u32[]{:S(2)}, u32[]{:S(2)}) collective-permute-start(bf16[64,1152]{1,0:T(8,128)(2,1)} %shard_map.271.own_ref), channel_id=1, source_target_pairs={{0,2},{1,3},{2,0},{3,1},{4,6},{5,7},{6,4},{7,5},{8,10},{9,11},{10,... | collective-permute-start | bytes 442376 | tf_op jit(solution)/shard_map/ppermute | solution.py:422
  3.8 12.4 %collective-permute-start.4 = (bf16[64,1152]{1,0:T(8,128)(2,1)}, bf16[64,1152]{1,0:T(8,128)(2,1)S(1)}, u32[]{:S(2)}, u32[]{:S(2)}) collective-permute-start(bf16[64,1152]{1,0:T(8,128)(2,1)} %shard_map.271.own_ref), channel_id=1, source_target_pairs={{0,3},{1,2},{2,1},{3,0},{4,7},{5,6},{6,5},{7,4},{8,11},{9,10},{10,... | collective-permute-start | bytes 442376 | tf_op jit(solution)/shard_map/ppermute | solution.py:422
  17.4 16.4 %collective-permute-start.6 = (bf16[192,1152]{1,0:T(8,128)(2,1)S(1)}, bf16[192,1152]{1,0:T(8,128)(2,1)S(1)}, u32[]{:S(2)}, u32[]{:S(2)}) collective-permute-start(bf16[192,1152]{1,0:T(8,128)(2,1)S(1)} %shard_map.273.came_ref.refs_1_), channel_id=1, source_target_pairs={{0,8},{4,12},{8,0},{12,4},{16,24},{20,28},{24,16},{28,20},{1,9},{5... | collective-permute-start | bytes 1327112 | tf_op jit(solution)/shard_map/ppermute | solution.py:414
  18.7 15.1 %collective-permute-start.7 = (bf16[192,1152]{1,0:T(8,128)(2,1)S(1)}, bf16[192,1152]{1,0:T(8,128)(2,1)S(1)}, u32[]{:S(2)}, u32[]{:S(2)}) collective-permute-start(bf16[192,1152]{1,0:T(8,128)(2,1)S(1)} %shard_map.273.came_ref.refs_1_), channel_id=1, source_target_pairs={{0,16},{4,20},{8,24},{12,28},{16,0},{20,4},{24,8},{28,12},{1,17},{... | collective-permute-start | bytes 1327112 | tf_op jit(solution)/shard_map/ppermute | solution.py:418
  19.9 17.2 %collective-permute-start.8 = (bf16[192,1152]{1,0:T(8,128)(2,1)S(1)}, bf16[192,1152]{1,0:T(8,128)(2,1)S(1)}, u32[]{:S(2)}, u32[]{:S(2)}) collective-permute-start(bf16[192,1152]{1,0:T(8,128)(2,1)S(1)} %shard_map.273.came_ref.refs_1_), channel_id=1, source_target_pairs={{0,24},{4,28},{8,16},{12,20},{16,8},{20,12},{24,0},{28,4},{1,25},{... | collective-permute-start | bytes 1327112 | tf_op jit(solution)/shard_map/ppermute | solution.py:426
  21.8 12.0 %collective-permute-start.2 = (bf16[256,768]{1,0:T(8,128)(2,1)}, bf16[256,768]{1,0:T(8,128)(2,1)S(1)}, u32[]{:S(2)}, u32[]{:S(2)}) collective-permute-start(bf16[256,768]{1,0:T(8,128)(2,1)} %get-tuple-element.172), channel_id=1, source_target_pairs={{0,1},{1,0},{2,5},{3,4},{4,3},{5,2},{6,7},{7,6},{8,9},{9,8},{10,13... | collective-permute-start | bytes 1179656 | tf_op jit(solution)/shard_map/ppermute | solution.py:452
  38.8 17.2 %collective-permute-start.9 = (bf16[512,768]{1,0:T(8,128)(2,1)S(1)}, bf16[512,768]{1,0:T(8,128)(2,1)}, u32[]{:S(2)}, u32[]{:S(2)}) collective-permute-start(bf16[512,768]{1,0:T(8,128)(2,1)S(1)} %shard_map.275.refs_0_), channel_id=1, source_target_pairs={{0,4},{4,0},{8,12},{12,8},{16,20},{20,16},{24,28},{28,24},{1,5},{5... | collective-permute-start | bytes 2359304 | tf_op jit(solution)/shard_map/ppermute | solution.py:410
  46.0 18.4 %collective-permute-start.10 = (bf16[48,1920]{1,0:T(8,128)(2,1)}, bf16[48,1920]{1,0:T(8,128)(2,1)S(1)}, u32[]{:S(2)}, u32[]{:S(2)}) collective-permute-start(bf16[48,1920]{1,0:T(8,128)(2,1)} %get-tuple-element.184), channel_id=1, source_target_pairs={{0,1},{1,0},{2,3},{3,2},{4,5},{5,4},{6,7},{7,6},{8,9},{9,8},{10,11... | collective-permute-start | bytes 552968 | tf_op jit(solution)/shard_map/ppermute | solution.py:422
  49.3 15.1 %collective-permute-start.11 = (bf16[48,1920]{1,0:T(8,128)(2,1)}, bf16[48,1920]{1,0:T(8,128)(2,1)S(1)}, u32[]{:S(2)}, u32[]{:S(2)}) collective-permute-start(bf16[48,1920]{1,0:T(8,128)(2,1)} %get-tuple-element.184), channel_id=1, source_target_pairs={{0,2},{1,3},{2,0},{3,1},{4,6},{5,7},{6,4},{7,5},{8,10},{9,11},{10,... | collective-permute-start | bytes 552968 | tf_op jit(solution)/shard_map/ppermute | solution.py:422
  49.3 15.1 %collective-permute-start.12 = (bf16[48,1920]{1,0:T(8,128)(2,1)}, bf16[48,1920]{1,0:T(8,128)(2,1)S(1)}, u32[]{:S(2)}, u32[]{:S(2)}) collective-permute-start(bf16[48,1920]{1,0:T(8,128)(2,1)} %get-tuple-element.184), channel_id=1, source_target_pairs={{0,3},{1,2},{2,1},{3,0},{4,7},{5,6},{6,5},{7,4},{8,11},{9,10},{10,... | collective-permute-start | bytes 552968 | tf_op jit(solution)/shard_map/ppermute | solution.py:422
  77.1 16.6 %collective-permute-start.17 = (bf16[144,1920]{1,0:T(8,128)(2,1)S(1)}, bf16[144,1920]{1,0:T(8,128)(2,1)S(1)}, u32[]{:S(2)}, u32[]{:S(2)}) collective-permute-start(bf16[144,1920]{1,0:T(8,128)(2,1)S(1)} %shard_map.279.refs_2_), channel_id=1, source_target_pairs={{0,8},{4,12},{8,0},{12,4},{16,24},{20,28},{24,16},{28,20},{1,9},{5... | collective-permute-start | bytes 1658888 | tf_op jit(solution)/shard_map/ppermute | solution.py:414
  78.3 15.4 %collective-permute-start.18 = (bf16[144,1920]{1,0:T(8,128)(2,1)S(1)}, bf16[144,1920]{1,0:T(8,128)(2,1)S(1)}, u32[]{:S(2)}, u32[]{:S(2)}) collective-permute-start(bf16[144,1920]{1,0:T(8,128)(2,1)S(1)} %shard_map.279.refs_2_), channel_id=1, source_target_pairs={{0,16},{4,20},{8,24},{12,28},{16,0},{20,4},{24,8},{28,12},{1,17},{... | collective-permute-start | bytes 1658888 | tf_op jit(solution)/shard_map/ppermute | solution.py:418
  79.6 23.1 %collective-permute-start.19 = (bf16[144,1920]{1,0:T(8,128)(2,1)S(1)}, bf16[144,1920]{1,0:T(8,128)(2,1)S(1)}, u32[]{:S(2)}, u32[]{:S(2)}) collective-permute-start(bf16[144,1920]{1,0:T(8,128)(2,1)S(1)} %shard_map.279.refs_2_), channel_id=1, source_target_pairs={{0,24},{4,28},{8,16},{12,20},{16,8},{20,12},{24,0},{28,4},{1,25},{... | collective-permute-start | bytes 1658888 | tf_op jit(solution)/shard_map/ppermute | solution.py:426
  79.8 10.5 %collective-permute-start.15 = (bf16[256,768]{1,0:T(8,128)(2,1)S(1)}, bf16[256,768]{1,0:T(8,128)(2,1)S(1)}, u32[]{:S(2)}, u32[]{:S(2)}) collective-permute-start(bf16[256,768]{1,0:T(8,128)(2,1)S(1)} %copy-done.35), channel_id=1, source_target_pairs={{0,0},{1,1},{2,4},{3,5},{4,2},{5,3},{6,6},{7,7},{8,8},{9,9},{10,12... | collective-permute-start | bytes 1179656 | tf_op jit(solution)/shard_map/ppermute | solution.py:448
  82.4 10.4 %collective-permute-start.16 = (bf16[256,768]{1,0:T(8,128)(2,1)S(1)}, bf16[256,768]{1,0:T(8,128)(2,1)S(1)}, u32[]{:S(2)}, u32[]{:S(2)}) collective-permute-start(bf16[256,768]{1,0:T(8,128)(2,1)S(1)} %copy-done.34), channel_id=1, source_target_pairs={{0,1},{1,0},{2,5},{3,4},{4,3},{5,2},{6,7},{7,6},{8,9},{9,8},{10,13... | collective-permute-start | bytes 1179656 | tf_op jit(solution)/shard_map/ppermute | solution.py:452
  110.0 8.4 %collective-permute-start.21 = (bf16[1024,768]{1,0:T(8,128)(2,1)S(1)}, bf16[1024,768]{1,0:T(8,128)(2,1)S(1)}, u32[]{:S(2)}, u32[]{:S(2)}) collective-permute-start(bf16[1024,768]{1,0:T(8,128)(2,1)S(1)} %convolution_convert_fusion.2.part_ref), channel_id=1, source_target_pairs={{0,4},{4,0},{8,12},{12,8},{16,20},{20,16},{24,28},{28,24},{1,5},{5... | collective-permute-start | bytes 4718600 | tf_op jit(solution)/shard_map/ppermute | solution.py:410
  110.9 17.3 %collective-permute-start.24 = (bf16[288,768]{1,0:T(8,128)(2,1)S(1)}, bf16[288,768]{1,0:T(8,128)(2,1)S(1)}, u32[]{:S(2)}, u32[]{:S(2)}) collective-permute-start(bf16[288,768]{1,0:T(8,128)(2,1)S(1)} %shard_map.283.refs_1_), channel_id=1, source_target_pairs={{0,8},{4,12},{8,0},{12,4},{16,24},{20,28},{24,16},{28,20},{1,9},{5... | collective-permute-start | bytes 1327112 | tf_op jit(solution)/shard_map/ppermute | solution.py:414
  111.9 16.4 %collective-permute-start.25 = (bf16[288,768]{1,0:T(8,128)(2,1)S(1)}, bf16[288,768]{1,0:T(8,128)(2,1)S(1)}, u32[]{:S(2)}, u32[]{:S(2)}) collective-permute-start(bf16[288,768]{1,0:T(8,128)(2,1)S(1)} %shard_map.283.refs_1_), channel_id=1, source_target_pairs={{0,16},{4,20},{8,24},{12,28},{16,0},{20,4},{24,8},{28,12},{1,17},{... | collective-permute-start | bytes 1327112 | tf_op jit(solution)/shard_map/ppermute | solution.py:418
  114.6 18.4 %collective-permute-start.26 = (bf16[288,768]{1,0:T(8,128)(2,1)S(1)}, bf16[288,768]{1,0:T(8,128)(2,1)S(1)}, u32[]{:S(2)}, u32[]{:S(2)}) collective-permute-start(bf16[288,768]{1,0:T(8,128)(2,1)S(1)} %shard_map.283.refs_1_), channel_id=1, source_target_pairs={{0,24},{4,28},{8,16},{12,20},{16,8},{20,12},{24,0},{28,4},{1,25},{... | collective-permute-start | bytes 1327112 | tf_op jit(solution)/shard_map/ppermute | solution.py:426
  156.2 25.3 %collective-permute-start.30 = (bf16[4,2,48,768]{3,2,1,0:T(8,128)(2,1)S(1)}, bf16[4,2,48,768]{3,2,1,0:T(8,128)(2,1)S(1)}, u32[]{:S(2)}, u32[]{:S(2)}) collective-permute-start(bf16[4,2,48,768]{3,2,1,0:T(8,128)(2,1)S(1)} %get-tuple-element.338), channel_id=1, source_target_pairs={{0,8},{4,12},{8,0},{12,4},{16,24},{20,28},{24,16},{28,20},{1,9},{5... | collective-permute-start | bytes 1769480 | tf_op jit(solution)/shard_map/ppermute | solution.py:414
  156.8 24.7 %collective-permute-start.31 = (bf16[4,2,48,768]{3,2,1,0:T(8,128)(2,1)S(1)}, bf16[4,2,48,768]{3,2,1,0:T(8,128)(2,1)S(1)}, u32[]{:S(2)}, u32[]{:S(2)}) collective-permute-start(bf16[4,2,48,768]{3,2,1,0:T(8,128)(2,1)S(1)} %get-tuple-element.336), channel_id=1, source_target_pairs={{0,16},{4,20},{8,24},{12,28},{16,0},{20,4},{24,8},{28,12},{1,17},{... | collective-permute-start | bytes 1769480 | tf_op jit(solution)/shard_map/ppermute | solution.py:418
  158.1 16.4 %collective-permute-start.28 = (bf16[256,768]{1,0:T(8,128)(2,1)S(1)}, bf16[256,768]{1,0:T(8,128)(2,1)S(1)}, u32[]{:S(2)}, u32[]{:S(2)}) collective-permute-start(bf16[256,768]{1,0:T(8,128)(2,1)S(1)} %get-tuple-element.213), channel_id=1, source_target_pairs={{0,0},{1,1},{4,2},{5,3},{2,4},{3,5},{6,6},{7,7},{8,8},{9,9},{12,10... | collective-permute-start | bytes 1179656 | tf_op jit(solution)/shard_map/ppermute | solution.py:460
  165.9 9.6 %collective-permute-start.32 = (bf16[1024,768]{1,0:T(8,128)(2,1)S(1)}, bf16[1024,768]{1,0:T(8,128)(2,1)S(1)}, u32[]{:S(2)}, u32[]{:S(2)}) collective-permute-start(bf16[1024,768]{1,0:T(8,128)(2,1)S(1)} %get-tuple-element.219.part_ref), channel_id=1, source_target_pairs={{0,4},{4,0},{8,12},{12,8},{16,20},{20,16},{24,28},{28,24},{1,5},{5... | collective-permute-start | bytes 4718600 | tf_op jit(solution)/shard_map/ppermute | solution.py:410
  174.1 21.7 %collective-permute-start.33 = (bf16[4,2,24,1536]{3,2,1,0:T(8,128)(2,1)S(1)}, bf16[4,2,24,1536]{3,2,1,0:T(8,128)(2,1)S(1)}, u32[]{:S(2)}, u32[]{:S(2)}) collective-permute-start(bf16[4,2,24,1536]{3,2,1,0:T(8,128)(2,1)S(1)} %get-tuple-element.334), channel_id=1, source_target_pairs={{0,8},{4,12},{8,0},{12,4},{16,24},{20,28},{24,16},{28,20},{1,9},{5... | collective-permute-start | bytes 1769480 | tf_op jit(solution)/shard_map/ppermute | solution.py:414
  174.5 21.3 %collective-permute-start.34 = (bf16[4,2,24,1536]{3,2,1,0:T(8,128)(2,1)S(1)}, bf16[4,2,24,1536]{3,2,1,0:T(8,128)(2,1)S(1)}, u32[]{:S(2)}, u32[]{:S(2)}) collective-permute-start(bf16[4,2,24,1536]{3,2,1,0:T(8,128)(2,1)S(1)} %get-tuple-element.332), channel_id=1, source_target_pairs={{0,16},{4,20},{8,24},{12,28},{16,0},{20,4},{24,8},{28,12},{1,17},{... | collective-permute-start | bytes 1769480 | tf_op jit(solution)/shard_map/ppermute | solution.py:418
  175.5 15.5 %collective-permute-start.29 = (bf16[256,768]{1,0:T(8,128)(2,1)S(1)}, bf16[256,768]{1,0:T(8,128)(2,1)S(1)}, u32[]{:S(2)}, u32[]{:S(2)}) collective-permute-start(bf16[256,768]{1,0:T(8,128)(2,1)S(1)} %get-tuple-element.221), channel_id=1, source_target_pairs={{1,0},{0,1},{5,2},{4,3},{3,4},{2,5},{7,6},{6,7},{9,8},{8,9},{13,10... | collective-permute-start | bytes 1179656 | tf_op jit(solution)/shard_map/ppermute | solution.py:460
  181.9 13.5 %collective-permute-start.35 = (bf16[4,48,768]{2,1,0:T(8,128)(2,1)S(1)}, bf16[4,48,768]{2,1,0:T(8,128)(2,1)S(1)}, u32[]{:S(2)}, u32[]{:S(2)}) collective-permute-start(bf16[4,48,768]{2,1,0:T(8,128)(2,1)S(1)} %get-tuple-element.362), channel_id=1, source_target_pairs={{0,16},{4,20},{8,24},{12,28},{16,0},{20,4},{24,8},{28,12},{1,17},{... | collective-permute-start | bytes 884744 | tf_op jit(solution)/shard_map/ppermute | solution.py:418
  182.2 13.3 %collective-permute-start.36 = (bf16[4,48,768]{2,1,0:T(8,128)(2,1)S(1)}, bf16[4,48,768]{2,1,0:T(8,128)(2,1)S(1)}, u32[]{:S(2)}, u32[]{:S(2)}) collective-permute-start(bf16[4,48,768]{2,1,0:T(8,128)(2,1)S(1)} %get-tuple-element.360), channel_id=1, source_target_pairs={{0,8},{4,12},{8,0},{12,4},{16,24},{20,28},{24,16},{28,20},{1,9},{5... | collective-permute-start | bytes 884744 | tf_op jit(solution)/shard_map/ppermute | solution.py:414
  196.2 14.3 %collective-permute-start.37 = (bf16[4,24,1536]{2,1,0:T(8,128)(2,1)S(1)}, bf16[4,24,1536]{2,1,0:T(8,128)(2,1)S(1)}, u32[]{:S(2)}, u32[]{:S(2)}) collective-permute-start(bf16[4,24,1536]{2,1,0:T(8,128)(2,1)S(1)} %get-tuple-element.358), channel_id=1, source_target_pairs={{0,16},{4,20},{8,24},{12,28},{16,0},{20,4},{24,8},{28,12},{1,17},{... | collective-permute-start | bytes 884744 | tf_op jit(solution)/shard_map/ppermute | solution.py:418
  197.2 13.4 %collective-permute-start.38 = (bf16[4,24,1536]{2,1,0:T(8,128)(2,1)S(1)}, bf16[4,24,1536]{2,1,0:T(8,128)(2,1)S(1)}, u32[]{:S(2)}, u32[]{:S(2)}) collective-permute-start(bf16[4,24,1536]{2,1,0:T(8,128)(2,1)S(1)} %get-tuple-element.356), channel_id=1, source_target_pairs={{0,8},{4,12},{8,0},{12,4},{16,24},{20,28},{24,16},{28,20},{1,9},{5... | collective-permute-start | bytes 884744 | tf_op jit(solution)/shard_map/ppermute | solution.py:414
  197.7 12.7 %collective-permute-start.39 = (bf16[2,96,768]{2,1,0:T(8,128)(2,1)S(1)}, bf16[2,96,768]{2,1,0:T(8,128)(2,1)S(1)}, u32[]{:S(2)}, u32[]{:S(2)}) collective-permute-start(bf16[2,96,768]{2,1,0:T(8,128)(2,1)S(1)} %get-tuple-element.354), channel_id=1, source_target_pairs={{0,1},{1,0},{2,3},{3,2},{4,5},{5,4},{6,7},{7,6},{8,9},{9,8},{10,11... | collective-permute-start | bytes 884744 | tf_op jit(solution)/shard_map/ppermute | solution.py:422
  208.6 12.9 %collective-permute-start.42 = (bf16[4,2,24,1152]{3,2,1,0:T(8,128)(2,1)S(1)}, bf16[4,2,24,1152]{3,2,1,0:T(8,128)(2,1)S(1)}, u32[]{:S(2)}, u32[]{:S(2)}) collective-permute-start(bf16[4,2,24,1152]{3,2,1,0:T(8,128)(2,1)S(1)} %pad_maximum_fusion.3), channel_id=1, source_target_pairs={{0,8},{4,12},{8,0},{12,4},{16,24},{20,28},{24,16},{28,20},{1,9},{5... | collective-permute-start | bytes 1327112 | tf_op jit(solution)/shard_map/ppermute | solution.py:414
  209.7 11.8 %collective-permute-start.43 = (bf16[4,2,24,1152]{3,2,0,1:T(8,128)(2,1)S(1)}, bf16[4,2,24,1152]{3,2,0,1:T(8,128)(2,1)S(1)}, u32[]{:S(2)}, u32[]{:S(2)}) collective-permute-start(bf16[4,2,24,1152]{3,2,0,1:T(8,128)(2,1)S(1)} %pad_maximum_fusion.4), channel_id=1, source_target_pairs={{0,16},{4,20},{8,24},{12,28},{16,0},{20,4},{24,8},{28,12},{1,17},{... | collective-permute-start | bytes 1327112 | tf_op jit(solution)/shard_map/ppermute | solution.py:418
  210.8 15.5 %collective-permute-start.40 = (bf16[2,48,1536]{2,1,0:T(8,128)(2,1)S(1)}, bf16[2,48,1536]{2,1,0:T(8,128)(2,1)S(1)}, u32[]{:S(2)}, u32[]{:S(2)}) collective-permute-start(bf16[2,48,1536]{2,1,0:T(8,128)(2,1)S(1)} %get-tuple-element.350), channel_id=1, source_target_pairs={{0,1},{1,0},{2,3},{3,2},{4,5},{5,4},{6,7},{7,6},{8,9},{9,8},{10,11... | collective-permute-start | bytes 884744 | tf_op jit(solution)/shard_map/ppermute | solution.py:422
  212.3 13.3 %collective-permute-start.41 = (bf16[96,768]{1,0:T(8,128)(2,1)S(1)}, bf16[96,768]{1,0:T(8,128)(2,1)S(1)}, u32[]{:S(2)}, u32[]{:S(2)}) collective-permute-start(bf16[96,768]{1,0:T(8,128)(2,1)S(1)} %get-tuple-element.376), channel_id=1, source_target_pairs={{0,2},{1,3},{2,0},{3,1},{4,6},{5,7},{6,4},{7,5},{8,10},{9,11},{10,... | collective-permute-start | bytes 442376 | tf_op jit(solution)/shard_map/ppermute | solution.py:422
  221.8 17.9 %collective-permute-start.50 = (bf16[4,24,1152]{2,1,0:T(8,128)(2,1)S(1)}, bf16[4,24,1152]{2,1,0:T(8,128)(2,1)S(1)}, u32[]{:S(2)}, u32[]{:S(2)}) collective-permute-start(bf16[4,24,1152]{2,1,0:T(8,128)(2,1)S(1)} %dynamic-slice_bitcast_fusion.24), channel_id=1, source_target_pairs={{0,8},{4,12},{8,0},{12,4},{16,24},{20,28},{24,16},{28,20},{1,9},{5... | collective-permute-start | bytes 663560 | tf_op jit(solution)/shard_map/ppermute | solution.py:414
  223.1 17.1 %collective-permute-start.49 = (bf16[4,24,1152]{2,1,0:T(8,128)(2,1)S(1)}, bf16[4,24,1152]{2,1,0:T(8,128)(2,1)S(1)}, u32[]{:S(2)}, u32[]{:S(2)}) collective-permute-start(bf16[4,24,1152]{2,1,0:T(8,128)(2,1)S(1)} %dynamic-slice_bitcast_fusion.25), channel_id=1, source_target_pairs={{0,16},{4,20},{8,24},{12,28},{16,0},{20,4},{24,8},{28,12},{1,17},{... | collective-permute-start | bytes 663560 | tf_op jit(solution)/shard_map/ppermute | solution.py:418
  225.6 10.3 %collective-permute-start.46 = (bf16[4,2,24,512]{3,2,1,0:T(8,128)(2,1)S(1)}, bf16[4,2,24,512]{3,2,1,0:T(8,128)(2,1)S(1)}, u32[]{:S(2)}, u32[]{:S(2)}) collective-permute-start(bf16[4,2,24,512]{3,2,1,0:T(8,128)(2,1)S(1)} %pad_maximum_fusion.8), channel_id=1, source_target_pairs={{0,16},{4,20},{8,24},{12,28},{16,0},{20,4},{24,8},{28,12},{1,17},{... | collective-permute-start | bytes 589832 | tf_op jit(solution)/shard_map/ppermute | solution.py:418
  226.3 12.4 %collective-permute-start.44 = (bf16[96,768]{1,0:T(8,128)(2,1)S(1)}, bf16[96,768]{1,0:T(8,128)(2,1)S(1)}, u32[]{:S(2)}, u32[]{:S(2)}) collective-permute-start(bf16[96,768]{1,0:T(8,128)(2,1)S(1)} %add_convert_fusion.19), channel_id=1, source_target_pairs={{0,8},{4,12},{8,0},{12,4},{16,24},{20,28},{24,16},{28,20},{1,9},{5... | collective-permute-start | bytes 442376 | tf_op jit(solution)/shard_map/ppermute | solution.py:414
  231.6 9.6 %collective-permute-start.47 = (bf16[512,768]{1,0:T(8,128)(2,1)S(1)}, bf16[512,768]{1,0:T(8,128)(2,1)S(1)}, u32[]{:S(2)}, u32[]{:S(2)}) collective-permute-start(bf16[512,768]{1,0:T(8,128)(2,1)S(1)} %convolution_convert_fusion.6), channel_id=1, source_target_pairs={{0,4},{4,0},{8,12},{12,8},{16,20},{20,16},{24,28},{28,24},{1,5},{5... | collective-permute-start | bytes 2359304 | tf_op jit(solution)/shard_map/ppermute | solution.py:410
  235.9 10.0 %collective-permute-start.53 = (bf16[48,1536]{1,0:T(8,128)(2,1)S(1)}, bf16[48,1536]{1,0:T(8,128)(2,1)S(1)}, u32[]{:S(2)}, u32[]{:S(2)}) collective-permute-start(bf16[48,1536]{1,0:T(8,128)(2,1)S(1)} %get-tuple-element.366), channel_id=1, source_target_pairs={{0,2},{1,3},{2,0},{3,1},{4,6},{5,7},{6,4},{7,5},{8,10},{9,11},{10,... | collective-permute-start | bytes 442376 | tf_op jit(solution)/shard_map/ppermute | solution.py:422
  240.2 9.0 %collective-permute-start.56 = (bf16[192,768]{1,0:T(8,128)(2,1)S(1)}, bf16[192,768]{1,0:T(8,128)(2,1)S(1)}, u32[]{:S(2)}, u32[]{:S(2)}) collective-permute-start(bf16[192,768]{1,0:T(8,128)(2,1)S(1)} %constant_dynamic-update-slice_fusion.18), channel_id=1, source_target_pairs={{0,16},{4,20},{8,24},{12,28},{16,0},{20,4},{24,8},{28,12},{1,17},{... | collective-permute-start | bytes 884744 | tf_op jit(solution)/shard_map/ppermute | solution.py:418
  241.5 17.8 %collective-permute-start.48 = (bf16[256,768]{1,0:T(8,128)(2,1)S(1)}, bf16[256,768]{1,0:T(8,128)(2,1)S(1)}, u32[]{:S(2)}, u32[]{:S(2)}) collective-permute-start(bf16[256,768]{1,0:T(8,128)(2,1)S(1)} %get-tuple-element.340), channel_id=1, source_target_pairs={{0,0},{1,1},{4,2},{5,3},{2,4},{3,5},{6,6},{7,7},{8,8},{9,9},{12,10... | collective-permute-start | bytes 1179656 | tf_op jit(solution)/shard_map/ppermute | solution.py:460
  247.1 12.2 %collective-permute-start.54 = (bf16[2,48,1664]{2,1,0:T(8,128)(2,1)S(1)}, bf16[2,48,1664]{2,1,0:T(8,128)(2,1)S(1)}, u32[]{:S(2)}, u32[]{:S(2)}) collective-permute-start(bf16[2,48,1664]{2,1,0:T(8,128)(2,1)S(1)} %get-tuple-element.341), channel_id=1, source_target_pairs={{0,1},{1,0},{2,3},{3,2},{4,5},{5,4},{6,7},{7,6},{8,9},{9,8},{10,11... | collective-permute-start | bytes 958472 | tf_op jit(solution)/shard_map/ppermute | solution.py:422
  249.3 13.6 %collective-permute-start.61 = (bf16[384,768]{1,0:T(8,128)(2,1)S(1)}, bf16[384,768]{1,0:T(8,128)(2,1)S(1)}, u32[]{:S(2)}, u32[]{:S(2)}) collective-permute-start(bf16[384,768]{1,0:T(8,128)(2,1)S(1)} %constant_dynamic-update-slice_fusion.20.mine_ref), channel_id=1, source_target_pairs={{0,4},{4,0},{8,12},{12,8},{16,20},{20,16},{24,28},{28,24},{1,5},{5... | collective-permute-start | bytes 1769480 | tf_op jit(solution)/shard_map/ppermute | solution.py:410
  262.0 14.1 %collective-permute-start.58 = (bf16[48,1664]{1,0:T(8,128)(2,1)S(1)}, bf16[48,1664]{1,0:T(8,128)(2,1)S(1)}, u32[]{:S(2)}, u32[]{:S(2)}) collective-permute-start(bf16[48,1664]{1,0:T(8,128)(2,1)S(1)} %get-tuple-element.364), channel_id=1, source_target_pairs={{0,2},{1,3},{2,0},{3,1},{4,6},{5,7},{6,4},{7,5},{8,10},{9,11},{10,... | collective-permute-start | bytes 479240 | tf_op jit(solution)/shard_map/ppermute | solution.py:422
  262.5 16.4 %collective-permute-start.57 = (bf16[256,768]{1,0:T(8,128)(2,1)S(1)}, bf16[256,768]{1,0:T(8,128)(2,1)S(1)}, u32[]{:S(2)}, u32[]{:S(2)}) collective-permute-start(bf16[256,768]{1,0:T(8,128)(2,1)S(1)} %get-tuple-element.297), channel_id=1, source_target_pairs={{1,0},{0,1},{5,2},{4,3},{3,4},{2,5},{7,6},{6,7},{9,8},{8,9},{13,10... | collective-permute-start | bytes 1179656 | tf_op jit(solution)/shard_map/ppermute | solution.py:460
  (54 other events, 396.5 us)
